TPU v7x, 32 devices: a whole 2x2x4 slice. The times are simulated.
32 devices in a mesh: wide: 8 (over y, x, core), depth: 4 (over z).
Axes of the slice: x: 2, y: 2, z: 4, core: 2. Of those that a mesh axis runs over, the one named last changes fastest.
Arguments:
- matrix_moles: float32 [16, 128, 64, 128], P(None, 'wide', 'depth'), may hold values from 0.2 to 4
- pore_matrix: float32 [128, 64, 128], P('wide', 'depth'), may hold values from 1 to 2
- matrix_rate: float32 [3, 128, 64, 128], P(None, 'wide', 'depth'), may hold values from 0 to 0.03
- matrix_upwind: int32 [2, 3, 128, 64, 128], P(None, None, 'wide', 'depth'), may hold values 0 or 1
- frac_moles: float32 [16, 256, 1024], P(None, ('wide', 'depth')), may hold values from 0.2 to 4
- pore_frac: float32 [256, 1024], P(('wide', 'depth')), may hold values from 1 to 2
- frac_rate: float32 [3, 256, 1024], P(None, ('wide', 'depth')), may hold values from 0 to 0.03
- frac_upwind: int32 [2, 3, 256, 1024], P(None, None, ('wide', 'depth')), may hold values 0 or 1
- ff_open: int32 [256, 2], P(('wide', 'depth')), may hold values 0 or 1
- kvalues: float32 [16], replicated, may hold values from 0.5 to 2
- slot_patch: int32 [256], replicated, may hold values from 0 to 255, as said below
- patch_block: int32 [256, 3], replicated, may hold values from 0 to 63, as said below
Outputs:
- matrix_next: float32 [16, 128, 64, 128], P(None, 'wide', 'depth')
- frac_next: float32 [16, 256, 1024], P(None, ('wide', 'depth'))
Inputs may be any that keep to these rules, and one draw needn't show every extreme that they name: `slot_patch`: A permutation of the patch numbers. The slots s * 8 to s * 8 + 7 belong to device s = w * 4 + d (wide index w, depth index d). Each patch q lies in its device's layers: patch_block[q, 1] // 16 == d. A device holds at most 4 patches of one square column patch_block[q, 0], and some device holds exactly 4 in every draw. `patch_block`: row q holds patch q's first-dimension square index, its layer along the second dimension and its third-dimension square index (the square of cells p0 * 32 to p0 * 32 + 31 and p2 * 32 to p2 * 32 + 31). No two patches share a square in a layer.
All inputs are finite; a program needn't handle non-finite values. No bound on the sum of `matrix_upwind` or of `frac_upwind` or of `ff_open` on one device may be relied on, other than what follows from the above.
Results may differ from a plain program's by a relative error of at most 0.0001.
Values sent between devices are 32-bit elements; how exact they have to be, the bound alone decides.
No kernel may reach another device: no remote copies, remote signals or barrier semaphores. Data moves between devices by JAX's collectives and lax.ppermute only.
A program may use at most 128 MiB of HBM per device.

v0:
```python
import functools

import jax
import jax.numpy as jnp
from jax import lax
from jax.experimental import pallas as pl
from jax.experimental.pallas import tpu as pltpu
from jax.sharding import PartitionSpec as P

SWEEPS = 4
SUBSTEPS = 2
MOBILITY_RATIO = 4.0
LANES = 128
SUB = 8
F32 = jnp.float32
I32 = jnp.int32

VMEM = pl.BlockSpec(memory_space=pltpu.VMEM)
SMEM = pl.BlockSpec(memory_space=pltpu.SMEM)


class Sizes:
    def __init__(self, matrix_moles, frac_moles):
        self.wide = lax.axis_size("wide")
        self.depth = lax.axis_size("depth")
        self.nc, self.x, self.z, self.y = matrix_moles.shape
        self.slots, self.pc = frac_moles.shape[1:]
        self.ps = 1
        while self.ps * self.ps < self.pc:
            self.ps *= 2
        self.by = self.y // self.ps
        self.half = self.pc // 2
        self.cols = self.wide // 2
        self.most = max(1, 4 * self.slots // self.wide)
        self.cpt = SUB // self.most
        self.out_ch = self.nc + 4 + 3 * SUBSTEPS
        self.tiles_out = -(-self.out_ch // self.cpt)
        self.tiles_back = -(-self.nc // self.cpt)
        self.groups = self.wide // SUB
        self.cells = self.x * self.z
        self.xt = LANES // self.ps
        self.jt = self.half // LANES
        assert self.y == LANES and self.slots == SUB and self.z == 2 * SUB
        assert self.x * self.ps == self.half and self.groups * self.most == self.xt == self.by


def iota(shape, dim):
    return lax.broadcasted_iota(I32, shape, dim)


def lane_roll(v, by):
    by = by % LANES
    return v if by == 0 else pltpu.roll(v, by, 1)


def sub_gather(v, idx):
    return jnp.take_along_axis(v, idx, axis=0, mode="promise_in_bounds")


def group_transpose(a, ps):
    grp = iota((SUB, LANES), 1) // ps
    odd, high = (grp & 1) == 1, (grp & 2) == 2

    def pair(u, v, upper, dist):
        return (
            jnp.where(upper, lane_roll(v, dist), u),
            jnp.where(upper, v, lane_roll(u, -dist)),
        )

    b0, b1 = pair(a[0], a[1], odd, ps)
    c0, c1 = pair(a[2], a[3], odd, ps)
    t0, t2 = pair(b0, c0, high, 2 * ps)
    t1, t3 = pair(b1, c1, high, 2 * ps)
    return [t0, t1, t2, t3]


def tree_sum(terms):
    terms = list(terms)
    while len(terms) > 1:
        terms = [a + b for a, b in zip(terms[::2], terms[1::2])] + (
            [terms[-1]] if len(terms) % 2 else []
        )
    return terms[0]


def flash_block(load, store, excess, first, nc):
    total = tree_sum([load(c) for c in range(nc)])
    vapour = None
    for sweep in range(SWEEPS):
        misfits, slopes = [], []
        for c in range(nc):
            if vapour is None:
                p = first[c]
            else:
                p = excess[c] * (1.0 / (1.0 + vapour * excess[c]))
            r = load(c) * p
            misfits.append(r)
            slopes.append(r * p)
        misfit, slope = running(misfits), running(slopes)
        before = 0.5 if vapour is None else vapour
        vapour = jnp.clip(before + misfit / (slope + total), 0.0, 1.0)
    liquid = (1.0 - vapour) * (1.0 - vapour)
    gas = MOBILITY_RATIO * vapour * vapour
    share = gas / (liquid + gas)
    for c in range(nc):
        q = 1.0 / (1.0 + vapour * excess[c])
        store(c, load(c) * q * (1.0 + share * excess[c]))


def running(terms):
    sums = [terms[0], terms[1]]
    for n, t in enumerate(terms[2:]):
        sums[n % 2] = sums[n % 2] + t
    return sums[0] + sums[1]


def k_scalars(k_ref, nc):
    excess = [k_ref[c] - 1.0 for c in range(nc)]
    first = []
    for c in range(nc):
        e = jnp.full((1, LANES), excess[c], F32)
        first.append(e / (1.0 + 0.5 * e))
    return excess, first


def own_slots(z, slot_ref, block_ref, visit):
    me = lax.axis_index("wide") * z.depth + lax.axis_index("depth")
    counts = jnp.int32(0)
    for i in range(z.slots):
        q = slot_ref[me * z.slots + i]
        p0 = block_ref[q * 3]
        rank = (counts >> (4 * p0)) & 15
        counts = counts + (jnp.int32(1) << (4 * p0))
        visit(i, p0, rank)


def pack_kernel(z, slot_ref, block_ref, moles, pore, rate, upwind, openings, out, src):
    nc, slots = z.nc, z.slots
    sub = iota((SUB, LANES), 0)
    picks = [jnp.zeros((SUB, LANES), I32) for _ in range(z.cols)]

    def visit(i, p0, rank):
        for c in range(z.cols):
            hit = ((sub % z.most) == rank) & (p0 == c)
            picks[c] = jnp.where(hit, i, picks[c])

    own_slots(z, slot_ref, block_ref, visit)
    src[pl.ds(0, nc * slots), :] = moles[...]
    src[pl.ds(nc * slots, slots), :] = pore[...]
    cell = iota((slots, z.pc), 1)
    flags = openings[...].astype(F32)
    open_x = jnp.where(cell // z.ps < z.ps - 1, 1.0, flags[:, 0:1])
    open_y = jnp.where(cell % z.ps < z.ps - 1, 1.0, flags[:, 1:2])
    base = (nc + 1) * slots
    src[pl.ds(base, slots), :] = rate[pl.ds(0, slots), :] * open_x
    src[pl.ds(base + slots, slots), :] = rate[pl.ds(slots, slots), :] * open_y
    src[pl.ds(base + 2 * slots, slots), :] = rate[pl.ds(2 * slots, slots), :]
    for n in range(3 * SUBSTEPS):
        src[pl.ds(base + (3 + n) * slots, slots), :] = upwind[pl.ds(n * slots, slots), :].astype(
            F32
        )
    for n in range(z.out_ch, z.tiles_out * z.cpt):
        src[pl.ds(n * slots, slots), :] = jnp.zeros((slots, z.pc), F32)

    def tile(m, carry):
        for h in range(2):
            for j in range(z.jt):
                lanes = pl.ds(h * z.half + j * LANES, LANES)
                parts = [
                    src[pl.ds(pl.multiple_of((m * z.cpt + cp) * slots, slots), slots), lanes]
                    for cp in range(z.cpt)
                ]
                for c in range(z.cols):
                    v = sub_gather(parts[0], picks[c])
                    for cp in range(1, z.cpt):
                        v = jnp.where(sub // z.most >= cp, sub_gather(parts[cp], picks[c]), v)
                    row = (((2 * c + h) * z.jt + j) * z.tiles_out + m) * SUB
                    out[pl.ds(pl.multiple_of(row, SUB), SUB), :] = v
        return carry

    lax.fori_loop(0, z.tiles_out, tile, 0)


def spread_kernel(z, slot_ref, block_ref, recv, out):
    sub = iota((SUB, LANES), 0)
    ranks = jnp.zeros((SUB, LANES), I32)
    column = jnp.zeros((SUB, LANES), I32)

    def visit(i, p0, rank):
        nonlocal ranks, column
        ranks = jnp.where(sub == i, rank, ranks)
        column = jnp.where(sub == i, p0, column)

    own_slots(z, slot_ref, block_ref, visit)

    def tile(m, carry):
        for h in range(2):
            for j in range(z.jt):
                parts = []
                for c in range(z.cols):
                    row = (((2 * c + h) * z.jt + j) * z.tiles_back + m) * SUB
                    parts.append(recv[pl.ds(pl.multiple_of(row, SUB), SUB), :])
                for cp in range(z.cpt):
                    v = sub_gather(parts[0], cp * z.most + ranks)
                    for c in range(1, z.cols):
                        v = jnp.where(
                            column == c, sub_gather(parts[c], cp * z.most + ranks), v
                        )
                    row = (m * z.cpt + cp) * SUB
                    out[
                        pl.ds(pl.multiple_of(row, SUB), SUB),
                        pl.ds(h * z.half + j * LANES, LANES),
                    ] = v
        return carry

    lax.fori_loop(0, z.tiles_back, tile, 0)


def tables(z, slot_ref, block_ref, tab):
    sub, grp = iota((SUB, LANES), 0), iota((SUB, LANES), 1) // z.ps
    bid = [(sub + SUB * h) * z.by + grp for h in range(2)]
    pid = sub + SUB * grp
    wide, deep = lax.axis_index("wide"), lax.axis_index("depth")
    here, after = wide // 2, jnp.where(wide + 1 < z.wide, (wide + 1) // 2, -1)

    def visit(w, state):
        v0, v1, n0, n1, back = state
        counts = jnp.int32(0)
        for i in range(z.slots):
            q = slot_ref[(w * z.depth + deep) * z.slots + i]
            p0 = block_ref[q * 3]
            block = lax.rem(block_ref[q * 3 + 1], z.z) * z.by + block_ref[q * 3 + 2]
            rank = (counts >> (4 * p0)) & 15
            counts = counts + (jnp.int32(1) << (4 * p0))
            place = lax.rem(w, SUB) + SUB * (lax.div(w, SUB) * z.most + rank)
            b_here = jnp.where(p0 == here, block, -1)
            b_next = jnp.where(p0 == after, block, -1)
            p_here = jnp.where(p0 == here, place, -1)
            v0 = jnp.where(bid[0] == b_here, place, v0)
            v1 = jnp.where(bid[1] == b_here, place, v1)
            n0 = jnp.where(bid[0] == b_next, 1, n0)
            n1 = jnp.where(bid[1] == b_next, 1, n1)
            back = jnp.where(pid == p_here, block, back)
        return v0, v1, n0, n1, back

    zero = jnp.zeros((SUB, LANES), I32)
    v0, v1, n0, n1, back = lax.fori_loop(
        0, z.wide, visit, (zero - 1, zero - 1, zero, zero, zero - 1)
    )
    for h, (v, n) in enumerate(((v0, n0), (v1, n1))):
        rows = pl.ds(h * SUB, SUB)
        tab[rows, :] = jnp.where(v >= 0, v & (SUB - 1), 0)
        tab[pl.ds(2 * SUB + h * SUB, SUB), :] = jnp.where(
            v >= 0, (grp - (v >> 3)) & (z.by - 1), -1
        )
        tab[pl.ds(4 * SUB + h * SUB, SUB), :] = n
    depth_row = back // z.by
    tab[pl.ds(6 * SUB, SUB), :] = jnp.where(back >= 0, depth_row & (SUB - 1), 0)
    shift = (grp - (back & (z.by - 1))) & (z.by - 1)
    tab[pl.ds(7 * SUB, SUB), :] = jnp.where(back >= 0, shift * 2 + (depth_row >> 3), -1)


def face(z, rate, upwind, t, d, x):
    g = rate[pl.ds(pl.multiple_of(d * z.cells + x * z.z, z.z), z.z), :]
    u = upwind[pl.ds(pl.multiple_of((t * 3 + d) * z.cells + x * z.z, z.z), z.z), :].astype(F32)
    if d == 0:
        keep = (x < z.x - 1) | (lax.axis_index("wide") < z.wide - 1)
    elif d == 1:
        keep = (iota((z.z, LANES), 0) < z.z - 1) | (lax.axis_index("depth") < z.depth - 1)
    else:
        keep = iota((z.z, LANES), 1) < LANES - 1
    g = jnp.where(keep, g, 0.0)
    out = g * u
    return out, g - out


def plane(z, ref, c, x):
    return ref[pl.ds(pl.multiple_of(c * z.cells + x * z.z, z.z), z.z), :]


def matrix_messages(z, mobile, rate, upwind, t, wide_a, wide_b, deep_a, deep_b):
    nc = z.nc
    even_w = lax.rem(lax.axis_index("wide"), 2) == 0
    even_d = lax.rem(lax.axis_index("depth"), 2) == 0
    out, into = face(z, rate, upwind, t, 0, z.x - 1)
    for c in range(nc):
        ahead = plane(z, mobile, c, z.x - 1) * out
        behind = plane(z, mobile, c, 0)
        rows = pl.ds(c * z.z, z.z)
        wide_a[rows, :] = jnp.where(even_w, ahead, behind)
        wide_b[rows, :] = jnp.where(even_w, behind, ahead)
    rows = pl.ds(nc * z.z, z.z)
    wide_a[rows, :] = into
    wide_b[rows, :] = into
    edge = lax.axis_index("depth") < z.depth - 1

    def last_rows(ref, base, h):
        return ref[pl.ds(base + h * SUB * z.z + z.z - 1, SUB, stride=z.z), :]

    for h in range(z.x // SUB):
        g = jnp.where(edge, last_rows(rate, z.cells, h), 0.0)
        u = last_rows(upwind, (t * 3 + 1) * z.cells, h).astype(F32)
        out = g * u
        for c in range(nc):
            ahead = last_rows(mobile, c * z.cells, h) * out
            behind = mobile[pl.ds(c * z.cells + h * SUB * z.z, SUB, stride=z.z), :]
            rows = pl.ds(c * z.x + h * SUB, SUB)
            deep_a[rows, :] = jnp.where(even_d, ahead, behind)
            deep_b[rows, :] = jnp.where(even_d, behind, ahead)
        rows = pl.ds(nc * z.x + h * SUB, SUB)
        deep_a[rows, :] = g - out
        deep_b[rows, :] = g - out


def flash_field(z, moles, mobile, k_ref):
    excess, first = k_scalars(k_ref, z.nc)
    step = 2

    def block(n, carry):
        def rows(c):
            return pl.ds(pl.multiple_of(c * z.cells + n * step * z.z, z.z), step * z.z)

        def store(c, v):
            mobile[rows(c), :] = v

        flash_block(lambda c: moles[rows(c), :], store, excess, first, z.nc)
        return carry

    lax.fori_loop(0, z.x // step, block, 0)


def first_matrix_kernel(
    z, k_ref, slot_ref, block_ref, moles, rate, upwind, mobile, wide_a, wide_b, deep_a, deep_b, tab
):
    tables(z, slot_ref, block_ref, tab)
    flash_field(z, moles, mobile, k_ref)
    matrix_messages(z, mobile, rate, upwind, 0, wide_a, wide_b, deep_a, deep_b)


def frac_messages(z, mobile, coef, tab, t, frac_a, frac_b):
    even = lax.rem(lax.axis_index("wide"), 2) == 0
    last = lax.axis_index("wide") == z.wide - 1
    here = (tab[pl.ds(2 * SUB, 2 * SUB), :] >= 0).astype(F32)
    out = plane(z, coef, 1, z.x - 1) * plane(z, coef, 4 + 3 * t, z.x - 1)
    into = plane(z, coef, 1, z.x - 1) - out
    out = jnp.where(last, 0.0, out)
    into = jnp.where(last, 0.0, into)
    for c in range(z.nc):
        ahead = plane(z, mobile, c, z.x - 1) * out
        behind = plane(z, mobile, c, 0) * here
        rows = pl.ds(c * z.z, z.z)
        frac_a[rows, :] = jnp.where(even, ahead, behind)
        frac_b[rows, :] = jnp.where(even, behind, ahead)
    rows = pl.ds(z.nc * z.z, z.z)
    frac_a[rows, :] = into
    frac_b[rows, :] = into


def first_frac_kernel(z, k_ref, tab, recv, moles, mobile, coef, frac_a, frac_b):
    lane_tile = z.tiles_out * SUB
    stride = z.jt * lane_tile
    from_sub = [tab[pl.ds(h * SUB, SUB), :] for h in range(2)]
    shift = [tab[pl.ds(2 * SUB + h * SUB, SUB), :] for h in range(2)]

    def channel(c, dst, first_row, default):
        for j in range(z.jt):
            a = [
                recv[
                    pl.ds(
                        g * SUB * stride + j * lane_tile + c * z.most + k, SUB, stride=stride
                    ),
                    :,
                ]
                for g in range(z.groups)
                for k in range(z.most)
            ]
            for xi, v in enumerate(group_transpose(a, z.ps)):
                rolled = [lane_roll(v, n * z.ps) for n in range(z.by)]
                for h in range(2):
                    got = jnp.full((SUB, LANES), default, F32)
                    for n in range(z.by):
                        got = jnp.where(shift[h] == n, sub_gather(rolled[n], from_sub[h]), got)
                    row = first_row + (z.xt * j + xi) * z.z + h * SUB
                    dst[pl.ds(pl.multiple_of(row, SUB), SUB), :] = got

    def amount(c, carry):
        channel(c, moles, c * z.cells, 1.0)
        return carry

    def weight(c, carry):
        channel(z.nc + c, coef, c * z.cells, jnp.where(c == 0, 1.0, 0.0))
        return carry

    lax.fori_loop(0, z.nc, amount, 0)
    lax.fori_loop(0, z.out_ch - z.nc, weight, 0)
    flash_field(z, moles, mobile, k_ref)
    frac_messages(z, mobile, coef, tab, 0, frac_a, frac_b)


def matrix_update(z, t, moles, mobile, mobile_f, coef, rate, upwind, pore, halos, new):
    wide_a, wide_b, deep_a, deep_b = halos
    nc = z.nc
    even_w = lax.rem(lax.axis_index("wide"), 2) == 0
    even_d = lax.rem(lax.axis_index("depth"), 2) == 0
    sub = iota((z.z, LANES), 0)

    def side(a, b, first, row, count):
        rows = pl.ds(row, count)
        even = even_w if a is wide_a else even_d
        if first:
            return jnp.where(even, b[rows, :], a[rows, :])
        return jnp.where(even, a[rows, :], b[rows, :])

    def at(x, low, high):
        inv = 1.0 / plane(z, pore, 0, x)
        ox, ix = face(z, rate, upwind, t, 0, x)
        oz, iz = face(z, rate, upwind, t, 1, x)
        oy, iy = face(z, rate, upwind, t, 2, x)
        if low:
            pox, pix = 1.0, side(wide_a, wide_b, True, nc * z.z, z.z)
        else:
            pox, pix = face(z, rate, upwind, t, 0, x - 1)
        wz = jnp.broadcast_to(side(deep_a, deep_b, True, nc * z.x + x, 1), (z.z, LANES))
        poz = jnp.where(sub == 0, 1.0, pltpu.roll(oz, 1, 0))
        piz = jnp.where(sub == 0, wz, pltpu.roll(iz, 1, 0))
        poy, piy = lane_roll(oy, 1), lane_roll(iy, 1)
        g2 = plane(z, coef, 3, x)
        w2 = g2 * plane(z, coef, 4 + 3 * t + 2, x)
        w5 = (g2 - w2) * inv
        own = (ox + pix + oz + piz + oy + piy + w2) * inv
        ax, bx = ix * inv, pox * inv
        az, bz = iz * inv, poz * inv
        ay, by = iy * inv, poy * inv
        for c in range(nc):
            g = plane(z, mobile, c, x)
            before = (
                side(wide_a, wide_b, True, c * z.z, z.z) if low else plane(z, mobile, c, x - 1)
            )
            after = (
                side(wide_a, wide_b, False, c * z.z, z.z) if high else plane(z, mobile, c, x + 1)
            )
            hz0 = jnp.broadcast_to(side(deep_a, deep_b, True, c * z.x + x, 1), (z.z, LANES))
            hz1 = jnp.broadcast_to(side(deep_a, deep_b, False, c * z.x + x, 1), (z.z, LANES))
            zb = jnp.where(sub == 0, hz0, pltpu.roll(g, 1, 0))
            za = jnp.where(sub == z.z - 1, hz1, pltpu.roll(g, z.z - 1, 0))
            v = plane(z, moles, c, x) - own * g + ax * after + bx * before
            v = v + (az * za + bz * zb)
            v = v + (ay * lane_roll(g, -1) + by * lane_roll(g, 1))
            v = v + w5 * plane(z, mobile_f, c, x)
            new[pl.ds(pl.multiple_of(c * z.cells + x * z.z, z.z), z.z), :] = v

    at(0, True, False)

    def middle(x, carry):
        at(x, False, False)
        return carry

    lax.fori_loop(1, z.x - 1, middle, 0)
    at(z.x - 1, False, True)


def matrix_kernel(
    z, t, k_ref, moles, mobile, mobile_f, coef, rate, upwind, pore, ha, hb, hc, hd, new,
    mobile_new=None, wide_a=None, wide_b=None, deep_a=None, deep_b=None,
):
    matrix_update(
        z, t, moles, mobile, mobile_f, coef, rate, upwind, pore, (ha, hb, hc, hd), new
    )
    if mobile_new is not None:
        flash_field(z, new, mobile_new, k_ref)
        matrix_messages(z, mobile_new, rate, upwind, t + 1, wide_a, wide_b, deep_a, deep_b)


def frac_update(z, t, tab, moles, mobile, mobile_m, coef, frac_a, frac_b, new):
    nc = z.nc
    even = lax.rem(lax.axis_index("wide"), 2) == 0
    here = (tab[pl.ds(2 * SUB, 2 * SUB), :] >= 0).astype(F32)
    beyond = tab[pl.ds(4 * SUB, 2 * SUB), :].astype(F32)
    lane = iota((z.z, LANES), 1)
    next_y = jnp.where(lane == LANES - 1, 0.0, lane_roll(here, -1))

    def side(first, row):
        rows = pl.ds(row, z.z)
        if first:
            return jnp.where(even, frac_b[rows, :], frac_a[rows, :])
        return jnp.where(even, frac_a[rows, :], frac_b[rows, :])

    def split(x, d, mask):
        g = plane(z, coef, 1 + d, x) * mask
        out = g * plane(z, coef, 4 + 3 * t + d, x)
        return out, g - out

    def at(x, low, high):
        inv = 1.0 / plane(z, coef, 0, x)
        ox, ix = split(x, 0, beyond if high else here)
        if low:
            pox, pix = here, side(True, nc * z.z) * here
        else:
            pox, pix = split(x - 1, 0, here)
        oy, iy = split(x, 1, next_y)
        poy, piy = lane_roll(oy, 1), lane_roll(iy, 1)
        w2, w5 = split(x, 2, 1.0)
        own = (ox + pix + oy + piy + w5) * inv
        ax, bx = ix * inv, pox * inv
        ay, by = iy * inv, poy * inv
        w2 = w2 * inv
        for c in range(nc):
            g = plane(z, mobile, c, x)
            before = side(True, c * z.z) if low else plane(z, mobile, c, x - 1)
            after = side(False, c * z.z) if high else plane(z, mobile, c, x + 1)
            v = plane(z, moles, c, x) - own * g + (ax * after + bx * before)
            v = v + (ay * lane_roll(g, -1) + by * lane_roll(g, 1))
            v = v + w2 * plane(z, mobile_m, c, x)
            new[pl.ds(pl.multiple_of(c * z.cells + x * z.z, z.z), z.z), :] = v

    at(0, True, False)

    def middle(x, carry):
        at(x, False, False)
        return carry

    lax.fori_loop(1, z.x - 1, middle, 0)
    at(z.x - 1, False, True)


def frac_kernel(
    z, t, k_ref, tab, moles, mobile, mobile_m, coef, fa, fb, new, mobile_new, frac_a, frac_b
):
    frac_update(z, t, tab, moles, mobile, mobile_m, coef, fa, fb, new)
    flash_field(z, new, mobile_new, k_ref)
    frac_messages(z, mobile_new, coef, tab, t + 1, frac_a, frac_b)


def last_frac_kernel(z, t, tab, moles, mobile, mobile_m, coef, fa, fb, back, new):
    frac_update(z, t, tab, moles, mobile, mobile_m, coef, fa, fb, new)
    lane_tile = z.tiles_back * SUB
    stride = z.jt * lane_tile
    to_sub = tab[pl.ds(6 * SUB, SUB), :]
    code = tab[pl.ds(7 * SUB, SUB), :]

    def channel(c, carry):
        for j in range(z.jt):
            tiles = []
            for xi in range(z.xt):
                x = z.xt * j + xi
                got = jnp.zeros((SUB, LANES), F32)
                for h in range(2):
                    row = c * z.cells + x * z.z + h * SUB
                    v = new[pl.ds(pl.multiple_of(row, SUB), SUB), :]
                    for n in range(z.by):
                        got = jnp.where(
                            code == 2 * n + h, sub_gather(lane_roll(v, n * z.ps), to_sub), got
                        )
                tiles.append(got)
            for n, v in enumerate(group_transpose(tiles, z.ps)):
                g, k = divmod(n, z.most)
                start = g * SUB * stride + j * lane_tile + c * z.most + k
                back[pl.ds(start, SUB, stride=stride), :] = v
        return carry

    lax.fori_loop(0, z.nc, channel, 0)


def swap(value, axis, ahead):
    count = lax.axis_size(axis)
    if ahead:
        pairs = [(i, i ^ 1) for i in range(count)]
    else:
        pairs = [(i, (i - 1 if i % 2 == 0 else i + 1) % count) for i in range(count)]
    return lax.ppermute(value, axis, pairs)


def call(kernel, name, in_specs, out_shape, args, scratch=(), mib=24, flops=10**8):
    bytes_accessed = sum(a.size * 4 for a in args)
    return pl.pallas_call(
        kernel,
        name=name,
        out_shape=out_shape,
        in_specs=in_specs,
        out_specs=jax.tree.map(lambda _: VMEM, out_shape),
        scratch_shapes=scratch,
        compiler_params=pltpu.CompilerParams(vmem_limit_bytes=mib << 20),
        cost_estimate=pl.CostEstimate(
            flops=flops, bytes_accessed=bytes_accessed, transcendentals=0
        ),
    )(*args)


def shape(rows, lanes=LANES, dtype=F32):
    return jax.ShapeDtypeStruct((rows, lanes), dtype)


def local(
    matrix_moles,
    pore_matrix,
    matrix_rate,
    matrix_upwind,
    frac_moles,
    pore_frac,
    frac_rate,
    frac_upwind,
    ff_open,
    kvalues,
    slot_patch,
    patch_block,
):
    z = Sizes(matrix_moles, frac_moles)
    bind = lambda f, *a: functools.partial(f, z, *a)
    block_flat = patch_block.reshape(-1)
    moles = matrix_moles.reshape(-1, z.y)
    pore = pore_matrix.reshape(-1, z.y)
    rate = matrix_rate.reshape(-1, z.y)
    upwind = matrix_upwind.reshape(-1, z.y)
    field = shape(z.nc * z.cells)
    msg_w, msg_d = shape((z.nc + 1) * z.z), shape((z.nc + 1) * z.x)

    send = call(
        bind(pack_kernel), "pack", [SMEM] * 2 + [VMEM] * 5,
        shape(z.wide * z.jt * z.tiles_out * SUB),
        (
            slot_patch,
            block_flat,
            frac_moles.reshape(-1, z.pc),
            pore_frac,
            frac_rate.reshape(-1, z.pc),
            frac_upwind.reshape(-1, z.pc),
            ff_open,
        ),
        scratch=[pltpu.VMEM((z.tiles_out * z.cpt * z.slots, z.pc), F32)],
    )
    recv = lax.all_to_all(send, "wide", split_axis=0, concat_axis=0, tiled=True)
    mobile_m, wa, wb, da, db, tab = call(
        bind(first_matrix_kernel), "matrix_first", [SMEM] * 3 + [VMEM] * 3,
        (field, msg_w, msg_w, msg_d, msg_d, shape(8 * SUB, dtype=I32)),
        (kvalues, slot_patch, block_flat, moles, rate, upwind),
    )

    def exchange_m(wa, wb, da, db):
        return (
            swap(wa, "wide", True),
            swap(wb, "wide", False),
            swap(da, "depth", True),
            swap(db, "depth", False),
        )

    halos = exchange_m(wa, wb, da, db)
    moles_f, mobile_f, coef, fa, fb = call(
        bind(first_frac_kernel), "frac_first", [SMEM] + [VMEM] * 2,
        (field, field, shape((z.out_ch - z.nc) * z.cells), msg_w, msg_w),
        (kvalues, tab, recv),
    )
    fa, fb = swap(fa, "wide", True), swap(fb, "wide", False)
    for t in range(SUBSTEPS - 1):
        moles, mobile_m_new, wa, wb, da, db = call(
            bind(matrix_kernel, t), "matrix_step", [SMEM] + [VMEM] * 11,
            (field, field, msg_w, msg_w, msg_d, msg_d),
            (kvalues, moles, mobile_m, mobile_f, coef, rate, upwind, pore, *halos),
        )
        halos = exchange_m(wa, wb, da, db)
        moles_f, mobile_f, fa, fb = call(
            bind(frac_kernel, t), "frac_step", [SMEM] + [VMEM] * 7,
            (field, field, msg_w, msg_w),
            (kvalues, tab, moles_f, mobile_f, mobile_m, coef, fa, fb),
        )
        mobile_m = mobile_m_new
        fa, fb = swap(fa, "wide", True), swap(fb, "wide", False)
    t = SUBSTEPS - 1
    back = call(
        bind(last_frac_kernel, t), "frac_last", [VMEM] * 7,
        shape(z.wide * z.jt * z.tiles_back * SUB),
        (tab, moles_f, mobile_f, mobile_m, coef, fa, fb),
        scratch=[pltpu.VMEM((z.nc * z.cells, LANES), F32)],
    )
    returned = lax.all_to_all(back, "wide", split_axis=0, concat_axis=0, tiled=True)
    moles = call(
        bind(matrix_kernel, t), "matrix_last", [SMEM] + [VMEM] * 11,
        field,
        (kvalues, moles, mobile_m, mobile_f, coef, rate, upwind, pore, *halos),
    )
    frac = call(
        bind(spread_kernel), "spread", [SMEM] * 2 + [VMEM],
        shape(z.nc * z.slots, z.pc),
        (slot_patch, block_flat, returned),
    )
    return moles.reshape(matrix_moles.shape), frac.reshape(frac_moles.shape)


def solution(mesh):
    placed = (
        P(None, "wide", "depth", None),
        P("wide", "depth", None),
        P(None, "wide", "depth", None),
        P(None, None, "wide", "depth", None),
        P(None, ("wide", "depth"), None),
        P(("wide", "depth"), None),
        P(None, ("wide", "depth"), None),
        P(None, None, ("wide", "depth"), None),
        P(("wide", "depth"), None),
        P(),
        P(),
        P(),
    )
    return jax.shard_map(
        local,
        mesh=mesh,
        in_specs=placed,
        out_specs=(P(None, "wide", "depth", None), P(None, ("wide", "depth"), None)),
        check_vma=False,
    )
```

profile of v0, /device:TPU:0, one launch (start us, length us, event | category | flops | bytes accessed | tf_op | source)
XLA Modules:
  0.0 116.6 jit_solution(11757990433652093299)
XLA Ops:
  0.6 0.8 copy.16.openings
  1.4 0.8 copy.15
  2.2 0.2 reshape.39.block_ref
  2.4 1.0 copy-done.18
  3.5 0.9 copy-done.22
  4.4 0.9 copy-done.23
  5.3 0.8 copy-done.24
  6.0 0.7 copy-done.26
  6.7 0.9 pack.1
  7.6 1.2 %copy-done.10 = f32[3328,128]{1,0:T(8,128)} copy-done((f32[3328,128]{1,0:T(8,128)}, f32[3328,128]{1,0:T(8,128)S(1)}, u32[]{:S(2)}) %copy-start.10) | copy-done | bytes 1703960
  8.8 5.5 %all-to-all-start = ((f32[8,416,128]{2,1,0:T(8,128)}), f32[8,416,128]{2,1,0:T(8,128)}, u32[]{:S(2)}, u32[]{:S(2)}) async-start(f32[8,416,128]{2,1,0:T(8,128)} %bitcast.18), calls=%async_computation | async-start | bytes 3407872 | tf_op jit(solution)/shard_map/all_to_all | solution.py:631
  14.4 4.2 %matrix_first.1 = (f32[4096,128]{1,0:T(8,128)S(1)}, f32[272,128]{1,0:T(8,128)S(1)}, f32[272,128]{1,0:T(8,128)S(1)}, f32[272,128]{1,0:T(8,128)S(1)}, f32[272,128]{1,0:T(8,128)S(1)}, /*index=5*/s32[64,128]{1,0:T(8,128)S(1)}) custom-call(f32[16]{0:T(128)S(1)} %copy-done.25, s32[256]{0:T(256)S(1)} %copy-done.27, s32[768]{0:T(1024)S(1)} %reshape.39.block_ref, ...), custom_call_target="tpu_custom_call" | custom-call | flops 100000000 | bytes 3280960 | tf_op jit(solution)/shard_map/matrix_first/pallas_call | solution.py:575
  18.6 1.3 %copy-done.3 = f32[4096,128]{1,0:T(8,128)} copy-done((f32[4096,128]{1,0:T(8,128)}, f32[4096,128]{1,0:T(8,128)S(1)}, u32[]{:S(2)}) %copy-start.3) | copy-done | bytes 2097176
  19.9 0.6 copy-done.28
  20.6 0.7 copy-done.29
  21.2 0.7 copy-done.30
  21.9 0.7 copy-done.31
  22.6 14.3 %all-to-all-done = f32[8,416,128]{2,1,0:T(8,128)} async-done(((f32[8,416,128]{2,1,0:T(8,128)}), f32[8,416,128]{2,1,0:T(8,128)}, u32[]{:S(2)}, u32[]{:S(2)}) %all-to-all-start) | async-done | bytes 1703968 | tf_op jit(solution)/shard_map/all_to_all | solution.py:631
  36.8 11.4 %frac_first.1 = (f32[4096,128]{1,0:T(8,128)S(1)}, f32[4096,128]{1,0:T(8,128)S(1)}, f32[2560,128]{1,0:T(8,128)S(1)}, f32[272,128]{1,0:T(8,128)S(1)}, f32[272,128]{1,0:T(8,128)S(1)}) custom-call(f32[16]{0:T(128)S(1)} %copy-done.25, s32[64,128]{1,0:T(8,128)S(1)} %get-tuple-element.24.tab, f32[3328,128]{1,0:T(8,128)} %bitcast.7.recv), custom_call_target="tpu_custom_call" | custom-call | flops 100000000 | bytes 1736768 | tf_op jit(solution)/shard_map/frac_first/pallas_call | solution.py:575
  48.2 0.1 collective-permute-start.4
  48.3 0.7 collective-permute-start.5
  49.0 2.0 %collective-permute-start.1 = (f32[272,128]{1,0:T(8,128)}, f32[272,128]{1,0:T(8,128)S(1)}, u32[]{:S(2)}, u32[]{:S(2)}) collective-permute-start(f32[272,128]{1,0:T(8,128)} %copy-done.30), channel_id=1, source_target_pairs={{0,28},{4,8},{8,4},{12,16},{16,12},{20,24},{24,20},{28,0},{1,29},{... | collective-permute-start | bytes 417800 | tf_op jit(solution)/shard_map/ppermute | solution.py:570
  51.0 2.1 %collective-permute-start.2 = (f32[272,128]{1,0:T(8,128)}, f32[272,128]{1,0:T(8,128)S(1)}, u32[]{:S(2)}, u32[]{:S(2)}) collective-permute-start(f32[272,128]{1,0:T(8,128)} %copy-done.29), channel_id=1, source_target_pairs={{0,1},{1,0},{2,3},{3,2},{4,5},{5,4},{6,7},{7,6},{8,9},{9,8},{10,11... | collective-permute-start | bytes 417800 | tf_op jit(solution)/shard_map/ppermute | solution.py:570
  53.1 2.5 %collective-permute-start.3 = (f32[272,128]{1,0:T(8,128)}, f32[272,128]{1,0:T(8,128)S(1)}, u32[]{:S(2)}, u32[]{:S(2)}) collective-permute-start(f32[272,128]{1,0:T(8,128)} %copy-done.28), channel_id=1, source_target_pairs={{0,3},{1,2},{2,1},{3,0},{4,7},{5,6},{6,5},{7,4},{8,11},{9,10},{10,... | collective-permute-start | bytes 417800 | tf_op jit(solution)/shard_map/ppermute | solution.py:570
  55.5 1.6 %copy-done.4 = f32[4096,128]{1,0:T(8,128)S(1)} copy-done((f32[4096,128]{1,0:T(8,128)S(1)}, f32[4096,128]{1,0:T(8,128)}, u32[]{:S(2)}) %copy-start.4) | copy-done | bytes 2097176
  57.1 0.8 copy-done.20
  57.9 5.9 %frac_step.1 = (f32[4096,128]{1,0:T(8,128)S(1)}, f32[4096,128]{1,0:T(8,128)S(1)}, f32[272,128]{1,0:T(8,128)S(1)}, f32[272,128]{1,0:T(8,128)S(1)}) custom-call(f32[16]{0:T(128)S(1)} %copy-done.25, s32[64,128]{1,0:T(8,128)S(1)} %copy-done.20, f32[4096,128]{1,0:T(8,128)S(1)} %get-tuple-element.33.moles, f32[4096,128]{1,0:T(8,128)S(1)} %get-tuple-element.25.mobile_f.mobile, ...), custom_call_target="tpu_custom_call" | custom-call | flops 100000000 | bytes 7913536 | tf_op jit(solution)/shard_map/frac_step/pallas_call | solution.py:575
  63.8 0.1 collective-permute-start.10
  63.9 1.0 collective-permute-start.11
  65.0 6.0 %matrix_step.1 = (f32[4096,128]{1,0:T(8,128)S(1)}, f32[4096,128]{1,0:T(8,128)S(1)}, f32[272,128]{1,0:T(8,128)S(1)}, f32[272,128]{1,0:T(8,128)S(1)}, f32[272,128]{1,0:T(8,128)S(1)}, /*index=5*/f32[272,128]{1,0:T(8,128)S(1)}) custom-call(f32[16]{0:T(128)S(1)} %copy-done.25, f32[4096,128]{1,0:T(8,128)S(1)} %bitcast.14, f32[4096,128]{1,0:T(8,128)S(1)} %copy-done.4, ...), custom_call_target="tpu_custom_call" | custom-call | flops 100000000 | bytes 9470016 | tf_op jit(solution)/shard_map/matrix_step/pallas_call | solution.py:575
  71.0 0.7 copy-done.32
  71.7 0.7 copy-done.33
  72.3 0.7 copy-done.34
  73.0 0.7 copy-done.35
  73.7 7.8 %frac_last.1 = f32[2048,128]{1,0:T(8,128)S(1)} custom-call(s32[64,128]{1,0:T(8,128)S(1)} %copy-done.21, f32[4096,128]{1,0:T(8,128)S(1)} %get-tuple-element.41.moles, f32[4096,128]{1,0:T(8,128)S(1)} %get-tuple-element.36.mobile_f.mobile, f32[4096,128]{1,0:T(8,128)S(1)} %get-tuple-element.32.mobile.mobile_m, f32[2560,128]{1,0:T(8,128)S(1)} %get-tuple-element.26.coef, ...), custom_call_target="tpu_custom_call" | custom-call | flops 100000000 | bytes 7913472 | tf_op jit(solution)/shard_map/frac_last/pallas_call | solution.py:575
  81.6 1.0 copy-done.11
  82.5 4.4 %all-to-all-start.1 = ((f32[8,256,128]{2,1,0:T(8,128)}), f32[8,256,128]{2,1,0:T(8,128)}, u32[]{:S(2)}, u32[]{:S(2)}) async-start(f32[8,256,128]{2,1,0:T(8,128)} %bitcast.19), calls=%async_computation.1 | async-start | bytes 2097152 | tf_op jit(solution)/shard_map/all_to_all | solution.py:674
  86.9 0.4 collective-permute-start.6
  87.3 2.6 %collective-permute-start.7 = (f32[272,128]{1,0:T(8,128)}, f32[272,128]{1,0:T(8,128)S(1)}, u32[]{:S(2)}, u32[]{:S(2)}) collective-permute-start(f32[272,128]{1,0:T(8,128)} %copy-done.34), channel_id=1, source_target_pairs={{0,28},{4,8},{8,4},{12,16},{16,12},{20,24},{24,20},{28,0},{1,29},{... | collective-permute-start | bytes 417800 | tf_op jit(solution)/shard_map/ppermute | solution.py:570
  89.9 1.4 %collective-permute-start.8 = (f32[272,128]{1,0:T(8,128)}, f32[272,128]{1,0:T(8,128)S(1)}, u32[]{:S(2)}, u32[]{:S(2)}) collective-permute-start(f32[272,128]{1,0:T(8,128)} %copy-done.33), channel_id=1, source_target_pairs={{0,1},{1,0},{2,3},{3,2},{4,5},{5,4},{6,7},{7,6},{8,9},{9,8},{10,11... | collective-permute-start | bytes 417800 | tf_op jit(solution)/shard_map/ppermute | solution.py:570
  91.3 2.5 %collective-permute-start.9 = (f32[272,128]{1,0:T(8,128)}, f32[272,128]{1,0:T(8,128)S(1)}, u32[]{:S(2)}, u32[]{:S(2)}) collective-permute-start(f32[272,128]{1,0:T(8,128)} %copy-done.32), channel_id=1, source_target_pairs={{0,3},{1,2},{2,1},{3,0},{4,7},{5,6},{6,5},{7,4},{8,11},{9,10},{10,... | collective-permute-start | bytes 417800 | tf_op jit(solution)/shard_map/ppermute | solution.py:570
  93.7 10.9 %collective-permute-done.7.hb = f32[272,128]{1,0:T(8,128)S(1)} collective-permute-done((f32[272,128]{1,0:T(8,128)}, f32[272,128]{1,0:T(8,128)S(1)}, u32[]{:S(2)}, u32[]{:S(2)}) %collective-permute-start.7) | collective-permute-done | bytes 139296 | tf_op jit(solution)/shard_map/ppermute | solution.py:570
  104.6 1.6 %copy-done.6 = f32[4096,128]{1,0:T(8,128)S(1)} copy-done((f32[4096,128]{1,0:T(8,128)S(1)}, f32[4096,128]{1,0:T(8,128)}, u32[]{:S(2)}) %copy-start.6) | copy-done | bytes 2097176
  106.2 1.1 copy-done.9
  107.4 1.0 copy-done.14
  108.4 1.6 %copy-done.16 = f32[4096,128]{1,0:T(8,128)S(1)} copy-done((f32[4096,128]{1,0:T(8,128)S(1)}, f32[4096,128]{1,0:T(8,128)}, u32[]{:S(2)}) %copy-start.16) | copy-done | bytes 2097176
  109.9 4.4 %matrix_last.1 = f32[4096,128]{1,0:T(8,128)} custom-call(f32[16]{0:T(128)S(1)} %copy-done.25, f32[4096,128]{1,0:T(8,128)S(1)} %copy-done.16, f32[4096,128]{1,0:T(8,128)S(1)} %copy-done.6, f32[4096,128]{1,0:T(8,128)S(1)} %copy-done.2, f32[2560,128]{1,0:T(8,128)S(1)} %get-tuple-element.26.coef, f32[768,128]{1,0:T(8,128)S(1)} %bitcast.22, ...), custom_call_target="tpu_custom_call" | custom-call | flops 100000000 | bytes 9470016 | tf_op jit(solution)/shard_map/matrix_last/pallas_call | solution.py:575
  114.4 2.2 %spread.1 = f32[128,1024]{1,0:T(8,128)} custom-call(s32[256]{0:T(256)S(1)} %copy-done.27, s32[768]{0:T(1024)S(1)} %reshape.39.block_ref, f32[2048,128]{1,0:T(8,128)} %bitcast.11.recv), custom_call_target="tpu_custom_call" | custom-call | flops 100000000 | bytes 1052672 | tf_op jit(solution)/shard_map/spread/pallas_call | solution.py:575
  (63 shorter events, 0.1 us)
Async XLA Ops:
  2.4 1.0 copy-start.18
  3.5 0.9 copy-start.22
  4.4 0.9 copy-start.23
  5.3 0.8 copy-start.24
  6.0 0.7 copy-start.26
  7.6 1.2 %copy-start.10 = (f32[3328,128]{1,0:T(8,128)}, f32[3328,128]{1,0:T(8,128)S(1)}, u32[]{:S(2)}) copy-start(f32[3328,128]{1,0:T(8,128)S(1)} %pack.1) | copy-start | bytes 5111812
  8.8 5.5 %copy-start = (f32[16,16,16,128]{3,2,1,0:T(8,128)S(1)}, f32[16,16,16,128]{3,2,1,0:T(8,128)}, u32[]{:S(2)}) copy-start(f32[16,16,16,128]{3,2,1,0:T(8,128)} %param.12) | copy-start | bytes 6291460
  8.8 5.5 %copy-start.7 = (s32[2,3,16,16,128]{4,3,2,1,0:T(8,128)S(1)}, s32[2,3,16,16,128]{4,3,2,1,0:T(8,128)}, u32[]{:S(2)}) copy-start(s32[2,3,16,16,128]{4,3,2,1,0:T(8,128)} %param.15) | copy-start | bytes 2359300
  8.8 5.5 %copy-start.12 = (f32[3,16,16,128]{3,2,1,0:T(8,128)S(1)}, f32[3,16,16,128]{3,2,1,0:T(8,128)}, u32[]{:S(2)}) copy-start(f32[3,16,16,128]{3,2,1,0:T(8,128)} %param.14) | copy-start | bytes 1179652
  8.8 5.5 %copy-start.25 = (f32[16]{0:T(128)S(1)}, f32[16]{0:T(128)}, u32[]{:S(2)}) copy-start(f32[16]{0:T(128)} %k_ref.9) | copy-start | bytes 196
  8.8 5.5 %copy-start.27 = (s32[256]{0:T(256)S(1)}, s32[256]{0:T(256)}, u32[]{:S(2)}) copy-start(s32[256]{0:T(256)} %slot_ref.5) | copy-start | bytes 3076
  8.8 28.0 %all-to-all-start = ((f32[8,416,128]{2,1,0:T(8,128)}), f32[8,416,128]{2,1,0:T(8,128)}, u32[]{:S(2)}, u32[]{:S(2)}) async-start(f32[8,416,128]{2,1,0:T(8,128)} %bitcast.18), calls=%async_computation | async-start | bytes 3407872 | tf_op jit(solution)/shard_map/all_to_all | solution.py:631
  18.6 1.3 %copy-start.3 = (f32[4096,128]{1,0:T(8,128)}, f32[4096,128]{1,0:T(8,128)S(1)}, u32[]{:S(2)}) copy-start(f32[4096,128]{1,0:T(8,128)S(1)} %get-tuple-element.23.mobile.mobile_m) | copy-start | bytes 6291460
  20.6 0.7 copy-start.29
  21.2 0.7 copy-start.30
  21.9 0.7 copy-start.31
  22.6 33.0 %copy-start.19 = (s32[64,128]{1,0:T(8,128)}, s32[64,128]{1,0:T(8,128)S(1)}, u32[]{:S(2)}) copy-start(s32[64,128]{1,0:T(8,128)S(1)} %get-tuple-element.24.tab) | copy-start | bytes 98308
  48.2 4.9 %collective-permute-start.4 = (f32[272,128]{1,0:T(8,128)S(1)}, f32[272,128]{1,0:T(8,128)S(1)}, u32[]{:S(2)}, u32[]{:S(2)}) collective-permute-start(f32[272,128]{1,0:T(8,128)S(1)} %get-tuple-element.34), channel_id=1, source_target_pairs={{0,4},{4,0},{8,12},{12,8},{16,20},{20,16},{24,28},{28,24},{1,5},{5... | collective-permute-start | bytes 417800 | tf_op jit(solution)/shard_map/ppermute | solution.py:570
  48.3 7.3 %collective-permute-start.5 = (f32[272,128]{1,0:T(8,128)S(1)}, f32[272,128]{1,0:T(8,128)S(1)}, u32[]{:S(2)}, u32[]{:S(2)}) collective-permute-start(f32[272,128]{1,0:T(8,128)S(1)} %get-tuple-element.35), channel_id=1, source_target_pairs={{0,28},{4,8},{8,4},{12,16},{16,12},{20,24},{24,20},{28,0},{1,29},{... | collective-permute-start | bytes 417800 | tf_op jit(solution)/shard_map/ppermute | solution.py:570
  49.0 14.9 %collective-permute-start = (f32[272,128]{1,0:T(8,128)}, f32[272,128]{1,0:T(8,128)S(1)}, u32[]{:S(2)}, u32[]{:S(2)}) collective-permute-start(f32[272,128]{1,0:T(8,128)} %copy-done.31), channel_id=1, source_target_pairs={{0,4},{4,0},{8,12},{12,8},{16,20},{20,16},{24,28},{28,24},{1,5},{5... | collective-permute-start | bytes 417800 | tf_op jit(solution)/shard_map/ppermute | solution.py:570
  49.0 15.9 %collective-permute-start.1 = (f32[272,128]{1,0:T(8,128)}, f32[272,128]{1,0:T(8,128)S(1)}, u32[]{:S(2)}, u32[]{:S(2)}) collective-permute-start(f32[272,128]{1,0:T(8,128)} %copy-done.30), channel_id=1, source_target_pairs={{0,28},{4,8},{8,4},{12,16},{16,12},{20,24},{24,20},{28,0},{1,29},{... | collective-permute-start | bytes 417800 | tf_op jit(solution)/shard_map/ppermute | solution.py:570
  51.0 13.9 %collective-permute-start.2 = (f32[272,128]{1,0:T(8,128)}, f32[272,128]{1,0:T(8,128)S(1)}, u32[]{:S(2)}, u32[]{:S(2)}) collective-permute-start(f32[272,128]{1,0:T(8,128)} %copy-done.29), channel_id=1, source_target_pairs={{0,1},{1,0},{2,3},{3,2},{4,5},{5,4},{6,7},{7,6},{8,9},{9,8},{10,11... | collective-permute-start | bytes 417800 | tf_op jit(solution)/shard_map/ppermute | solution.py:570
  53.1 11.9 %collective-permute-start.3 = (f32[272,128]{1,0:T(8,128)}, f32[272,128]{1,0:T(8,128)S(1)}, u32[]{:S(2)}, u32[]{:S(2)}) collective-permute-start(f32[272,128]{1,0:T(8,128)} %copy-done.28), channel_id=1, source_target_pairs={{0,3},{1,2},{2,1},{3,0},{4,7},{5,6},{6,5},{7,4},{8,11},{9,10},{10,... | collective-permute-start | bytes 417800 | tf_op jit(solution)/shard_map/ppermute | solution.py:570
  55.5 1.6 %copy-start.4 = (f32[4096,128]{1,0:T(8,128)S(1)}, f32[4096,128]{1,0:T(8,128)}, u32[]{:S(2)}) copy-start(f32[4096,128]{1,0:T(8,128)} %copy-done.3) | copy-start | bytes 6291460
  57.1 0.8 copy-start.20
  57.9 7.0 %copy-start.8 = (s32[2,3,16,16,128]{4,3,2,1,0:T(8,128)S(1)}, s32[2,3,16,16,128]{4,3,2,1,0:T(8,128)}, u32[]{:S(2)}) copy-start(s32[2,3,16,16,128]{4,3,2,1,0:T(8,128)} %param.15) | copy-start | bytes 2359300
  57.9 7.0 %copy-start.13 = (f32[3,16,16,128]{3,2,1,0:T(8,128)S(1)}, f32[3,16,16,128]{3,2,1,0:T(8,128)}, u32[]{:S(2)}) copy-start(f32[3,16,16,128]{3,2,1,0:T(8,128)} %param.14) | copy-start | bytes 1179652
  57.9 7.0 %copy-start.17 = (f32[16,16,128]{2,1,0:T(8,128)S(1)}, f32[16,16,128]{2,1,0:T(8,128)}, u32[]{:S(2)}) copy-start(f32[16,16,128]{2,1,0:T(8,128)} %param.13) | copy-start | bytes 393220
  63.8 9.9 %copy-start.1 = (f32[4096,128]{1,0:T(8,128)}, f32[4096,128]{1,0:T(8,128)S(1)}, u32[]{:S(2)}) copy-start(f32[4096,128]{1,0:T(8,128)S(1)} %get-tuple-element.36.mobile_f.mobile) | copy-start | bytes 6291460
  63.8 9.9 %collective-permute-start.10 = (f32[272,128]{1,0:T(8,128)S(1)}, f32[272,128]{1,0:T(8,128)S(1)}, u32[]{:S(2)}, u32[]{:S(2)}) collective-permute-start(f32[272,128]{1,0:T(8,128)S(1)} %get-tuple-element.42), channel_id=1, source_target_pairs={{0,4},{4,0},{8,12},{12,8},{16,20},{20,16},{24,28},{28,24},{1,5},{5... | collective-permute-start | bytes 417800 | tf_op jit(solution)/shard_map/ppermute | solution.py:570
  63.9 9.8 %collective-permute-start.11 = (f32[272,128]{1,0:T(8,128)S(1)}, f32[272,128]{1,0:T(8,128)S(1)}, u32[]{:S(2)}, u32[]{:S(2)}) collective-permute-start(f32[272,128]{1,0:T(8,128)S(1)} %get-tuple-element.43), channel_id=1, source_target_pairs={{0,28},{4,8},{8,4},{12,16},{16,12},{20,24},{24,20},{28,0},{1,29},{... | collective-permute-start | bytes 417800 | tf_op jit(solution)/shard_map/ppermute | solution.py:570
  65.0 8.7 %copy-start.21 = (s32[64,128]{1,0:T(8,128)S(1)}, s32[64,128]{1,0:T(8,128)}, u32[]{:S(2)}) copy-start(s32[64,128]{1,0:T(8,128)} %copy-done.19) | copy-start | bytes 98308
  71.0 0.7 copy-start.32
  71.7 0.7 copy-start.33
  73.0 0.7 copy-start.35
  73.7 7.9 %copy-start.5 = (f32[4096,128]{1,0:T(8,128)}, f32[4096,128]{1,0:T(8,128)S(1)}, u32[]{:S(2)}) copy-start(f32[4096,128]{1,0:T(8,128)S(1)} %get-tuple-element.32.mobile.mobile_m) | copy-start | bytes 6291460
  73.7 7.9 %copy-start.15 = (f32[4096,128]{1,0:T(8,128)}, f32[4096,128]{1,0:T(8,128)S(1)}, u32[]{:S(2)}) copy-start(f32[4096,128]{1,0:T(8,128)S(1)} %get-tuple-element.31.moles) | copy-start | bytes 6291460
  81.5 1.0 copy-start.11
  82.5 22.1 %copy-start.2 = (f32[4096,128]{1,0:T(8,128)S(1)}, f32[4096,128]{1,0:T(8,128)}, u32[]{:S(2)}) copy-start(f32[4096,128]{1,0:T(8,128)} %copy-done.1) | copy-start | bytes 6291460
  82.5 31.8 %all-to-all-start.1 = ((f32[8,256,128]{2,1,0:T(8,128)}), f32[8,256,128]{2,1,0:T(8,128)}, u32[]{:S(2)}, u32[]{:S(2)}) async-start(f32[8,256,128]{2,1,0:T(8,128)} %bitcast.19), calls=%async_computation.1 | async-start | bytes 2097152 | tf_op jit(solution)/shard_map/all_to_all | solution.py:674
  86.9 6.8 %collective-permute-start.6 = (f32[272,128]{1,0:T(8,128)}, f32[272,128]{1,0:T(8,128)S(1)}, u32[]{:S(2)}, u32[]{:S(2)}) collective-permute-start(f32[272,128]{1,0:T(8,128)} %copy-done.35), channel_id=1, source_target_pairs={{0,4},{4,0},{8,12},{12,8},{16,20},{20,16},{24,28},{28,24},{1,5},{5... | collective-permute-start | bytes 417800 | tf_op jit(solution)/shard_map/ppermute | solution.py:570
  87.3 17.3 %collective-permute-start.7 = (f32[272,128]{1,0:T(8,128)}, f32[272,128]{1,0:T(8,128)S(1)}, u32[]{:S(2)}, u32[]{:S(2)}) collective-permute-start(f32[272,128]{1,0:T(8,128)} %copy-done.34), channel_id=1, source_target_pairs={{0,28},{4,8},{8,4},{12,16},{16,12},{20,24},{24,20},{28,0},{1,29},{... | collective-permute-start | bytes 417800 | tf_op jit(solution)/shard_map/ppermute | solution.py:570
  89.9 14.8 %collective-permute-start.8 = (f32[272,128]{1,0:T(8,128)}, f32[272,128]{1,0:T(8,128)S(1)}, u32[]{:S(2)}, u32[]{:S(2)}) collective-permute-start(f32[272,128]{1,0:T(8,128)} %copy-done.33), channel_id=1, source_target_pairs={{0,1},{1,0},{2,3},{3,2},{4,5},{5,4},{6,7},{7,6},{8,9},{9,8},{10,11... | collective-permute-start | bytes 417800 | tf_op jit(solution)/shard_map/ppermute | solution.py:570
  91.3 13.4 %collective-permute-start.9 = (f32[272,128]{1,0:T(8,128)}, f32[272,128]{1,0:T(8,128)S(1)}, u32[]{:S(2)}, u32[]{:S(2)}) collective-permute-start(f32[272,128]{1,0:T(8,128)} %copy-done.32), channel_id=1, source_target_pairs={{0,3},{1,2},{2,1},{3,0},{4,7},{5,6},{6,5},{7,4},{8,11},{9,10},{10,... | collective-permute-start | bytes 417800 | tf_op jit(solution)/shard_map/ppermute | solution.py:570
  104.6 1.6 %copy-start.6 = (f32[4096,128]{1,0:T(8,128)S(1)}, f32[4096,128]{1,0:T(8,128)}, u32[]{:S(2)}) copy-start(f32[4096,128]{1,0:T(8,128)} %copy-done.5) | copy-start | bytes 6291460
  106.2 1.1 copy-start.9
  107.4 1.0 copy-start.14
  108.3 1.6 %copy-start.16 = (f32[4096,128]{1,0:T(8,128)S(1)}, f32[4096,128]{1,0:T(8,128)}, u32[]{:S(2)}) copy-start(f32[4096,128]{1,0:T(8,128)} %copy-done.15) | copy-start | bytes 6291460
  (2 other events, 1.3 us)
where the time goes:
time: 117 us
  Pallas kernels  42.9 us (37%)
  waiting for transfers between devices  25.2 us (22%)
  starting transfers between devices  25.1 us (21%)
  local copies, waits for them, and re-layouts  22.5 us (19%)
    pallas_call x8, Pallas kernels, call(): pl.pallas_call(kernel, name=name, out_shape=out_shape, in_specs=in_specs,...  42.9 us
    unnamed x74, local copies, waits for them, and re-layouts  22.3 us
    ppermute x12, starting transfers between devices, swap(): return lax.ppermute(value, axis, pairs)  15.3 us
    all_to_all x1, waiting for transfers between devices, local(): recv = lax.all_to_all(send, 'wide', split_axis=0, concat_axis=0, tiled=True)  14.3 us
    ppermute x12, waiting for transfers between devices, swap(): return lax.ppermute(value, axis, pairs)  10.9 us
    all_to_all x1, starting transfers between devices, local(): recv = lax.all_to_all(send, 'wide', split_axis=0, concat_axis=0, tiled=True)  5.47 us
    all_to_all x1, starting transfers between devices, local(): lax.all_to_all(back, 'wide', split_axis=0, concat_axis=0, tiled=True)  4.38 us
  transfers between devices with their start and end apart: 14, of which 2 were waited for; matrix products, arithmetic and copies ran while one was open for 0% of the time, Pallas kernels for 18%

commit v1 on v0

v1 whole, which is shorter than its diff:
```python
import functools

import jax
import jax.numpy as jnp
from jax import lax
from jax.experimental import pallas as pl
from jax.experimental.pallas import tpu as pltpu
from jax.sharding import PartitionSpec as P


SWEEPS = 4
SUBSTEPS = 2
MOBILITY_RATIO = 4.0
LANES = 128
SUB = 8
PARTS = 4
FLASH_PLANES = 2
F32 = jnp.float32
I32 = jnp.int32

VMEM = pl.BlockSpec(memory_space=pltpu.VMEM)
SMEM = pl.BlockSpec(memory_space=pltpu.SMEM)
HBM = pl.BlockSpec(memory_space=pltpu.HBM)


class Sizes:
    def __init__(self, matrix_moles, frac_moles):
        self.wide = lax.axis_size("wide")
        self.depth = lax.axis_size("depth")
        self.nc, self.x, self.z, self.y = matrix_moles.shape
        self.slots, self.pc = frac_moles.shape[1:]
        self.ps = 1
        while self.ps * self.ps < self.pc:
            self.ps *= 2
        self.by = self.y // self.ps
        self.half = self.pc // 2
        self.cols = self.wide // 2
        self.most = max(1, 4 * self.slots // self.wide)
        self.cpt = SUB // self.most
        self.coefs = 4 + 3 * SUBSTEPS
        self.out_ch = self.nc + self.coefs
        self.tiles_out = -(-self.out_ch // self.cpt)
        self.tiles_back = -(-self.nc // self.cpt)
        self.groups = self.wide // SUB
        self.cells = self.x * self.z
        self.places = SUB * self.by
        self.blocks = self.z * self.by
        self.xt = LANES // self.ps
        self.jt = self.half // LANES
        assert self.y == LANES and self.slots == SUB and self.z == 2 * SUB
        assert self.x * self.ps == self.half and self.groups * self.most == self.xt == self.by


def iota(shape, dim):
    return lax.broadcasted_iota(I32, shape, dim)


def lane_roll(v, by):
    by = by % LANES
    return v if by == 0 else pltpu.roll(v, by, 1)


def sub_gather(v, idx):
    return jnp.take_along_axis(v, idx, axis=0, mode="promise_in_bounds")


def group_transpose(a, ps):
    grp = iota((SUB, LANES), 1) // ps
    odd, high = (grp & 1) == 1, (grp & 2) == 2

    def pair(u, v, upper, dist):
        return (
            jnp.where(upper, lane_roll(v, dist), u),
            jnp.where(upper, v, lane_roll(u, -dist)),
        )

    b0, b1 = pair(a[0], a[1], odd, ps)
    c0, c1 = pair(a[2], a[3], odd, ps)
    t0, t2 = pair(b0, c0, high, 2 * ps)
    t1, t3 = pair(b1, c1, high, 2 * ps)
    return [t0, t1, t2, t3]


def tree_sum(terms):
    terms = list(terms)
    while len(terms) > 1:
        terms = [a + b for a, b in zip(terms[::2], terms[1::2])] + (
            [terms[-1]] if len(terms) % 2 else []
        )
    return terms[0]


def flash_block(load, store, excess, first, nc):
    total = tree_sum([load(c) for c in range(nc)])
    vapour = None
    for _ in range(SWEEPS):
        misfits, slopes = [], []
        for c in range(nc):
            if vapour is None:
                p = first[c]
            else:
                p = excess[c] * (1.0 / (1.0 + vapour * excess[c]))
            r = load(c) * p
            misfits.append(r)
            slopes.append(r * p)
        misfit, slope = running(misfits), running(slopes)
        before = 0.5 if vapour is None else vapour
        vapour = jnp.clip(before + misfit / (slope + total), 0.0, 1.0)
    liquid = (1.0 - vapour) * (1.0 - vapour)
    gas = MOBILITY_RATIO * vapour * vapour
    share = gas / (liquid + gas)
    for c in range(nc):
        q = 1.0 / (1.0 + vapour * excess[c])
        store(c, load(c) * q * (1.0 + share * excess[c]))


def running(terms):
    sums = [terms[0], terms[1]]
    for n, t in enumerate(terms[2:]):
        sums[n % 2] = sums[n % 2] + t
    return sums[0] + sums[1]


def k_scalars(k_ref, nc):
    excess = [k_ref[c] - 1.0 for c in range(nc)]
    first = []
    for c in range(nc):
        e = jnp.full((1, LANES), excess[c], F32)
        first.append(e / (1.0 + 0.5 * e))
    return excess, first


def own_slots(z, slot_ref, block_ref, visit):
    me = lax.axis_index("wide") * z.depth + lax.axis_index("depth")
    counts = jnp.int32(0)
    for i in range(z.slots):
        q = slot_ref[me * z.slots + i]
        p0 = block_ref[0, q]
        rank = (counts >> (4 * p0)) & 15
        counts = counts + (jnp.int32(1) << (4 * p0))
        visit(i, p0, rank)


def pack_kernel(
    z, slot_ref, block_ref, open_ref, moles, pore, rate, upwind, out, src, flags, stage,
    in_sem, out_sem,
):
    nc, slots = z.nc, z.slots
    first = nc * slots
    reads = [
        pltpu.make_async_copy(moles, src.at[pl.ds(0, first), :], in_sem.at[0]),
        pltpu.make_async_copy(pore, src.at[pl.ds(first, slots), :], in_sem.at[1]),
        pltpu.make_async_copy(rate, src.at[pl.ds(first + slots, 3 * slots), :], in_sem.at[2]),
        pltpu.make_async_copy(upwind, flags, in_sem.at[3]),
    ]
    for copy in reads:
        copy.start()
    sub = iota((SUB, LANES), 0)
    picks = [jnp.zeros((SUB, LANES), I32) for _ in range(z.cols)]
    opens = [jnp.zeros((SUB, z.pc), I32) for _ in range(2)]
    row_id = iota((SUB, z.pc), 0)

    def visit(i, p0, rank):
        for c in range(z.cols):
            hit = ((sub % z.most) == rank) & (p0 == c)
            picks[c] = jnp.where(hit, i, picks[c])
        for d in range(2):
            opens[d] = jnp.where(row_id == i, open_ref[d, i], opens[d])

    own_slots(z, slot_ref, block_ref, visit)

    def send(c):
        per = z.jt * z.tiles_out * SUB

        def tile(m, carry):
            for h in range(2):
                for j in range(z.jt):
                    v = None
                    for cp in range(z.cpt):
                        part = sub_gather(
                            src[
                                pl.ds(pl.multiple_of((m * z.cpt + cp) * slots, slots), slots),
                                pl.ds(h * z.half + j * LANES, LANES),
                            ],
                            picks[c],
                        )
                        v = part if v is None else jnp.where(sub // z.most >= cp, part, v)
                    row = ((2 * c + h) * z.jt + j) * z.tiles_out * SUB + m * SUB
                    stage[pl.ds(pl.multiple_of(row, SUB), SUB), :] = v
            return carry

        lax.fori_loop(0, z.tiles_out, tile, 0)
        rows = pl.ds(2 * c * per, 2 * per)
        return pltpu.make_async_copy(stage.at[rows, :], out.at[rows, :], out_sem.at[c])

    for copy in reads:
        copy.wait()
    cell = iota((slots, z.pc), 1)
    g = first + slots
    open_x = jnp.where(cell // z.ps < z.ps - 1, 1, opens[0]).astype(F32)
    open_y = jnp.where(cell % z.ps < z.ps - 1, 1, opens[1]).astype(F32)
    src[pl.ds(g, slots), :] = src[pl.ds(g, slots), :] * open_x
    src[pl.ds(g + slots, slots), :] = src[pl.ds(g + slots, slots), :] * open_y
    n_flags = 3 * SUBSTEPS * slots
    src[pl.ds(g + 3 * slots, n_flags), :] = flags[...].astype(F32)
    spare = src.shape[0] - (g + 3 * slots + n_flags)
    if spare:
        src[pl.ds(g + 3 * slots + n_flags, spare), :] = jnp.zeros((spare, z.pc), F32)
    writes = []
    for c in range(z.cols):
        writes.append(send(c))
        writes[-1].start()
    for copy in writes:
        copy.wait()


def spread_kernel(z, slot_ref, block_ref, recv_hbm, out, recv, sem):
    read = pltpu.make_async_copy(recv_hbm, recv, sem)
    read.start()
    sub = iota((SUB, LANES), 0)
    ranks = jnp.zeros((SUB, LANES), I32)
    column = jnp.zeros((SUB, LANES), I32)

    def visit(i, p0, rank):
        nonlocal ranks, column
        ranks = jnp.where(sub == i, rank, ranks)
        column = jnp.where(sub == i, p0, column)

    own_slots(z, slot_ref, block_ref, visit)
    read.wait()

    def tile(m, carry):
        for h in range(2):
            for j in range(z.jt):
                parts = []
                for c in range(z.cols):
                    row = (((2 * c + h) * z.jt + j) * z.tiles_back + m) * SUB
                    parts.append(recv[pl.ds(pl.multiple_of(row, SUB), SUB), :])
                for cp in range(z.cpt):
                    v = sub_gather(parts[0], cp * z.most + ranks)
                    for c in range(1, z.cols):
                        v = jnp.where(
                            column == c, sub_gather(parts[c], cp * z.most + ranks), v
                        )
                    row = (m * z.cpt + cp) * SUB
                    out[
                        pl.ds(pl.multiple_of(row, SUB), SUB),
                        pl.ds(h * z.half + j * LANES, LANES),
                    ] = v
        return carry

    lax.fori_loop(0, z.tiles_back, tile, 0)


def tables(z, slot_ref, block_ref, tab, gather):
    sub, grp = iota((SUB, LANES), 0), iota((SUB, LANES), 1) // z.ps
    bid = [(sub + SUB * h) * z.by + grp for h in range(2)]
    wide, deep = lax.axis_index("wide"), lax.axis_index("depth")
    here, after = wide // 2, jnp.where(wide + 1 < z.wide, (wide + 1) // 2, -1)

    def visit(w, state):
        v0, v1, n0, n1 = state
        counts = jnp.int32(0)
        for i in range(z.slots):
            q = slot_ref[(w * z.depth + deep) * z.slots + i]
            p0 = block_ref[0, q]
            block = lax.rem(block_ref[1, q], z.z) * z.by + block_ref[2, q]
            rank = (counts >> (4 * p0)) & 15
            counts = counts + (jnp.int32(1) << (4 * p0))
            place = lax.rem(w, SUB) + SUB * (lax.div(w, SUB) * z.most + rank)
            b_here = jnp.where(p0 == here, block, -1)
            b_next = jnp.where(p0 == after, block, -1)
            v0 = jnp.where(bid[0] == b_here, place, v0)
            v1 = jnp.where(bid[1] == b_here, place, v1)
            n0 = jnp.where(bid[0] == b_next, 1, n0)
            n1 = jnp.where(bid[1] == b_next, 1, n1)
            column = lax.rem(block, z.by) * z.z + lax.div(block, z.by)

            @pl.when(p0 == here)
            def _():
                gather[pl.ds(place, 1), :] = (
                    (lane % z.blocks == column) & (lane < 3 * z.blocks)
                ).astype(F32)

        return v0, v1, n0, n1

    gather[...] = jnp.zeros(gather.shape, F32)
    lane = iota((1, gather.shape[1]), 1)
    zero = jnp.zeros((SUB, LANES), I32)
    v0, v1, n0, n1 = lax.fori_loop(0, z.wide, visit, (zero - 1, zero - 1, zero, zero))
    for h, (v, n) in enumerate(((v0, n0), (v1, n1))):
        rows = pl.ds(h * SUB, SUB)
        tab[rows, :] = jnp.where(v >= 0, v & (SUB - 1), 0)
        tab[pl.ds(2 * SUB + h * SUB, SUB), :] = jnp.where(
            v >= 0, (grp - (v >> 3)) & (z.by - 1), -1
        )
        tab[pl.ds(4 * SUB + h * SUB, SUB), :] = n


def split3(v):
    hi = v.astype(jnp.bfloat16)
    rest = v - hi.astype(F32)
    mid = rest.astype(jnp.bfloat16)
    low = (rest - mid.astype(F32)).astype(jnp.bfloat16)
    return jnp.concatenate([hi, mid, low], axis=0)


def field_to_rows(z, src, first_row, gather, back, c):
    lane_tile = z.tiles_back * SUB
    stride = z.jt * lane_tile
    for jj in range(0, z.jt, 2):
        columns = []
        for n in range(2):
            parts = [None] * (z.by * (z.z // SUB))
            for h in range(z.z // SUB):
                tiles_x = []
                for xi in range(z.xt):
                    row = first_row + (z.xt * (jj + n) + xi) * z.z + h * SUB
                    tiles_x.append(src[pl.ds(pl.multiple_of(row, SUB), SUB), :])
                for p, v in enumerate(group_transpose(tiles_x, z.ps)):
                    parts[p * (z.z // SUB) + h] = v
            columns.append(jnp.concatenate(parts, axis=0))
        block_rows = jnp.concatenate(columns, axis=1)
        rows = jnp.dot(gather, split3(block_rows), preferred_element_type=F32)
        for n in range(2):
            for i in range(z.by):
                g, k = divmod(i, z.most)
                start = g * SUB * stride + (jj + n) * lane_tile + c * z.most + k
                back[pl.ds(start, SUB, stride=stride), :] = rows[
                    i * SUB : (i + 1) * SUB, n * LANES : (n + 1) * LANES
                ]


def face(z, rate, upwind, t, d, x):
    g = rate[pl.ds(pl.multiple_of(d * z.cells + x * z.z, z.z), z.z), :]
    u = upwind[pl.ds(pl.multiple_of((t * 3 + d) * z.cells + x * z.z, z.z), z.z), :].astype(F32)
    if d == 0:
        keep = (x < z.x - 1) | (lax.axis_index("wide") < z.wide - 1)
    elif d == 1:
        keep = (iota((z.z, LANES), 0) < z.z - 1) | (lax.axis_index("depth") < z.depth - 1)
    else:
        keep = iota((z.z, LANES), 1) < LANES - 1
    g = jnp.where(keep, g, 0.0)
    out = g * u
    return out, g - out


def stream(z, src, dst, sem):
    rows = [pl.ds(n * z.cells // PARTS, z.cells // PARTS) for n in range(PARTS)]
    return [
        pltpu.make_async_copy(src.at[:, r, :], dst.at[:, r, :], sem.at[n])
        for n, r in enumerate(rows)
    ]


def plane(z, ref, c, x):
    if len(ref.shape) == 3:
        return ref[c, pl.ds(pl.multiple_of(x * z.z, z.z), z.z), :]
    return ref[pl.ds(pl.multiple_of(c * z.cells + x * z.z, z.z), z.z), :]


def matrix_messages(z, mobile, rate, upwind, t, wide_a, wide_b, deep_a, deep_b):
    nc = z.nc
    even_w = lax.rem(lax.axis_index("wide"), 2) == 0
    even_d = lax.rem(lax.axis_index("depth"), 2) == 0
    out, into = face(z, rate, upwind, t, 0, z.x - 1)
    for c in range(nc):
        ahead = plane(z, mobile, c, z.x - 1) * out
        behind = plane(z, mobile, c, 0)
        rows = pl.ds(c * z.z, z.z)
        wide_a[rows, :] = jnp.where(even_w, ahead, behind)
        wide_b[rows, :] = jnp.where(even_w, behind, ahead)
    rows = pl.ds(nc * z.z, z.z)
    wide_a[rows, :] = into
    wide_b[rows, :] = into
    edge = lax.axis_index("depth") < z.depth - 1

    def last_rows(ref, base, h):
        return ref[pl.ds(base + h * SUB * z.z + z.z - 1, SUB, stride=z.z), :]

    for h in range(z.x // SUB):
        g = jnp.where(edge, last_rows(rate, z.cells, h), 0.0)
        u = last_rows(upwind, (t * 3 + 1) * z.cells, h).astype(F32)
        out = g * u
        for c in range(nc):
            ahead = last_rows(mobile, c * z.cells, h) * out
            behind = mobile[pl.ds(c * z.cells + h * SUB * z.z, SUB, stride=z.z), :]
            rows = pl.ds(c * z.x + h * SUB, SUB)
            deep_a[rows, :] = jnp.where(even_d, ahead, behind)
            deep_b[rows, :] = jnp.where(even_d, behind, ahead)
        rows = pl.ds(nc * z.x + h * SUB, SUB)
        deep_a[rows, :] = g - out
        deep_b[rows, :] = g - out


def flash_field(z, moles, mobile, k_ref, low=0, high=None, hop=1):
    excess, first = k_scalars(k_ref, z.nc)
    step = FLASH_PLANES
    high = z.x // step if high is None else high

    def block(n, carry):
        def rows(c):
            return pl.ds(pl.multiple_of(c * z.cells + n * step * z.z, z.z), step * z.z)

        def store(c, v):
            mobile[rows(c), :] = v

        flash_block(lambda c: moles[rows(c), :], store, excess, first, z.nc)
        return carry

    lax.fori_loop(0, -(-(high - low) // hop), lambda i, a: block(low + i * hop, a), 0)


def first_matrix_kernel(
    z, k_ref, slot_ref, block_ref, moles, rate, upwind, mobile, wide_a, wide_b, deep_a, deep_b,
    tab, gather,
):
    tables(z, slot_ref, block_ref, tab, gather)
    flash_field(z, moles, mobile, k_ref)
    matrix_messages(z, mobile, rate, upwind, 0, wide_a, wide_b, deep_a, deep_b)


def frac_messages(z, mobile, coef, tab, t, frac_a, frac_b):
    even = lax.rem(lax.axis_index("wide"), 2) == 0
    last = lax.axis_index("wide") == z.wide - 1
    here = (tab[pl.ds(2 * SUB, 2 * SUB), :] >= 0).astype(F32)
    out = plane(z, coef, 1, z.x - 1) * plane(z, coef, 4 + 3 * t, z.x - 1)
    into = plane(z, coef, 1, z.x - 1) - out
    out = jnp.where(last, 0.0, out)
    into = jnp.where(last, 0.0, into)
    for c in range(z.nc):
        ahead = plane(z, mobile, c, z.x - 1) * out
        behind = plane(z, mobile, c, 0) * here
        rows = pl.ds(c * z.z, z.z)
        frac_a[rows, :] = jnp.where(even, ahead, behind)
        frac_b[rows, :] = jnp.where(even, behind, ahead)
    rows = pl.ds(z.nc * z.z, z.z)
    frac_a[rows, :] = into
    frac_b[rows, :] = into


def unpack_rows(z, tab, recv_hbm, recv, sem, js, moles, coef):
    lane_tile = z.tiles_out * SUB
    stride = len(js) * lane_tile
    reads = [
        pltpu.make_async_copy(
            recv_hbm.at[pl.ds((w * z.jt + j) * lane_tile, lane_tile), :],
            recv.at[pl.ds((w * len(js) + n) * lane_tile, lane_tile), :],
            sem.at[w * len(js) + n],
        )
        for w in range(z.wide)
        for n, j in enumerate(js)
    ]
    for read in reads:
        read.start()
    from_sub = [tab[pl.ds(h * SUB, SUB), :] for h in range(2)]
    shift = [tab[pl.ds(2 * SUB + h * SUB, SUB), :] for h in range(2)]
    for read in reads:
        read.wait()

    def channel(c, dst, first_row, default):
        for t, j in enumerate(js):
            a = [
                recv[
                    pl.ds(
                        g * SUB * stride + t * lane_tile + c * z.most + k, SUB, stride=stride
                    ),
                    :,
                ]
                for g in range(z.groups)
                for k in range(z.most)
            ]
            for xi, v in enumerate(group_transpose(a, z.ps)):
                rolled = [lane_roll(v, n * z.ps) for n in range(z.by)]
                for h in range(2):
                    got = jnp.full((SUB, LANES), default, F32)
                    for n in range(z.by):
                        got = jnp.where(shift[h] == n, sub_gather(rolled[n], from_sub[h]), got)
                    row = first_row + (z.xt * j + xi) * z.z + h * SUB
                    dst[pl.ds(pl.multiple_of(row, SUB), SUB), :] = got

    def amount(c, carry):
        channel(c, moles, c * z.cells, 1.0)
        return carry

    def weight(c, carry):
        channel(z.nc + c, coef, c * z.cells, jnp.where(c == 0, 1.0, 0.0))
        return carry

    unroll = max(1, 8 // len(js))
    lax.fori_loop(0, z.nc, amount, 0, unroll=unroll)
    lax.fori_loop(0, z.coefs, weight, 0, unroll=2)


def frac_edge_kernel(z, k_ref, tab, recv_hbm, moles, mobile, coef, frac_a, frac_b, recv, sem):
    unpack_rows(z, tab, recv_hbm, recv, sem, (0, z.jt - 1), moles, coef)
    last = z.x // FLASH_PLANES
    flash_field(z, moles, mobile, k_ref, 0, last, last - 1)
    frac_messages(z, mobile, coef, tab, 0, frac_a, frac_b)


def frac_inner_kernel(
    z, k_ref, tab, recv_hbm, moles_in, mobile_in, coef_in, moles, mobile, coef, recv, sem
):
    unpack_rows(z, tab, recv_hbm, recv, sem, tuple(range(1, z.jt - 1)), moles, coef)
    flash_field(z, moles, mobile, k_ref, 1, z.x // FLASH_PLANES - 1)


def each_plane(z, at, streams=()):
    def arrived(x):
        for n in range(1, PARTS):

            @pl.when(x == n * z.x // PARTS - 1)
            def _(n=n):
                for copies in streams:
                    copies[n].wait()

    def middle(x, carry):
        if streams:
            arrived(x)
        at(x, False, False)
        return carry

    for copies in streams:
        copies[0].wait()
    at(0, True, False)
    lax.fori_loop(1, z.x - 1, middle, 0)
    at(z.x - 1, False, True)


def matrix_update(z, t, moles, mobile, rate, upwind, pore, halos, new, mobile_f=None, coef=None,
                  streams=()):
    *wide, deep_a, deep_b = halos
    wide_a, wide_b = wide or (None, None)
    nc = z.nc
    even_w = lax.rem(lax.axis_index("wide"), 2) == 0
    even_d = lax.rem(lax.axis_index("depth"), 2) == 0
    sub = iota((z.z, LANES), 0)

    def side(a, b, first, row, count):
        rows = pl.ds(row, count)
        even = even_w if a is wide_a else even_d
        if first:
            return jnp.where(even, b[rows, :], a[rows, :])
        return jnp.where(even, a[rows, :], b[rows, :])

    def at(x, low, high):
        inv = 1.0 / plane(z, pore, 0, x)
        ox, ix = face(z, rate, upwind, t, 0, x)
        oz, iz = face(z, rate, upwind, t, 1, x)
        oy, iy = face(z, rate, upwind, t, 2, x)
        if low:
            pox, pix = (1.0, side(wide_a, wide_b, True, nc * z.z, z.z)) if wide else (0.0, 0.0)
        else:
            pox, pix = face(z, rate, upwind, t, 0, x - 1)
        wz = jnp.broadcast_to(side(deep_a, deep_b, True, nc * z.x + x, 1), (z.z, LANES))
        poz = jnp.where(sub == 0, 1.0, pltpu.roll(oz, 1, 0))
        piz = jnp.where(sub == 0, wz, pltpu.roll(iz, 1, 0))
        poy, piy = lane_roll(oy, 1), lane_roll(iy, 1)
        own = ox + pix + oz + piz + oy + piy
        if coef is not None:
            w2, w5 = exchange_weights(z, t, coef, x)
            own = own + w2
            w5 = w5 * inv
        own = own * inv
        ax, bx = ix * inv, pox * inv
        az, bz = iz * inv, poz * inv
        ay, by = iy * inv, poy * inv
        for c in range(nc):
            g = plane(z, mobile, c, x)
            v = plane(z, moles, c, x) - own * g
            if not low:
                v = v + bx * plane(z, mobile, c, x - 1)
            elif wide:
                v = v + bx * side(wide_a, wide_b, True, c * z.z, z.z)
            if not high:
                v = v + ax * plane(z, mobile, c, x + 1)
            elif wide:
                v = v + ax * side(wide_a, wide_b, False, c * z.z, z.z)
            hz0 = jnp.broadcast_to(side(deep_a, deep_b, True, c * z.x + x, 1), (z.z, LANES))
            hz1 = jnp.broadcast_to(side(deep_a, deep_b, False, c * z.x + x, 1), (z.z, LANES))
            zb = jnp.where(sub == 0, hz0, pltpu.roll(g, 1, 0))
            za = jnp.where(sub == z.z - 1, hz1, pltpu.roll(g, z.z - 1, 0))
            v = v + (az * za + bz * zb)
            v = v + (ay * lane_roll(g, -1) + by * lane_roll(g, 1))
            if coef is not None:
                v = v + w5 * plane(z, mobile_f, c, x)
            new[pl.ds(pl.multiple_of(c * z.cells + x * z.z, z.z), z.z), :] = v

    each_plane(z, at, streams)


def exchange_weights(z, t, coef, x):
    g = plane(z, coef, 3, x)
    into = g * plane(z, coef, 4 + 3 * t + 2, x)
    return into, g - into


def matrix_early_kernel(
    z, t, moles, mobile, rate, upwind, pore, hc, hd, new, stage, sem
):
    matrix_update(z, t, moles, mobile, rate, upwind, pore, (hc, hd), stage)
    writes = [
        pltpu.make_async_copy(stage.at[rows, :], new.at[rows, :], sem.at[n])
        for n, rows in enumerate(
            pl.ds(n * z.nc * z.cells // PARTS, z.nc * z.cells // PARTS) for n in range(PARTS)
        )
    ]
    for copy in writes:
        copy.start()
    for copy in writes:
        copy.wait()


def matrix_kernel(
    z, t, k_ref, early, mobile_hbm, mobile_f, coef, rate, upwind, pore, ha, hb, new,
    mobile_new, wide_a, wide_b, deep_a, deep_b, moles, mobile, sem,
):
    streams = (stream(z, early, moles, sem.at[0]), stream(z, mobile_hbm, mobile, sem.at[1]))
    for n in range(PARTS):
        for copies in streams:
            copies[n].start()

    even = lax.rem(lax.axis_index("wide"), 2) == 0

    def side(first, row):
        rows = pl.ds(row, z.z)
        if first:
            return jnp.where(even, hb[rows, :], ha[rows, :])
        return jnp.where(even, ha[rows, :], hb[rows, :])

    def at(x, low, high):
        inv = 1.0 / plane(z, pore, 0, x)
        w2, w5 = exchange_weights(z, t, coef, x)
        if low:
            w2 = w2 + side(True, z.nc * z.z)
        w2, w5 = w2 * inv, w5 * inv
        ax = face(z, rate, upwind, t, 0, x)[1] * inv if high else None
        for c in range(z.nc):
            v = plane(z, moles, c, x) - w2 * plane(z, mobile, c, x)
            v = v + w5 * plane(z, mobile_f, c, x)
            if low:
                v = v + inv * side(True, c * z.z)
            if high:
                v = v + ax * side(False, c * z.z)
            new[pl.ds(pl.multiple_of(c * z.cells + x * z.z, z.z), z.z), :] = v

    each_plane(z, at, streams)
    flash_field(z, new, mobile_new, k_ref)
    matrix_messages(z, mobile_new, rate, upwind, t + 1, wide_a, wide_b, deep_a, deep_b)


def last_matrix_kernel(
    z, t, moles_hbm, mobile_hbm, mobile_f_hbm, coef, rate, upwind, pore, ha, hb, hc, hd, new,
    moles, mobile, mobile_f, sem,
):
    streams = tuple(
        stream(z, src, dst, sem.at[n])
        for n, (src, dst) in enumerate(
            ((moles_hbm, moles), (mobile_hbm, mobile), (mobile_f_hbm, mobile_f))
        )
    )
    for n in range(PARTS):
        for copies in streams:
            copies[n].start()
    matrix_update(
        z, t, moles, mobile, rate, upwind, pore, (ha, hb, hc, hd), new, mobile_f, coef, streams
    )


def frac_update(z, t, tab, moles, mobile, mobile_m, coef, frac_a, frac_b, new, streams=()):
    nc = z.nc
    even = lax.rem(lax.axis_index("wide"), 2) == 0
    here = (tab[pl.ds(2 * SUB, 2 * SUB), :] >= 0).astype(F32)
    beyond = tab[pl.ds(4 * SUB, 2 * SUB), :].astype(F32)
    lane = iota((z.z, LANES), 1)
    next_y = jnp.where(lane == LANES - 1, 0.0, lane_roll(here, -1))

    def side(first, row):
        rows = pl.ds(row, z.z)
        if first:
            return jnp.where(even, frac_b[rows, :], frac_a[rows, :])
        return jnp.where(even, frac_a[rows, :], frac_b[rows, :])

    def split(x, d, mask):
        g = plane(z, coef, 1 + d, x) * mask
        out = g * plane(z, coef, 4 + 3 * t + d, x)
        return out, g - out

    def at(x, low, high):
        inv = 1.0 / plane(z, coef, 0, x)
        ox, ix = split(x, 0, beyond if high else here)
        if low:
            pox, pix = here, side(True, nc * z.z) * here
        else:
            pox, pix = split(x - 1, 0, here)
        oy, iy = split(x, 1, next_y)
        poy, piy = lane_roll(oy, 1), lane_roll(iy, 1)
        w2, w5 = split(x, 2, 1.0)
        own = (ox + pix + oy + piy + w5) * inv
        ax, bx = ix * inv, pox * inv
        ay, by = iy * inv, poy * inv
        w2 = w2 * inv
        for c in range(nc):
            g = plane(z, mobile, c, x)
            before = side(True, c * z.z) if low else plane(z, mobile, c, x - 1)
            after = side(False, c * z.z) if high else plane(z, mobile, c, x + 1)
            v = plane(z, moles, c, x) - own * g + (ax * after + bx * before)
            v = v + (ay * lane_roll(g, -1) + by * lane_roll(g, 1))
            v = v + w2 * plane(z, mobile_m, c, x)
            new[pl.ds(pl.multiple_of(c * z.cells + x * z.z, z.z), z.z), :] = v

    each_plane(z, at, streams)


def frac_kernel(
    z, t, k_ref, tab, moles, mobile, mobile_hbm, coef, fa, fb, new, mobile_new, frac_a, frac_b,
    mobile_m, sem,
):
    copies = stream(z, mobile_hbm, mobile_m, sem)
    for copy in copies:
        copy.start()
    frac_update(z, t, tab, moles, mobile, mobile_m, coef, fa, fb, new, (copies,))
    flash_field(z, new, mobile_new, k_ref)
    frac_messages(z, mobile_new, coef, tab, t + 1, frac_a, frac_b)


def last_frac_kernel(
    z, t, tab, gather, moles, mobile, mobile_m, coef, fa, fb, back, new, stage, sem
):
    frac_update(z, t, tab, moles, mobile, mobile_m, coef, fa, fb, new)
    maps = gather[:, : 3 * z.blocks].astype(jnp.bfloat16)

    def channel(c, carry):
        field_to_rows(z, new, c * z.cells, maps, stage, c)
        return carry

    lax.fori_loop(0, z.nc, channel, 0, unroll=4)
    copy = pltpu.make_async_copy(stage, back, sem)
    copy.start()
    copy.wait()


def swap(value, axis, ahead, ends=True):
    count = lax.axis_size(axis)
    if ahead:
        pairs = [(i, i ^ 1) for i in range(count)]
    else:
        pairs = [(i, i - 1 if i % 2 == 0 else i + 1) for i in range(count)]
        pairs = [(i, n % count) for i, n in pairs if ends or 0 <= n < count]
    return lax.ppermute(value, axis, pairs)


def call(
    kernel, in_specs, out_shape, args, scratch=(), mib=12, out_specs=None, kept=(),
    aliases=None,
):
    body = kernel
    if kept:
        kept = in_vmem(*kept)
        at, count = len(args), len(kept)
        body = lambda *refs: kernel(*refs[:at], *refs[at + count :])
        args = (*args, *kept)
        in_specs = in_specs + [VMEM] * count
    return pl.pallas_call(
        body,
        out_shape=out_shape,
        in_specs=in_specs,
        out_specs=out_specs or (
            (VMEM,) * len(out_shape) if isinstance(out_shape, tuple) else VMEM
        ),
        scratch_shapes=scratch,
        input_output_aliases=aliases or {},
        compiler_params=pltpu.CompilerParams(vmem_limit_bytes=mib << 20),
        cost_estimate=pl.CostEstimate(
            flops=10**8, bytes_accessed=sum(a.size * 4 for a in args), transcendentals=0
        ),
    )(*args)


def shape(rows, lanes=LANES, space=pltpu.VMEM):
    return space((rows, lanes), F32)


def in_vmem(*values):
    return tuple(pltpu.with_memory_space_constraint(v, pltpu.VMEM) for v in values)


def in_hbm(v):
    return pltpu.with_memory_space_constraint(v, pltpu.HBM)


def local(
    matrix_moles,
    pore_matrix,
    matrix_rate,
    matrix_upwind,
    frac_moles,
    pore_frac,
    frac_rate,
    frac_upwind,
    ff_open,
    kvalues,
    slot_patch,
    patch_block,
):
    z = Sizes(matrix_moles, frac_moles)
    bind = lambda f, *a: functools.partial(f, z, *a)
    blocks, slot_patch, kvalues = in_hbm(patch_block.T), in_hbm(slot_patch), in_hbm(kvalues)
    moles = matrix_moles.reshape(-1, z.y)
    pore = pore_matrix.reshape(-1, z.y)
    rate = matrix_rate.reshape(-1, z.y)
    upwind = matrix_upwind.reshape(-1, z.y)
    field = shape(z.nc * z.cells)
    msg_w, msg_d = shape((z.nc + 1) * z.z), shape((z.nc + 1) * z.x)
    rows_out = z.wide * z.jt * z.tiles_out * SUB
    rows_back = z.wide * z.jt * z.tiles_back * SUB
    src_rows = z.tiles_out * z.cpt * z.slots
    hbm_field = shape(z.nc * z.cells, space=pltpu.HBM)
    stacked = lambda v: in_hbm(v.reshape(z.nc, z.cells, LANES))
    stream_buf = pltpu.VMEM((z.nc, z.cells, LANES), F32)

    send = call(
        bind(pack_kernel), [SMEM] * 3 + [HBM] * 4,
        shape(rows_out, space=pltpu.HBM),
        (
            slot_patch,
            blocks,
            in_hbm(ff_open.T),
            in_hbm(frac_moles.reshape(-1, z.pc)),
            in_hbm(pore_frac),
            in_hbm(frac_rate.reshape(-1, z.pc)),
            in_hbm(frac_upwind.reshape(-1, z.pc)),
        ),
        scratch=[
            pltpu.VMEM((src_rows, z.pc), F32),
            pltpu.VMEM((3 * SUBSTEPS * z.slots, z.pc), I32),
            pltpu.VMEM((rows_out, LANES), F32),
            pltpu.SemaphoreType.DMA((4,)),
            pltpu.SemaphoreType.DMA((z.cols,)),
        ],
        out_specs=HBM,
    )

    def trade(v):
        return lax.all_to_all(v, "wide", split_axis=0, concat_axis=0, tiled=True)

    def exchange(a, b, axis):
        return swap(a, axis, True), swap(b, axis, False, axis == "wide")

    recv = trade(send)
    mobile_m, wa, wb, da, db, tab, gather = call(
        bind(first_matrix_kernel), [SMEM] * 3 + [VMEM] * 3,
        (
            field, msg_w, msg_w, msg_d, msg_d, pltpu.VMEM((6 * SUB, LANES), I32),
            shape(z.places, -(-3 * z.blocks // LANES) * LANES),
        ),
        (kvalues, slot_patch, blocks, *in_vmem(moles, rate, upwind)),
    )
    wide_halos = exchange(wa, wb, "wide")
    deep_halos = exchange(da, db, "depth")
    early = call(
        bind(matrix_early_kernel, 0), [VMEM] * 7, hbm_field,
        in_vmem(moles, mobile_m, rate, upwind, pore, *deep_halos),
        scratch=[
            pltpu.VMEM((z.nc * z.cells, LANES), F32), pltpu.SemaphoreType.DMA((PARTS,))
        ],
        out_specs=HBM,
    )
    coef_field = shape(z.coefs * z.cells)
    tiles = z.wide * z.tiles_out * SUB
    moles_f, mobile_f, coef, fa, fb = call(
        bind(frac_edge_kernel), [SMEM, VMEM, HBM],
        (field, field, coef_field, msg_w, msg_w),
        (kvalues, *in_vmem(tab), in_hbm(recv)),
        scratch=[pltpu.VMEM((2 * tiles, LANES), F32), pltpu.SemaphoreType.DMA((2 * z.wide,))],
    )
    fa, fb = exchange(fa, fb, "wide")
    inner = z.jt - 2
    moles_f, mobile_f, coef = call(
        bind(frac_inner_kernel), [SMEM, VMEM, HBM] + [VMEM] * 3,
        (field, field, coef_field),
        (kvalues, *in_vmem(tab), in_hbm(recv), *in_vmem(moles_f, mobile_f, coef)),
        scratch=[
            pltpu.VMEM((inner * tiles, LANES), F32),
            pltpu.SemaphoreType.DMA((inner * z.wide,)),
        ],
        aliases={3: 0, 4: 1, 5: 2},
    )
    new_f, new_mobile_f, fa, fb = call(
        bind(frac_kernel, 0), [SMEM] + [VMEM] * 3 + [HBM] + [VMEM] * 3,
        (field, field, msg_w, msg_w),
        (
            kvalues, *in_vmem(tab, moles_f, mobile_f), stacked(mobile_m),
            *in_vmem(coef, fa, fb),
        ),
        scratch=[stream_buf, pltpu.SemaphoreType.DMA((PARTS,))],
        kept=(rate, upwind, pore),
    )
    fa, fb = exchange(fa, fb, "wide")
    moles, mobile_m, wa, wb, da, db = call(
        bind(matrix_kernel, 0), [SMEM] + [HBM] * 2 + [VMEM] * 7,
        (field, field, msg_w, msg_w, msg_d, msg_d),
        (
            kvalues, stacked(early), stacked(mobile_m),
            *in_vmem(mobile_f, coef, rate, upwind, pore, *wide_halos),
        ),
        scratch=[stream_buf, stream_buf, pltpu.SemaphoreType.DMA((2, PARTS))],
        kept=(new_f, new_mobile_f, tab),
    )
    wide_halos = exchange(wa, wb, "wide")
    deep_halos = exchange(da, db, "depth")
    t = SUBSTEPS - 1
    back = call(
        bind(last_frac_kernel, t), [VMEM] * 8,
        shape(rows_back, space=pltpu.HBM),
        in_vmem(tab, gather, new_f, new_mobile_f, mobile_m, coef, fa, fb),
        scratch=[
            pltpu.VMEM((z.nc * z.cells, LANES), F32),
            pltpu.VMEM((rows_back, LANES), F32),
            pltpu.SemaphoreType.DMA,
        ],
        out_specs=HBM,
    )
    returned = trade(back)
    moles = call(
        bind(last_matrix_kernel, t), [HBM] * 3 + [VMEM] * 8,
        jax.ShapeDtypeStruct((z.nc * z.cells, LANES), F32),
        (
            stacked(moles), stacked(mobile_m), stacked(new_mobile_f),
            *in_vmem(coef, rate, upwind, pore, *wide_halos, *deep_halos),
        ),
        scratch=[stream_buf] * 3 + [pltpu.SemaphoreType.DMA((3, PARTS))],
    )
    frac = call(
        bind(spread_kernel), [SMEM] * 2 + [HBM],
        jax.ShapeDtypeStruct((z.nc * z.slots, z.pc), F32),
        (slot_patch, blocks, in_hbm(returned)),
        scratch=[pltpu.VMEM((rows_back, LANES), F32), pltpu.SemaphoreType.DMA],
    )
    return moles.reshape(matrix_moles.shape), frac.reshape(frac_moles.shape)


def solution(mesh):
    placed = (
        P(None, "wide", "depth", None),
        P("wide", "depth", None),
        P(None, "wide", "depth", None),
        P(None, None, "wide", "depth", None),
        P(None, ("wide", "depth"), None),
        P(("wide", "depth"), None),
        P(None, ("wide", "depth"), None),
        P(None, None, ("wide", "depth"), None),
        P(("wide", "depth"), None),
        P(),
        P(),
        P(),
    )
    return jax.shard_map(
        local,
        mesh=mesh,
        in_specs=placed,
        out_specs=(P(None, "wide", "depth", None), P(None, ("wide", "depth"), None)),
        check_vma=False,
    )
```

time: 117 us -> 106 us (0.906); the launches traced: 117 us -> 104 us
  local copies, waits for them, and re-layouts: 22.5 us -> 2.94 us
  Pallas kernels: 42.9 us -> 51.8 us
    unnamed x74 -> x20, local copies, waits for them, and re-layouts: 22.3 us -> 2.94 us
    pallas_call x8 -> x10, Pallas kernels: 42.9 us -> 51.8 us  [call(): pl.pallas_call(body, out_shape=out_shape, in_specs=in_specs, out_specs=ou...]
    ppermute x12, waiting for transfers between devices: 10.9 us -> 9.72 us  [swap(): return lax.ppermute(value, axis, pairs)]
  transfers between devices with their start and end apart: 14 -> 14, of which waited for: 2 -> 2; matrix products, arithmetic and copies ran while one was open for 0% -> 0% of each run, Pallas kernels for 18% -> 33%
where the time goes in v1:
time: 106 us; the launch traced here: 104 us
  Pallas kernels  51.8 us (49%)
  starting transfers between devices  24.3 us (23%)
  waiting for transfers between devices  24.3 us (23%)
  local copies, waits for them, and re-layouts  2.94 us (3%)
    pallas_call x10, Pallas kernels, call(): pl.pallas_call(body, out_shape=out_shape, in_specs=in_specs, out_specs=ou...  51.8 us
    ppermute x12, starting transfers between devices, swap(): return lax.ppermute(value, axis, pairs)  14.7 us
    all_to_all x2, waiting for transfers between devices, trade(): return lax.all_to_all(v, 'wide', split_axis=0, concat_axis=0, tiled=True)  14.6 us
    ppermute x12, waiting for transfers between devices, swap(): return lax.ppermute(value, axis, pairs)  9.72 us
    all_to_all x2, starting transfers between devices, trade(): return lax.all_to_all(v, 'wide', split_axis=0, concat_axis=0, tiled=True)  9.61 us
    unnamed x20, local copies, waits for them, and re-layouts  2.94 us
  transfers between devices with their start and end apart: 14, of which 2 were waited for; matrix products, arithmetic and copies ran while one was open for 0% of the time, Pallas kernels for 33%

profile of v1, /device:TPU:0, one launch (start us, length us, event | category | flops | bytes accessed | tf_op | source)
XLA Modules:
  0.0 104.3 jit_solution(1978721359460499927)
XLA Ops:
  0.6 3.3 %shard_map.133 = f32[3328,128]{1,0:T(8,128)} custom-call(s32[256]{0:T(256)} %slot_ref.5, s32[3,256]{1,0:T(4,128)} %bitcast.49, s32[2,8]{1,0:T(2,128)} %bitcast.52, f32[128,1024]{1,0:T(8,128)} %bitcast.45, f32[8,1024]{1,0:T(8,128)} %pore.1, f32[24,1024]{1,0:T(8,128)} %bitcast.48, s32[48,1024]{1,0:T(8,128)} %bitcast.47), custom_call_target="tpu_custom_call" | custom-call | flops 100000000 | bytes 856128 | tf_op jit(solution)/shard_map/pallas_call | solution.py:765
  4.0 0.0 copy-start
  4.0 0.0 copy-start.4
  4.0 5.3 %all-to-all-start = ((f32[8,416,128]{2,1,0:T(8,128)}), f32[8,416,128]{2,1,0:T(8,128)}, u32[]{:S(2)}, u32[]{:S(2)}) async-start(f32[8,416,128]{2,1,0:T(8,128)} %bitcast.42), calls=%async_computation | async-start | bytes 3407872 | tf_op jit(solution)/shard_map/all_to_all | solution.py:846
  9.3 0.0 copy-done
  9.3 0.0 copy-done.4
  9.3 0.0 copy-start.6
  9.3 1.6 %copy-done.6 = f32[16,16,16,128]{3,2,1,0:T(8,128)S(1)} copy-done((f32[16,16,16,128]{3,2,1,0:T(8,128)S(1)}, f32[16,16,16,128]{3,2,1,0:T(8,128)}, u32[]{:S(2)}) %copy-start.6) | copy-done | bytes 2097176
  10.9 5.0 %shard_map.131 = (f32[4096,128]{1,0:T(8,128)S(1)}, f32[272,128]{1,0:T(8,128)S(1)}, f32[272,128]{1,0:T(8,128)S(1)}, f32[272,128]{1,0:T(8,128)S(1)}, f32[272,128]{...) custom-call(f32[16]{0:T(128)} %refs_0_.3, s32[256]{0:T(256)} %slot_ref.5, s32[3,256]{1,0:T(4,128)} %bitcast.50, ...), custom_call_target="tpu_custom_call" | custom-call | flops 100000000 | bytes 3280960 | tf_op jit(solution)/shard_map/pallas_call | solution.py:765
  15.9 0.0 copy-start.2
  16.0 1.3 %copy-done.2 = f32[4096,128]{1,0:T(8,128)} copy-done((f32[4096,128]{1,0:T(8,128)}, f32[4096,128]{1,0:T(8,128)S(1)}, u32[]{:S(2)}) %copy-start.2) | copy-done | bytes 2097176
  17.3 14.6 %all-to-all-done = f32[8,416,128]{2,1,0:T(8,128)} async-done(((f32[8,416,128]{2,1,0:T(8,128)}), f32[8,416,128]{2,1,0:T(8,128)}, u32[]{:S(2)}, u32[]{:S(2)}) %all-to-all-start) | async-done | bytes 1703968 | tf_op jit(solution)/shard_map/all_to_all | solution.py:846
  31.8 5.2 %shard_map.134 = (f32[4096,128]{1,0:T(8,128)S(1)}, f32[4096,128]{1,0:T(8,128)S(1)}, f32[2560,128]{1,0:T(8,128)S(1)}, f32[272,128]{1,0:T(8,128)S(1)}, f32[272,128]{1,0:T(8,128)S(1)}) custom-call(f32[16]{0:T(128)} %refs_0_.3, s32[48,128]{1,0:T(8,128)S(1)} %get-tuple-element.30.tab.refs_1_.refs_12_, f32[3328,128]{1,0:T(8,128)} %bitcast.12.recv_hbm), custom_call_target="tpu_custom_call" | custom-call | flops 100000000 | bytes 1728576 | tf_op jit(solution)/shard_map/pallas_call | solution.py:765
  37.0 0.1 collective-permute-start.4
  37.1 0.7 collective-permute-start.5
  37.8 2.1 %collective-permute-start = (f32[272,128]{1,0:T(8,128)S(1)}, f32[272,128]{1,0:T(8,128)S(1)}, u32[]{:S(2)}, u32[]{:S(2)}) collective-permute-start(f32[272,128]{1,0:T(8,128)S(1)} %get-tuple-element.28), channel_id=1, source_target_pairs={{0,1},{1,0},{2,3},{3,2},{4,5},{5,4},{6,7},{7,6},{8,9},{9,8},{10,11... | collective-permute-start | bytes 417800 | tf_op jit(solution)/shard_map/ppermute | solution.py:751
  39.9 0.7 collective-permute-start.1
  40.6 0.1 collective-permute-start.2
  40.6 0.0 copy-start.8
  40.6 6.7 %shard_map.135 = (f32[4096,128]{1,0:T(8,128)S(1)}, f32[4096,128]{1,0:T(8,128)S(1)}, f32[2560,128]{1,0:T(8,128)S(1)}) custom-call(f32[16]{0:T(128)} %refs_0_.3, s32[48,128]{1,0:T(8,128)S(1)} %get-tuple-element.30.tab.refs_1_.refs_12_, f32[3328,128]{1,0:T(8,128)} %bitcast.12.recv_hbm, ...), custom_call_target="tpu_custom_call", output_to_operand_aliasing={{0}: (3, {}), {1}: (4, {}), {2}: (5, {})} | custom-call | flops 100000000 | bytes 7233600 | tf_op jit(solution)/shard_map/pallas_call | solution.py:765
  47.3 0.0 collective-permute-done.4.refs_6_
  47.4 1.8 %collective-permute-start.3 = (f32[272,128]{1,0:T(8,128)S(1)}, f32[272,128]{1,0:T(8,128)S(1)}, u32[]{:S(2)}, u32[]{:S(2)}) collective-permute-start(f32[272,128]{1,0:T(8,128)S(1)} %get-tuple-element.37), channel_id=1, source_target_pairs={{0,28},{4,8},{8,4},{12,16},{16,12},{20,24},{24,20},{28,0},{1,29},{... | collective-permute-start | bytes 417800 | tf_op jit(solution)/shard_map/ppermute | solution.py:751
  49.2 0.0 collective-permute-done.5.refs_7_
  49.2 7.5 %shard_map.136 = (f32[4096,128]{1,0:T(8,128)S(1)}, f32[4096,128]{1,0:T(8,128)S(1)}, f32[272,128]{1,0:T(8,128)S(1)}, f32[272,128]{1,0:T(8,128)S(1)}) custom-call(f32[16]{0:T(128)} %refs_0_.3, s32[48,128]{1,0:T(8,128)S(1)} %get-tuple-element.30.tab.refs_1_.refs_12_, f32[4096,128]{1,0:T(8,128)S(1)} %get-tuple-element.38.refs_2_, ...), custom_call_target="tpu_custom_call" | custom-call | flops 100000000 | bytes 9216064 | tf_op jit(solution)/shard_map/pallas_call | solution.py:765
  56.6 0.1 collective-permute-start.10
  56.7 0.0 collective-permute-done.hc
  56.7 1.3 %collective-permute-start.11 = (f32[272,128]{1,0:T(8,128)S(1)}, f32[272,128]{1,0:T(8,128)S(1)}, u32[]{:S(2)}, u32[]{:S(2)}) collective-permute-start(f32[272,128]{1,0:T(8,128)S(1)} %get-tuple-element.51), channel_id=1, source_target_pairs={{0,28},{4,8},{8,4},{12,16},{16,12},{20,24},{24,20},{28,0},{1,29},{... | collective-permute-start | bytes 417800 | tf_op jit(solution)/shard_map/ppermute | solution.py:751
  58.0 0.0 collective-permute-done.1.hd
  58.0 3.8 %shard_map.132 = f32[4096,128]{1,0:T(8,128)} custom-call(f32[4096,128]{1,0:T(8,128)S(1)} %bitcast.35, f32[4096,128]{1,0:T(8,128)S(1)} %copy-done.3, f32[768,128]{1,0:T(8,128)S(1)} %bitcast.30, s32[1536,128]{1,0:T(8,128)S(1)} %bitcast.22, f32[256,128]{1,0:T(8,128)S(1)} %bitcast.37, f32[272,128]{1,0:T(8,128)S(1)} %collective-permute-done.hc, ...), custom_call_target="tpu_custom_call" | custom-call | flops 100000000 | bytes 5783552 | tf_op jit(solution)/shard_map/pallas_call | solution.py:765
  61.8 0.0 collective-permute-done.2.refs_8_
  61.9 0.0 collective-permute-done.3.refs_9_
  61.9 5.9 %shard_map.137 = (f32[4096,128]{1,0:T(8,128)S(1)}, f32[4096,128]{1,0:T(8,128)S(1)}, f32[272,128]{1,0:T(8,128)S(1)}, f32[272,128]{1,0:T(8,128)S(1)}, f32[272,128]{1,0:T(8,128)S(1)}, /*index=5*/f32[272,128]{1,0:T(8,128)S(1)}) custom-call(f32[16]{0:T(128)} %refs_0_.3, f32[16,256,128]{2,1,0:T(8,128)} %bitcast.41, f32[16,256,128]{2,1,0:T(8,128)} %bitcast.27, ...), custom_call_target="tpu_custom_call" | custom-call | flops 100000000 | bytes 13410368 | tf_op jit(solution)/shard_map/pallas_call | solution.py:765
  67.8 0.0 collective-permute-done.10.fa
  67.8 0.0 collective-permute-done.11.fb
  67.8 0.0 copy-done.1
  67.8 6.0 %shard_map.139 = f32[2048,128]{1,0:T(8,128)} custom-call(s32[48,128]{1,0:T(8,128)S(1)} %get-tuple-element.30.tab.refs_1_.refs_12_, f32[32,256]{1,0:T(8,128)S(1)} %get-tuple-element.49.gather, f32[4096,128]{1,0:T(8,128)S(1)} %get-tuple-element.41.refs_10_.moles, f32[4096,128]{1,0:T(8,128)S(1)} %get-tuple-element.42.refs_11_.mobile, ...), custom_call_target="tpu_custom_call" | custom-call | flops 100000000 | bytes 7938048 | tf_op jit(solution)/shard_map/pallas_call | solution.py:765
  73.9 4.3 %all-to-all-start.1 = ((f32[8,256,128]{2,1,0:T(8,128)}), f32[8,256,128]{2,1,0:T(8,128)}, u32[]{:S(2)}, u32[]{:S(2)}) async-start(f32[8,256,128]{2,1,0:T(8,128)} %bitcast.43), calls=%async_computation.1 | async-start | bytes 2097152 | tf_op jit(solution)/shard_map/all_to_all | solution.py:846
  78.1 0.4 collective-permute-start.6
  78.5 2.6 %collective-permute-start.7 = (f32[272,128]{1,0:T(8,128)S(1)}, f32[272,128]{1,0:T(8,128)S(1)}, u32[]{:S(2)}, u32[]{:S(2)}) collective-permute-start(f32[272,128]{1,0:T(8,128)S(1)} %get-tuple-element.46), channel_id=1, source_target_pairs={{0,28},{4,8},{8,4},{12,16},{16,12},{20,24},{24,20},{28,0},{1,29},{... | collective-permute-start | bytes 417800 | tf_op jit(solution)/shard_map/ppermute | solution.py:751
  81.1 4.4 %collective-permute-start.8 = (f32[272,128]{1,0:T(8,128)S(1)}, f32[272,128]{1,0:T(8,128)S(1)}, u32[]{:S(2)}, u32[]{:S(2)}) collective-permute-start(f32[272,128]{1,0:T(8,128)S(1)} %get-tuple-element.47), channel_id=1, source_target_pairs={{0,1},{1,0},{2,3},{3,2},{4,5},{5,4},{6,7},{7,6},{8,9},{9,8},{10,11... | collective-permute-start | bytes 417800 | tf_op jit(solution)/shard_map/ppermute | solution.py:751
  85.5 0.7 collective-permute-start.9
  86.1 0.0 collective-permute-done.6.ha
  86.1 9.7 %collective-permute-done.7.hb = f32[272,128]{1,0:T(8,128)S(1)} collective-permute-done((f32[272,128]{1,0:T(8,128)S(1)}, f32[272,128]{1,0:T(8,128)S(1)}, u32[]{:S(2)}, u32[]{:S(2)}) %collective-permute-start.7) | collective-permute-done | bytes 139296 | tf_op jit(solution)/shard_map/ppermute | solution.py:751
  95.8 0.0 collective-permute-done.8.hc
  95.8 0.0 collective-permute-done.9.hd
  95.8 5.5 %shard_map.138 = f32[4096,128]{1,0:T(8,128)} custom-call(f32[16,256,128]{2,1,0:T(8,128)} %bitcast.40, f32[16,256,128]{2,1,0:T(8,128)} %bitcast.33, f32[16,256,128]{2,1,0:T(8,128)} %bitcast.25, f32[2560,128]{1,0:T(8,128)S(1)} %get-tuple-element.35.refs_5_.refs_4_.coef, f32[768,128]{1,0:T(8,128)S(1)} %bitcast.32, s32[1536,128]{1,0:T(8,128)S(1)} %bitcast.24, ...), custom_call_target="tpu_custom_call" | custom-call | flops 100000000 | bytes 9469952 | tf_op jit(solution)/shard_map/pallas_call | solution.py:765
  101.4 0.0 all-to-all-done.1
  101.4 2.9 %shard_map.140 = f32[128,1024]{1,0:T(8,128)} custom-call(s32[256]{0:T(256)} %slot_ref.5, s32[3,256]{1,0:T(4,128)} %bitcast.51, f32[2048,128]{1,0:T(8,128)} %bitcast.18.recv_hbm), custom_call_target="tpu_custom_call" | custom-call | flops 100000000 | bytes 1052672 | tf_op jit(solution)/shard_map/pallas_call | solution.py:765
  (10 shorter events, 0.0 us)
Async XLA Ops:
  4.0 5.4 %copy-start = (s32[2,3,16,16,128]{4,3,2,1,0:T(8,128)S(1)}, s32[2,3,16,16,128]{4,3,2,1,0:T(8,128)}, u32[]{:S(2)}) copy-start(s32[2,3,16,16,128]{4,3,2,1,0:T(8,128)} %param.15) | copy-start | bytes 2359300
  4.0 5.4 %copy-start.4 = (f32[3,16,16,128]{3,2,1,0:T(8,128)S(1)}, f32[3,16,16,128]{3,2,1,0:T(8,128)}, u32[]{:S(2)}) copy-start(f32[3,16,16,128]{3,2,1,0:T(8,128)} %param.14) | copy-start | bytes 1179652
  4.0 27.8 %all-to-all-start = ((f32[8,416,128]{2,1,0:T(8,128)}), f32[8,416,128]{2,1,0:T(8,128)}, u32[]{:S(2)}, u32[]{:S(2)}) async-start(f32[8,416,128]{2,1,0:T(8,128)} %bitcast.42), calls=%async_computation | async-start | bytes 3407872 | tf_op jit(solution)/shard_map/all_to_all | solution.py:846
  9.3 1.6 %copy-start.6 = (f32[16,16,16,128]{3,2,1,0:T(8,128)S(1)}, f32[16,16,16,128]{3,2,1,0:T(8,128)}, u32[]{:S(2)}) copy-start(f32[16,16,16,128]{3,2,1,0:T(8,128)} %param.12) | copy-start | bytes 6291460
  15.9 1.3 %copy-start.2 = (f32[4096,128]{1,0:T(8,128)}, f32[4096,128]{1,0:T(8,128)S(1)}, u32[]{:S(2)}) copy-start(f32[4096,128]{1,0:T(8,128)S(1)} %get-tuple-element.27.mobile) | copy-start | bytes 6291460
  37.0 10.3 %collective-permute-start.4 = (f32[272,128]{1,0:T(8,128)S(1)}, f32[272,128]{1,0:T(8,128)S(1)}, u32[]{:S(2)}, u32[]{:S(2)}) collective-permute-start(f32[272,128]{1,0:T(8,128)S(1)} %get-tuple-element.39), channel_id=1, source_target_pairs={{0,4},{4,0},{8,12},{12,8},{16,20},{20,16},{24,28},{28,24},{1,5},{5... | collective-permute-start | bytes 417800 | tf_op jit(solution)/shard_map/ppermute | solution.py:751
  37.1 12.0 %collective-permute-start.5 = (f32[272,128]{1,0:T(8,128)S(1)}, f32[272,128]{1,0:T(8,128)S(1)}, u32[]{:S(2)}, u32[]{:S(2)}) collective-permute-start(f32[272,128]{1,0:T(8,128)S(1)} %get-tuple-element.40), channel_id=1, source_target_pairs={{0,28},{4,8},{8,4},{12,16},{16,12},{20,24},{24,20},{28,0},{1,29},{... | collective-permute-start | bytes 417800 | tf_op jit(solution)/shard_map/ppermute | solution.py:751
  37.8 18.9 %collective-permute-start = (f32[272,128]{1,0:T(8,128)S(1)}, f32[272,128]{1,0:T(8,128)S(1)}, u32[]{:S(2)}, u32[]{:S(2)}) collective-permute-start(f32[272,128]{1,0:T(8,128)S(1)} %get-tuple-element.28), channel_id=1, source_target_pairs={{0,1},{1,0},{2,3},{3,2},{4,5},{5,4},{6,7},{7,6},{8,9},{9,8},{10,11... | collective-permute-start | bytes 417800 | tf_op jit(solution)/shard_map/ppermute | solution.py:751
  39.9 18.1 %collective-permute-start.1 = (f32[272,128]{1,0:T(8,128)S(1)}, f32[272,128]{1,0:T(8,128)S(1)}, u32[]{:S(2)}, u32[]{:S(2)}) collective-permute-start(f32[272,128]{1,0:T(8,128)S(1)} %get-tuple-element.29), channel_id=1, source_target_pairs={{1,2},{2,1},{5,6},{6,5},{9,10},{10,9},{13,14},{14,13},{17,18},{18,... | collective-permute-start | bytes 417800 | tf_op jit(solution)/shard_map/ppermute | solution.py:751
  40.6 21.3 %collective-permute-start.2 = (f32[272,128]{1,0:T(8,128)S(1)}, f32[272,128]{1,0:T(8,128)S(1)}, u32[]{:S(2)}, u32[]{:S(2)}) collective-permute-start(f32[272,128]{1,0:T(8,128)S(1)} %get-tuple-element.36), channel_id=1, source_target_pairs={{0,4},{4,0},{8,12},{12,8},{16,20},{20,16},{24,28},{28,24},{1,5},{5... | collective-permute-start | bytes 417800 | tf_op jit(solution)/shard_map/ppermute | solution.py:751
  40.6 8.5 %copy-start.8 = (f32[16,16,128]{2,1,0:T(8,128)S(1)}, f32[16,16,128]{2,1,0:T(8,128)}, u32[]{:S(2)}) copy-start(f32[16,16,128]{2,1,0:T(8,128)} %param.13) | copy-start | bytes 393220
  47.4 14.5 %collective-permute-start.3 = (f32[272,128]{1,0:T(8,128)S(1)}, f32[272,128]{1,0:T(8,128)S(1)}, u32[]{:S(2)}, u32[]{:S(2)}) collective-permute-start(f32[272,128]{1,0:T(8,128)S(1)} %get-tuple-element.37), channel_id=1, source_target_pairs={{0,28},{4,8},{8,4},{12,16},{16,12},{20,24},{24,20},{28,0},{1,29},{... | collective-permute-start | bytes 417800 | tf_op jit(solution)/shard_map/ppermute | solution.py:751
  49.2 8.9 %copy-start.3 = (f32[4096,128]{1,0:T(8,128)S(1)}, f32[4096,128]{1,0:T(8,128)}, u32[]{:S(2)}) copy-start(f32[4096,128]{1,0:T(8,128)} %copy-done.2) | copy-start | bytes 6291460
  49.2 8.9 %copy-start.7 = (f32[16,16,16,128]{3,2,1,0:T(8,128)S(1)}, f32[16,16,16,128]{3,2,1,0:T(8,128)}, u32[]{:S(2)}) copy-start(f32[16,16,16,128]{3,2,1,0:T(8,128)} %param.12) | copy-start | bytes 6291460
  56.6 11.2 %copy-start.1 = (f32[4096,128]{1,0:T(8,128)}, f32[4096,128]{1,0:T(8,128)S(1)}, u32[]{:S(2)}) copy-start(f32[4096,128]{1,0:T(8,128)S(1)} %get-tuple-element.42.refs_11_.mobile) | copy-start | bytes 6291460
  56.6 11.2 %collective-permute-start.10 = (f32[272,128]{1,0:T(8,128)S(1)}, f32[272,128]{1,0:T(8,128)S(1)}, u32[]{:S(2)}, u32[]{:S(2)}) collective-permute-start(f32[272,128]{1,0:T(8,128)S(1)} %get-tuple-element.50), channel_id=1, source_target_pairs={{0,4},{4,0},{8,12},{12,8},{16,20},{20,16},{24,28},{28,24},{1,5},{5... | collective-permute-start | bytes 417800 | tf_op jit(solution)/shard_map/ppermute | solution.py:751
  56.7 11.1 %collective-permute-start.11 = (f32[272,128]{1,0:T(8,128)S(1)}, f32[272,128]{1,0:T(8,128)S(1)}, u32[]{:S(2)}, u32[]{:S(2)}) collective-permute-start(f32[272,128]{1,0:T(8,128)S(1)} %get-tuple-element.51), channel_id=1, source_target_pairs={{0,28},{4,8},{8,4},{12,16},{16,12},{20,24},{24,20},{28,0},{1,29},{... | collective-permute-start | bytes 417800 | tf_op jit(solution)/shard_map/ppermute | solution.py:751
  67.8 6.1 %copy-start.5 = (f32[4096,128]{1,0:T(8,128)}, f32[4096,128]{1,0:T(8,128)S(1)}, u32[]{:S(2)}) copy-start(f32[4096,128]{1,0:T(8,128)S(1)} %get-tuple-element.44.mobile_m) | copy-start | bytes 6291460
  67.8 6.1 %copy-start.9 = (f32[4096,128]{1,0:T(8,128)}, f32[4096,128]{1,0:T(8,128)S(1)}, u32[]{:S(2)}) copy-start(f32[4096,128]{1,0:T(8,128)S(1)} %get-tuple-element.43) | copy-start | bytes 6291460
  73.9 27.5 %all-to-all-start.1 = ((f32[8,256,128]{2,1,0:T(8,128)}), f32[8,256,128]{2,1,0:T(8,128)}, u32[]{:S(2)}, u32[]{:S(2)}) async-start(f32[8,256,128]{2,1,0:T(8,128)} %bitcast.43), calls=%async_computation.1 | async-start | bytes 2097152 | tf_op jit(solution)/shard_map/all_to_all | solution.py:846
  78.1 8.0 %collective-permute-start.6 = (f32[272,128]{1,0:T(8,128)S(1)}, f32[272,128]{1,0:T(8,128)S(1)}, u32[]{:S(2)}, u32[]{:S(2)}) collective-permute-start(f32[272,128]{1,0:T(8,128)S(1)} %get-tuple-element.45), channel_id=1, source_target_pairs={{0,4},{4,0},{8,12},{12,8},{16,20},{20,16},{24,28},{28,24},{1,5},{5... | collective-permute-start | bytes 417800 | tf_op jit(solution)/shard_map/ppermute | solution.py:751
  78.5 17.3 %collective-permute-start.7 = (f32[272,128]{1,0:T(8,128)S(1)}, f32[272,128]{1,0:T(8,128)S(1)}, u32[]{:S(2)}, u32[]{:S(2)}) collective-permute-start(f32[272,128]{1,0:T(8,128)S(1)} %get-tuple-element.46), channel_id=1, source_target_pairs={{0,28},{4,8},{8,4},{12,16},{16,12},{20,24},{24,20},{28,0},{1,29},{... | collective-permute-start | bytes 417800 | tf_op jit(solution)/shard_map/ppermute | solution.py:751
  81.1 14.8 %collective-permute-start.8 = (f32[272,128]{1,0:T(8,128)S(1)}, f32[272,128]{1,0:T(8,128)S(1)}, u32[]{:S(2)}, u32[]{:S(2)}) collective-permute-start(f32[272,128]{1,0:T(8,128)S(1)} %get-tuple-element.47), channel_id=1, source_target_pairs={{0,1},{1,0},{2,3},{3,2},{4,5},{5,4},{6,7},{7,6},{8,9},{9,8},{10,11... | collective-permute-start | bytes 417800 | tf_op jit(solution)/shard_map/ppermute | solution.py:751
  85.5 10.4 %collective-permute-start.9 = (f32[272,128]{1,0:T(8,128)S(1)}, f32[272,128]{1,0:T(8,128)S(1)}, u32[]{:S(2)}, u32[]{:S(2)}) collective-permute-start(f32[272,128]{1,0:T(8,128)S(1)} %get-tuple-element.48), channel_id=1, source_target_pairs={{1,2},{2,1},{5,6},{6,5},{9,10},{10,9},{13,14},{14,13},{17,18},{18,... | collective-permute-start | bytes 417800 | tf_op jit(solution)/shard_map/ppermute | solution.py:751

commit v2 on v1

--- a/solution.py
+++ b/solution.py
@@ -11,12 +11,14 @@
 SWEEPS = 4
 SUBSTEPS = 2
 MOBILITY_RATIO = 4.0
+NEVER = 1e30
 LANES = 128
 SUB = 8
 PARTS = 4
 FLASH_PLANES = 2
 F32 = jnp.float32
 I32 = jnp.int32
+
 
 VMEM = pl.BlockSpec(memory_space=pltpu.VMEM)
 SMEM = pl.BlockSpec(memory_space=pltpu.SMEM)
@@ -34,7 +36,6 @@
             self.ps *= 2
         self.by = self.y // self.ps
         self.half = self.pc // 2
-        self.cols = self.wide // 2
         self.most = max(1, 4 * self.slots // self.wide)
         self.cpt = SUB // self.most
         self.coefs = 4 + 3 * SUBSTEPS
@@ -90,16 +91,13 @@
     return terms[0]
 
 
-def flash_block(load, store, excess, first, nc):
+def flash_block(load, store, inverse, first, nc):
     total = tree_sum([load(c) for c in range(nc)])
     vapour = None
     for _ in range(SWEEPS):
         misfits, slopes = [], []
         for c in range(nc):
-            if vapour is None:
-                p = first[c]
-            else:
-                p = excess[c] * (1.0 / (1.0 + vapour * excess[c]))
+            p = first[c] if vapour is None else 1.0 / (vapour + inverse[c])
             r = load(c) * p
             misfits.append(r)
             slopes.append(r * p)
@@ -110,8 +108,8 @@
     gas = MOBILITY_RATIO * vapour * vapour
     share = gas / (liquid + gas)
     for c in range(nc):
-        q = 1.0 / (1.0 + vapour * excess[c])
-        store(c, load(c) * q * (1.0 + share * excess[c]))
+        p = 1.0 / (vapour + inverse[c])
+        store(c, load(c) * p * (share + inverse[c]))
 
 
 def running(terms):
@@ -122,12 +120,12 @@
 
 
 def k_scalars(k_ref, nc):
-    excess = [k_ref[c] - 1.0 for c in range(nc)]
-    first = []
+    inverse, first = [], []
     for c in range(nc):
-        e = jnp.full((1, LANES), excess[c], F32)
-        first.append(e / (1.0 + 0.5 * e))
-    return excess, first
+        e = jnp.full((1, LANES), k_ref[c], F32) - 1.0
+        inverse.append(jnp.where(e == 0.0, NEVER, 1.0 / e))
+        first.append(1.0 / (0.5 + inverse[c]))
+    return inverse, first
 
 
 def own_slots(z, slot_ref, block_ref, visit):
@@ -142,9 +140,9 @@
 
 
 def pack_kernel(
-    z, slot_ref, block_ref, open_ref, moles, pore, rate, upwind, out, src, flags, stage,
-    in_sem, out_sem,
+    z, slot_ref, block_ref, open_ref, moles, pore, rate, upwind, *refs
 ):
+    outs, (src, flags, in_sem) = refs[: z.wide], refs[z.wide :]
     nc, slots = z.nc, z.slots
     first = nc * slots
     reads = [
@@ -156,42 +154,19 @@
     for copy in reads:
         copy.start()
     sub = iota((SUB, LANES), 0)
-    picks = [jnp.zeros((SUB, LANES), I32) for _ in range(z.cols)]
+    picks = [jnp.zeros((SUB, LANES), I32) for _ in range(z.wide)]
+    target = [lax.rem(lax.axis_index("wide") + s, z.wide) for s in range(z.wide)]
     opens = [jnp.zeros((SUB, z.pc), I32) for _ in range(2)]
     row_id = iota((SUB, z.pc), 0)
 
     def visit(i, p0, rank):
-        for c in range(z.cols):
-            hit = ((sub % z.most) == rank) & (p0 == c)
-            picks[c] = jnp.where(hit, i, picks[c])
+        for s in range(z.wide):
+            hit = (sub % z.most) == jnp.where(p0 == lax.div(target[s], 2), rank, -1)
+            picks[s] = jnp.where(hit, i, picks[s])
         for d in range(2):
             opens[d] = jnp.where(row_id == i, open_ref[d, i], opens[d])
 
     own_slots(z, slot_ref, block_ref, visit)
-
-    def send(c):
-        per = z.jt * z.tiles_out * SUB
-
-        def tile(m, carry):
-            for h in range(2):
-                for j in range(z.jt):
-                    v = None
-                    for cp in range(z.cpt):
-                        part = sub_gather(
-                            src[
-                                pl.ds(pl.multiple_of((m * z.cpt + cp) * slots, slots), slots),
-                                pl.ds(h * z.half + j * LANES, LANES),
-                            ],
-                            picks[c],
-                        )
-                        v = part if v is None else jnp.where(sub // z.most >= cp, part, v)
-                    row = ((2 * c + h) * z.jt + j) * z.tiles_out * SUB + m * SUB
-                    stage[pl.ds(pl.multiple_of(row, SUB), SUB), :] = v
-            return carry
-
-        lax.fori_loop(0, z.tiles_out, tile, 0)
-        rows = pl.ds(2 * c * per, 2 * per)
-        return pltpu.make_async_copy(stage.at[rows, :], out.at[rows, :], out_sem.at[c])
 
     for copy in reads:
         copy.wait()
@@ -206,17 +181,30 @@
     spare = src.shape[0] - (g + 3 * slots + n_flags)
     if spare:
         src[pl.ds(g + 3 * slots + n_flags, spare), :] = jnp.zeros((spare, z.pc), F32)
-    writes = []
-    for c in range(z.cols):
-        writes.append(send(c))
-        writes[-1].start()
-    for copy in writes:
-        copy.wait()
-
-
-def spread_kernel(z, slot_ref, block_ref, recv_hbm, out, recv, sem):
-    read = pltpu.make_async_copy(recv_hbm, recv, sem)
-    read.start()
+
+    def tile(m, carry):
+        for s in range(z.wide):
+            left = lax.rem(target[s], 2) * z.half
+            for j in range(z.jt):
+                lanes = pl.ds(pl.multiple_of(left + j * LANES, LANES), LANES)
+                v = None
+                for cp in range(z.cpt):
+                    rows = pl.ds(pl.multiple_of((m * z.cpt + cp) * slots, slots), slots)
+                    part = sub_gather(src[rows, lanes], picks[s])
+                    v = part if v is None else jnp.where(sub // z.most >= cp, part, v)
+                row = (j * z.tiles_out + m) * SUB
+                outs[s][pl.ds(pl.multiple_of(row, SUB), SUB), :] = v
+        return carry
+
+    lax.fori_loop(0, z.tiles_out, tile, 0)
+
+
+def sender(z, s):
+    return lax.rem(lax.axis_index("wide") + (z.wide - s), z.wide)
+
+
+def spread_kernel(z, slot_ref, block_ref, *refs):
+    chunks, out = refs[: z.wide], refs[z.wide]
     sub = iota((SUB, LANES), 0)
     ranks = jnp.zeros((SUB, LANES), I32)
     column = jnp.zeros((SUB, LANES), I32)
@@ -227,29 +215,24 @@
         column = jnp.where(sub == i, p0, column)
 
     own_slots(z, slot_ref, block_ref, visit)
-    read.wait()
-
-    def tile(m, carry):
-        for h in range(2):
+    for s in range(z.wide):
+        source = sender(z, s)
+        left = lax.rem(source, 2) * z.half
+        hit = column == lax.div(source, 2)
+
+        def tile(m, carry, s=s, left=left, hit=hit):
             for j in range(z.jt):
-                parts = []
-                for c in range(z.cols):
-                    row = (((2 * c + h) * z.jt + j) * z.tiles_back + m) * SUB
-                    parts.append(recv[pl.ds(pl.multiple_of(row, SUB), SUB), :])
+                row = (j * z.tiles_back + m) * SUB
+                part = chunks[s][pl.ds(pl.multiple_of(row, SUB), SUB), :]
+                lanes = pl.ds(pl.multiple_of(left + j * LANES, LANES), LANES)
                 for cp in range(z.cpt):
-                    v = sub_gather(parts[0], cp * z.most + ranks)
-                    for c in range(1, z.cols):
-                        v = jnp.where(
-                            column == c, sub_gather(parts[c], cp * z.most + ranks), v
-                        )
-                    row = (m * z.cpt + cp) * SUB
-                    out[
-                        pl.ds(pl.multiple_of(row, SUB), SUB),
-                        pl.ds(h * z.half + j * LANES, LANES),
-                    ] = v
-        return carry
-
-    lax.fori_loop(0, z.tiles_back, tile, 0)
+                    rows = pl.ds(pl.multiple_of((m * z.cpt + cp) * SUB, SUB), SUB)
+                    out[rows, lanes] = jnp.where(
+                        hit, sub_gather(part, cp * z.most + ranks), out[rows, lanes]
+                    )
+            return carry
+
+        lax.fori_loop(0, z.tiles_back, tile, 0, unroll=2)
 
 
 def tables(z, slot_ref, block_ref, tab, gather):
@@ -345,18 +328,14 @@
     return out, g - out
 
 
-def stream(z, src, dst, sem):
-    rows = [pl.ds(n * z.cells // PARTS, z.cells // PARTS) for n in range(PARTS)]
-    return [
-        pltpu.make_async_copy(src.at[:, r, :], dst.at[:, r, :], sem.at[n])
-        for n, r in enumerate(rows)
-    ]
+def cells_of(z, ref, c, start, count):
+    if len(ref.shape) == 3:
+        return ref[c, pl.ds(start, count), :]
+    return ref[pl.ds(pl.multiple_of(c * z.cells + start, z.z), count), :]
 
 
 def plane(z, ref, c, x):
-    if len(ref.shape) == 3:
-        return ref[c, pl.ds(pl.multiple_of(x * z.z, z.z), z.z), :]
-    return ref[pl.ds(pl.multiple_of(c * z.cells + x * z.z, z.z), z.z), :]
+    return cells_of(z, ref, c, pl.multiple_of(x * z.z, z.z), z.z)
 
 
 def matrix_messages(z, mobile, rate, upwind, t, wide_a, wide_b, deep_a, deep_b):
@@ -393,31 +372,61 @@
         deep_b[rows, :] = g - out
 
 
-def flash_field(z, moles, mobile, k_ref, low=0, high=None, hop=1):
-    excess, first = k_scalars(k_ref, z.nc)
+def flash_field(z, moles, mobile, k_ref, low=0, high=None, hop=1, arrived=None):
+    inverse, first = k_scalars(k_ref, z.nc)
     step = FLASH_PLANES
     high = z.x // step if high is None else high
 
     def block(n, carry):
-        def rows(c):
-            return pl.ds(pl.multiple_of(c * z.cells + n * step * z.z, z.z), step * z.z)
+        if arrived is not None:
+            arrived(n * step)
+        start = pl.multiple_of(n * step * z.z, step * z.z)
 
         def store(c, v):
-            mobile[rows(c), :] = v
-
-        flash_block(lambda c: moles[rows(c), :], store, excess, first, z.nc)
+            mobile[pl.ds(pl.multiple_of(c * z.cells + start, z.z), step * z.z), :] = v
+
+        flash_block(
+            lambda c: cells_of(z, moles, c, start, step * z.z), store, inverse, first, z.nc
+        )
         return carry
 
     lax.fori_loop(0, -(-(high - low) // hop), lambda i, a: block(low + i * hop, a), 0)
 
 
 def first_matrix_kernel(
-    z, k_ref, slot_ref, block_ref, moles, rate, upwind, mobile, wide_a, wide_b, deep_a, deep_b,
-    tab, gather,
+    z, k_ref, slot_ref, block_ref, moles_hbm, rate_hbm, upwind_hbm, pore_hbm,
+    mobile, early, wide_a, wide_b, deep_a, deep_b, tab, gather, rate, upwind, pore,
+    moles, sem, part_sem,
 ):
+    reads = [
+        pltpu.make_async_copy(src, dst, sem.at[n])
+        for n, (src, dst) in enumerate(
+            ((rate_hbm, rate), (upwind_hbm, upwind), (pore_hbm, pore))
+        )
+    ]
+    planes = z.x // PARTS
+    parts = []
+    for n in range(PARTS):
+        rows = pl.ds(n * planes * z.z, planes * z.z)
+        parts.append(
+            pltpu.make_async_copy(moles_hbm.at[:, rows, :], moles.at[:, rows, :], part_sem.at[n])
+        )
+    for read in parts + reads:
+        read.start()
     tables(z, slot_ref, block_ref, tab, gather)
-    flash_field(z, moles, mobile, k_ref)
+
+    def arrived(x):
+        for n, part in enumerate(parts):
+
+            @pl.when(x == n * planes)
+            def _(part=part):
+                part.wait()
+
+    flash_field(z, moles, mobile, k_ref, arrived=arrived)
+    for read in reads:
+        read.wait()
     matrix_messages(z, mobile, rate, upwind, 0, wide_a, wide_b, deep_a, deep_b)
+    matrix_update(z, 0, moles, mobile, rate, upwind, pore, None, early)
 
 
 def frac_messages(z, mobile, coef, tab, t, frac_a, frac_b):
@@ -439,24 +448,24 @@
     frac_b[rows, :] = into
 
 
-def unpack_rows(z, tab, recv_hbm, recv, sem, js, moles, coef):
+def staged(z, chunks, js, recv, sem):
+    lane_tile = z.tiles_out * SUB
+    return [
+        pltpu.make_async_copy(
+            chunks[s].at[pl.ds(j * lane_tile, lane_tile), :],
+            recv.at[pl.ds((sender(z, s) * len(js) + n) * lane_tile, lane_tile), :],
+            sem.at[s * len(js) + n],
+        )
+        for s in range(z.wide)
+        for n, j in enumerate(js)
+    ]
+
+
+def unpack_rows(z, tab, recv, js, moles, coef):
     lane_tile = z.tiles_out * SUB
     stride = len(js) * lane_tile
-    reads = [
-        pltpu.make_async_copy(
-            recv_hbm.at[pl.ds((w * z.jt + j) * lane_tile, lane_tile), :],
-            recv.at[pl.ds((w * len(js) + n) * lane_tile, lane_tile), :],
-            sem.at[w * len(js) + n],
-        )
-        for w in range(z.wide)
-        for n, j in enumerate(js)
-    ]
-    for read in reads:
-        read.start()
     from_sub = [tab[pl.ds(h * SUB, SUB), :] for h in range(2)]
     shift = [tab[pl.ds(2 * SUB + h * SUB, SUB), :] for h in range(2)]
-    for read in reads:
-        read.wait()
 
     def channel(c, dst, first_row, default):
         for t, j in enumerate(js):
@@ -492,46 +501,43 @@
     lax.fori_loop(0, z.coefs, weight, 0, unroll=2)
 
 
-def frac_edge_kernel(z, k_ref, tab, recv_hbm, moles, mobile, coef, frac_a, frac_b, recv, sem):
-    unpack_rows(z, tab, recv_hbm, recv, sem, (0, z.jt - 1), moles, coef)
+def frac_edge_kernel(z, k_ref, tab, *refs):
+    chunks, refs = refs[: z.wide], refs[z.wide :]
+    moles, mobile, coef, frac_a, frac_b, recv_inner, recv, sem, sem_inner = refs
+    edge = (0, z.jt - 1)
+    now = staged(z, chunks, edge, recv, sem)
+    later = staged(z, chunks, tuple(range(1, z.jt - 1)), recv_inner, sem_inner)
+    for read in now:
+        read.start()
+    for read in now:
+        read.wait()
+    for read in later:
+        read.start()
+    unpack_rows(z, tab, recv, edge, moles, coef)
     last = z.x // FLASH_PLANES
     flash_field(z, moles, mobile, k_ref, 0, last, last - 1)
     frac_messages(z, mobile, coef, tab, 0, frac_a, frac_b)
-
-
-def frac_inner_kernel(
-    z, k_ref, tab, recv_hbm, moles_in, mobile_in, coef_in, moles, mobile, coef, recv, sem
-):
-    unpack_rows(z, tab, recv_hbm, recv, sem, tuple(range(1, z.jt - 1)), moles, coef)
+    for read in later:
+        read.wait()
+
+
+def frac_inner_kernel(z, k_ref, tab, recv, moles_in, mobile_in, coef_in, moles, mobile, coef):
+    unpack_rows(z, tab, recv, tuple(range(1, z.jt - 1)), moles, coef)
     flash_field(z, moles, mobile, k_ref, 1, z.x // FLASH_PLANES - 1)
 
 
-def each_plane(z, at, streams=()):
-    def arrived(x):
-        for n in range(1, PARTS):
-
-            @pl.when(x == n * z.x // PARTS - 1)
-            def _(n=n):
-                for copies in streams:
-                    copies[n].wait()
-
+def each_plane(z, at):
     def middle(x, carry):
-        if streams:
-            arrived(x)
         at(x, False, False)
         return carry
 
-    for copies in streams:
-        copies[0].wait()
     at(0, True, False)
     lax.fori_loop(1, z.x - 1, middle, 0)
     at(z.x - 1, False, True)
 
 
-def matrix_update(z, t, moles, mobile, rate, upwind, pore, halos, new, mobile_f=None, coef=None,
-                  streams=()):
-    *wide, deep_a, deep_b = halos
-    wide_a, wide_b = wide or (None, None)
+def matrix_update(z, t, moles, mobile, rate, upwind, pore, halos, new, mobile_f=None, coef=None):
+    wide_a, wide_b, deep_a, deep_b = halos or (None,) * 4
     nc = z.nc
     even_w = lax.rem(lax.axis_index("wide"), 2) == 0
     even_d = lax.rem(lax.axis_index("depth"), 2) == 0
@@ -550,12 +556,18 @@
         oz, iz = face(z, rate, upwind, t, 1, x)
         oy, iy = face(z, rate, upwind, t, 2, x)
         if low:
-            pox, pix = (1.0, side(wide_a, wide_b, True, nc * z.z, z.z)) if wide else (0.0, 0.0)
+            pox, pix = (1.0, side(wide_a, wide_b, True, nc * z.z, z.z)) if halos else (0.0, 0.0)
         else:
             pox, pix = face(z, rate, upwind, t, 0, x - 1)
-        wz = jnp.broadcast_to(side(deep_a, deep_b, True, nc * z.x + x, 1), (z.z, LANES))
-        poz = jnp.where(sub == 0, 1.0, pltpu.roll(oz, 1, 0))
-        piz = jnp.where(sub == 0, wz, pltpu.roll(iz, 1, 0))
+        if halos:
+            wz = jnp.broadcast_to(side(deep_a, deep_b, True, nc * z.x + x, 1), (z.z, LANES))
+            poz = jnp.where(sub == 0, 1.0, pltpu.roll(oz, 1, 0))
+            piz = jnp.where(sub == 0, wz, pltpu.roll(iz, 1, 0))
+            niz = iz
+        else:
+            poz = jnp.where(sub == 0, 0.0, pltpu.roll(oz, 1, 0))
+            piz = jnp.where(sub == 0, 0.0, pltpu.roll(iz, 1, 0))
+            niz = jnp.where(sub == z.z - 1, 0.0, iz)
         poy, piy = lane_roll(oy, 1), lane_roll(iy, 1)
         own = ox + pix + oz + piz + oy + piy
         if coef is not None:
@@ -564,30 +576,32 @@
             w5 = w5 * inv
         own = own * inv
         ax, bx = ix * inv, pox * inv
-        az, bz = iz * inv, poz * inv
+        az, bz = niz * inv, poz * inv
         ay, by = iy * inv, poy * inv
         for c in range(nc):
             g = plane(z, mobile, c, x)
             v = plane(z, moles, c, x) - own * g
             if not low:
                 v = v + bx * plane(z, mobile, c, x - 1)
-            elif wide:
+            elif halos:
                 v = v + bx * side(wide_a, wide_b, True, c * z.z, z.z)
             if not high:
                 v = v + ax * plane(z, mobile, c, x + 1)
-            elif wide:
+            elif halos:
                 v = v + ax * side(wide_a, wide_b, False, c * z.z, z.z)
-            hz0 = jnp.broadcast_to(side(deep_a, deep_b, True, c * z.x + x, 1), (z.z, LANES))
-            hz1 = jnp.broadcast_to(side(deep_a, deep_b, False, c * z.x + x, 1), (z.z, LANES))
-            zb = jnp.where(sub == 0, hz0, pltpu.roll(g, 1, 0))
-            za = jnp.where(sub == z.z - 1, hz1, pltpu.roll(g, z.z - 1, 0))
+            zb, za = pltpu.roll(g, 1, 0), pltpu.roll(g, z.z - 1, 0)
+            if halos:
+                hz0 = jnp.broadcast_to(side(deep_a, deep_b, True, c * z.x + x, 1), (z.z, LANES))
+                hz1 = jnp.broadcast_to(side(deep_a, deep_b, False, c * z.x + x, 1), (z.z, LANES))
+                zb = jnp.where(sub == 0, hz0, zb)
+                za = jnp.where(sub == z.z - 1, hz1, za)
             v = v + (az * za + bz * zb)
             v = v + (ay * lane_roll(g, -1) + by * lane_roll(g, 1))
             if coef is not None:
                 v = v + w5 * plane(z, mobile_f, c, x)
             new[pl.ds(pl.multiple_of(c * z.cells + x * z.z, z.z), z.z), :] = v
 
-    each_plane(z, at, streams)
+    each_plane(z, at)
 
 
 def exchange_weights(z, t, coef, x):
@@ -596,79 +610,63 @@
     return into, g - into
 
 
-def matrix_early_kernel(
-    z, t, moles, mobile, rate, upwind, pore, hc, hd, new, stage, sem
+def matrix_kernel(
+    z, t, k_ref, moles, mobile, mobile_f, coef, rate, upwind, pore, ha, hb, hc, hd, new,
+    mobile_new, wide_a, wide_b, deep_a, deep_b,
 ):
-    matrix_update(z, t, moles, mobile, rate, upwind, pore, (hc, hd), stage)
-    writes = [
-        pltpu.make_async_copy(stage.at[rows, :], new.at[rows, :], sem.at[n])
-        for n, rows in enumerate(
-            pl.ds(n * z.nc * z.cells // PARTS, z.nc * z.cells // PARTS) for n in range(PARTS)
-        )
-    ]
-    for copy in writes:
-        copy.start()
-    for copy in writes:
-        copy.wait()
-
-
-def matrix_kernel(
-    z, t, k_ref, early, mobile_hbm, mobile_f, coef, rate, upwind, pore, ha, hb, new,
-    mobile_new, wide_a, wide_b, deep_a, deep_b, moles, mobile, sem,
-):
-    streams = (stream(z, early, moles, sem.at[0]), stream(z, mobile_hbm, mobile, sem.at[1]))
-    for n in range(PARTS):
-        for copies in streams:
-            copies[n].start()
-
-    even = lax.rem(lax.axis_index("wide"), 2) == 0
-
-    def side(first, row):
+    even_w = lax.rem(lax.axis_index("wide"), 2) == 0
+    even_d = lax.rem(lax.axis_index("depth"), 2) == 0
+    sub = iota((z.z, LANES), 0)
+
+    def wide_side(first, row):
         rows = pl.ds(row, z.z)
         if first:
-            return jnp.where(even, hb[rows, :], ha[rows, :])
-        return jnp.where(even, ha[rows, :], hb[rows, :])
+            return jnp.where(even_w, hb[rows, :], ha[rows, :])
+        return jnp.where(even_w, ha[rows, :], hb[rows, :])
+
+    def deep_side(first, row):
+        rows = pl.ds(row, 1)
+        v = (
+            jnp.where(even_d, hd[rows, :], hc[rows, :])
+            if first
+            else jnp.where(even_d, hc[rows, :], hd[rows, :])
+        )
+        return jnp.broadcast_to(v, (z.z, LANES))
 
     def at(x, low, high):
         inv = 1.0 / plane(z, pore, 0, x)
         w2, w5 = exchange_weights(z, t, coef, x)
+        w2 = w2 + jnp.where(sub == 0, deep_side(True, z.nc * z.x + x), 0.0)
         if low:
-            w2 = w2 + side(True, z.nc * z.z)
+            w2 = w2 + wide_side(True, z.nc * z.z)
         w2, w5 = w2 * inv, w5 * inv
+        bz = jnp.where(sub == 0, inv, 0.0)
+        az = jnp.where(sub == z.z - 1, face(z, rate, upwind, t, 1, x)[1] * inv, 0.0)
         ax = face(z, rate, upwind, t, 0, x)[1] * inv if high else None
         for c in range(z.nc):
             v = plane(z, moles, c, x) - w2 * plane(z, mobile, c, x)
             v = v + w5 * plane(z, mobile_f, c, x)
+            v = v + (bz * deep_side(True, c * z.x + x) + az * deep_side(False, c * z.x + x))
             if low:
-                v = v + inv * side(True, c * z.z)
+                v = v + inv * wide_side(True, c * z.z)
             if high:
-                v = v + ax * side(False, c * z.z)
+                v = v + ax * wide_side(False, c * z.z)
             new[pl.ds(pl.multiple_of(c * z.cells + x * z.z, z.z), z.z), :] = v
 
-    each_plane(z, at, streams)
+    each_plane(z, at)
     flash_field(z, new, mobile_new, k_ref)
     matrix_messages(z, mobile_new, rate, upwind, t + 1, wide_a, wide_b, deep_a, deep_b)
 
 
 def last_matrix_kernel(
-    z, t, moles_hbm, mobile_hbm, mobile_f_hbm, coef, rate, upwind, pore, ha, hb, hc, hd, new,
-    moles, mobile, mobile_f, sem,
+    z, t, moles, mobile, mobile_f, coef, rate, upwind, pore, ha, hb, hc, hd, new
 ):
-    streams = tuple(
-        stream(z, src, dst, sem.at[n])
-        for n, (src, dst) in enumerate(
-            ((moles_hbm, moles), (mobile_hbm, mobile), (mobile_f_hbm, mobile_f))
-        )
-    )
-    for n in range(PARTS):
-        for copies in streams:
-            copies[n].start()
     matrix_update(
-        z, t, moles, mobile, rate, upwind, pore, (ha, hb, hc, hd), new, mobile_f, coef, streams
-    )
-
-
-def frac_update(z, t, tab, moles, mobile, mobile_m, coef, frac_a, frac_b, new, streams=()):
+        z, t, moles, mobile, rate, upwind, pore, (ha, hb, hc, hd), new, mobile_f, coef
+    )
+
+
+def frac_update(z, t, tab, moles, mobile, mobile_m, coef, frac_a, frac_b, new):
     nc = z.nc
     even = lax.rem(lax.axis_index("wide"), 2) == 0
     here = (tab[pl.ds(2 * SUB, 2 * SUB), :] >= 0).astype(F32)
@@ -710,24 +708,21 @@
             v = v + w2 * plane(z, mobile_m, c, x)
             new[pl.ds(pl.multiple_of(c * z.cells + x * z.z, z.z), z.z), :] = v
 
-    each_plane(z, at, streams)
+    each_plane(z, at)
 
 
 def frac_kernel(
-    z, t, k_ref, tab, moles, mobile, mobile_hbm, coef, fa, fb, new, mobile_new, frac_a, frac_b,
-    mobile_m, sem,
+    z, t, k_ref, tab, moles, mobile, mobile_m, coef, fa, fb, new, mobile_new, frac_a, frac_b
 ):
-    copies = stream(z, mobile_hbm, mobile_m, sem)
-    for copy in copies:
-        copy.start()
-    frac_update(z, t, tab, moles, mobile, mobile_m, coef, fa, fb, new, (copies,))
+    frac_update(z, t, tab, moles, mobile, mobile_m, coef, fa, fb, new)
     flash_field(z, new, mobile_new, k_ref)
     frac_messages(z, mobile_new, coef, tab, t + 1, frac_a, frac_b)
 
 
 def last_frac_kernel(
-    z, t, tab, gather, moles, mobile, mobile_m, coef, fa, fb, back, new, stage, sem
+    z, t, tab, gather, moles, mobile, mobile_m, coef, fa, fb, *refs
 ):
+    backs, (new, stage, sem) = refs[: z.wide], refs[z.wide :]
     frac_update(z, t, tab, moles, mobile, mobile_m, coef, fa, fb, new)
     maps = gather[:, : 3 * z.blocks].astype(jnp.bfloat16)
 
@@ -736,9 +731,18 @@
         return carry
 
     lax.fori_loop(0, z.nc, channel, 0, unroll=4)
-    copy = pltpu.make_async_copy(stage, back, sem)
-    copy.start()
-    copy.wait()
+    size = z.jt * z.tiles_back * SUB
+    writes = []
+    for s in range(z.wide):
+        target = lax.rem(lax.axis_index("wide") + s, z.wide)
+        writes.append(
+            pltpu.make_async_copy(
+                stage.at[pl.ds(target * size, size), :], backs[s], sem.at[s]
+            )
+        )
+        writes[-1].start()
+    for copy in writes:
+        copy.wait()
 
 
 def swap(value, axis, ahead, ends=True):
@@ -807,7 +811,6 @@
     z = Sizes(matrix_moles, frac_moles)
     bind = lambda f, *a: functools.partial(f, z, *a)
     blocks, slot_patch, kvalues = in_hbm(patch_block.T), in_hbm(slot_patch), in_hbm(kvalues)
-    moles = matrix_moles.reshape(-1, z.y)
     pore = pore_matrix.reshape(-1, z.y)
     rate = matrix_rate.reshape(-1, z.y)
     upwind = matrix_upwind.reshape(-1, z.y)
@@ -816,13 +819,9 @@
     rows_out = z.wide * z.jt * z.tiles_out * SUB
     rows_back = z.wide * z.jt * z.tiles_back * SUB
     src_rows = z.tiles_out * z.cpt * z.slots
-    hbm_field = shape(z.nc * z.cells, space=pltpu.HBM)
-    stacked = lambda v: in_hbm(v.reshape(z.nc, z.cells, LANES))
-    stream_buf = pltpu.VMEM((z.nc, z.cells, LANES), F32)
-
     send = call(
         bind(pack_kernel), [SMEM] * 3 + [HBM] * 4,
-        shape(rows_out, space=pltpu.HBM),
+        (shape(rows_out // z.wide),) * z.wide,
         (
             slot_patch,
             blocks,
@@ -835,108 +834,99 @@
         scratch=[
             pltpu.VMEM((src_rows, z.pc), F32),
             pltpu.VMEM((3 * SUBSTEPS * z.slots, z.pc), I32),
-            pltpu.VMEM((rows_out, LANES), F32),
             pltpu.SemaphoreType.DMA((4,)),
-            pltpu.SemaphoreType.DMA((z.cols,)),
         ],
-        out_specs=HBM,
-    )
-
-    def trade(v):
-        return lax.all_to_all(v, "wide", split_axis=0, concat_axis=0, tiled=True)
+    )
+
+    def trade(chunks):
+        got = [chunks[0]]
+        for s in range(1, z.wide):
+            pairs = [(i, (i + s) % z.wide) for i in range(z.wide)]
+            got.append(lax.ppermute(chunks[s], "wide", pairs))
+        return tuple(got)
 
     def exchange(a, b, axis):
         return swap(a, axis, True), swap(b, axis, False, axis == "wide")
 
     recv = trade(send)
-    mobile_m, wa, wb, da, db, tab, gather = call(
-        bind(first_matrix_kernel), [SMEM] * 3 + [VMEM] * 3,
+    mobile_m, early, wa, wb, da, db, tab, gather, rate, upwind, pore = call(
+        bind(first_matrix_kernel), [SMEM] * 3 + [HBM] * 4,
         (
-            field, msg_w, msg_w, msg_d, msg_d, pltpu.VMEM((6 * SUB, LANES), I32),
+            field, field, msg_w, msg_w, msg_d, msg_d, pltpu.VMEM((6 * SUB, LANES), I32),
             shape(z.places, -(-3 * z.blocks // LANES) * LANES),
+            shape(3 * z.cells), pltpu.VMEM((3 * SUBSTEPS * z.cells, LANES), I32),
+            shape(z.cells),
         ),
-        (kvalues, slot_patch, blocks, *in_vmem(moles, rate, upwind)),
+        (
+            kvalues, slot_patch, blocks, in_hbm(matrix_moles.reshape(z.nc, z.cells, LANES)),
+            in_hbm(rate), in_hbm(upwind), in_hbm(pore),
+        ),
+        scratch=[
+            pltpu.VMEM((z.nc, z.cells, LANES), F32),
+            pltpu.SemaphoreType.DMA((3,)),
+            pltpu.SemaphoreType.DMA((PARTS,)),
+        ],
     )
     wide_halos = exchange(wa, wb, "wide")
     deep_halos = exchange(da, db, "depth")
-    early = call(
-        bind(matrix_early_kernel, 0), [VMEM] * 7, hbm_field,
-        in_vmem(moles, mobile_m, rate, upwind, pore, *deep_halos),
+    coef_field = shape(z.coefs * z.cells)
+    tiles, inner = z.wide * z.tiles_out * SUB, z.jt - 2
+    moles_f, mobile_f, coef, fa, fb, staged_rows = call(
+        bind(frac_edge_kernel), [SMEM] + [VMEM] * 2 + [HBM] * (z.wide - 1),
+        (field, field, coef_field, msg_w, msg_w, shape(inner * tiles)),
+        (kvalues, *in_vmem(tab, recv[0]), *(in_hbm(v) for v in recv[1:])),
         scratch=[
-            pltpu.VMEM((z.nc * z.cells, LANES), F32), pltpu.SemaphoreType.DMA((PARTS,))
-        ],
-        out_specs=HBM,
-    )
-    coef_field = shape(z.coefs * z.cells)
-    tiles = z.wide * z.tiles_out * SUB
-    moles_f, mobile_f, coef, fa, fb = call(
-        bind(frac_edge_kernel), [SMEM, VMEM, HBM],
-        (field, field, coef_field, msg_w, msg_w),
-        (kvalues, *in_vmem(tab), in_hbm(recv)),
-        scratch=[pltpu.VMEM((2 * tiles, LANES), F32), pltpu.SemaphoreType.DMA((2 * z.wide,))],
-    )
-    fa, fb = exchange(fa, fb, "wide")
-    inner = z.jt - 2
-    moles_f, mobile_f, coef = call(
-        bind(frac_inner_kernel), [SMEM, VMEM, HBM] + [VMEM] * 3,
-        (field, field, coef_field),
-        (kvalues, *in_vmem(tab), in_hbm(recv), *in_vmem(moles_f, mobile_f, coef)),
-        scratch=[
-            pltpu.VMEM((inner * tiles, LANES), F32),
+            pltpu.VMEM((2 * tiles, LANES), F32),
+            pltpu.SemaphoreType.DMA((2 * z.wide,)),
             pltpu.SemaphoreType.DMA((inner * z.wide,)),
         ],
+    )
+    fa, fb = exchange(fa, fb, "wide")
+    moles_f, mobile_f, coef = call(
+        bind(frac_inner_kernel), [SMEM] + [VMEM] * 5,
+        (field, field, coef_field),
+        (kvalues, *in_vmem(tab, staged_rows, moles_f, mobile_f, coef)),
         aliases={3: 0, 4: 1, 5: 2},
     )
     new_f, new_mobile_f, fa, fb = call(
-        bind(frac_kernel, 0), [SMEM] + [VMEM] * 3 + [HBM] + [VMEM] * 3,
+        bind(frac_kernel, 0), [SMEM] + [VMEM] * 7,
         (field, field, msg_w, msg_w),
-        (
-            kvalues, *in_vmem(tab, moles_f, mobile_f), stacked(mobile_m),
-            *in_vmem(coef, fa, fb),
-        ),
-        scratch=[stream_buf, pltpu.SemaphoreType.DMA((PARTS,))],
-        kept=(rate, upwind, pore),
+        (kvalues, *in_vmem(tab, moles_f, mobile_f, mobile_m, coef, fa, fb)),
     )
     fa, fb = exchange(fa, fb, "wide")
     moles, mobile_m, wa, wb, da, db = call(
-        bind(matrix_kernel, 0), [SMEM] + [HBM] * 2 + [VMEM] * 7,
+        bind(matrix_kernel, 0), [SMEM] + [VMEM] * 11,
         (field, field, msg_w, msg_w, msg_d, msg_d),
         (
-            kvalues, stacked(early), stacked(mobile_m),
-            *in_vmem(mobile_f, coef, rate, upwind, pore, *wide_halos),
+            kvalues,
+            *in_vmem(early, mobile_m, mobile_f, coef, rate, upwind, pore),
+            *in_vmem(*wide_halos, *deep_halos),
         ),
-        scratch=[stream_buf, stream_buf, pltpu.SemaphoreType.DMA((2, PARTS))],
-        kept=(new_f, new_mobile_f, tab),
     )
     wide_halos = exchange(wa, wb, "wide")
     deep_halos = exchange(da, db, "depth")
     t = SUBSTEPS - 1
     back = call(
         bind(last_frac_kernel, t), [VMEM] * 8,
-        shape(rows_back, space=pltpu.HBM),
+        (shape(rows_back // z.wide, space=pltpu.HBM),) * z.wide,
         in_vmem(tab, gather, new_f, new_mobile_f, mobile_m, coef, fa, fb),
         scratch=[
             pltpu.VMEM((z.nc * z.cells, LANES), F32),
             pltpu.VMEM((rows_back, LANES), F32),
-            pltpu.SemaphoreType.DMA,
+            pltpu.SemaphoreType.DMA((z.wide,)),
         ],
-        out_specs=HBM,
+        out_specs=(HBM,) * z.wide,
     )
     returned = trade(back)
     moles = call(
-        bind(last_matrix_kernel, t), [HBM] * 3 + [VMEM] * 8,
+        bind(last_matrix_kernel, t), [VMEM] * 11,
         jax.ShapeDtypeStruct((z.nc * z.cells, LANES), F32),
-        (
-            stacked(moles), stacked(mobile_m), stacked(new_mobile_f),
-            *in_vmem(coef, rate, upwind, pore, *wide_halos, *deep_halos),
-        ),
-        scratch=[stream_buf] * 3 + [pltpu.SemaphoreType.DMA((3, PARTS))],
+        in_vmem(moles, mobile_m, new_mobile_f, coef, rate, upwind, pore, *wide_halos, *deep_halos),
     )
     frac = call(
-        bind(spread_kernel), [SMEM] * 2 + [HBM],
+        bind(spread_kernel), [SMEM] * 2 + [VMEM] * z.wide,
         jax.ShapeDtypeStruct((z.nc * z.slots, z.pc), F32),
-        (slot_patch, blocks, in_hbm(returned)),
-        scratch=[pltpu.VMEM((rows_back, LANES), F32), pltpu.SemaphoreType.DMA],
+        (slot_patch, blocks, *in_vmem(*returned)),
     )
     return moles.reshape(matrix_moles.shape), frac.reshape(frac_moles.shape)
 

time: 106 us -> 85.4 us (0.81)
  waiting for transfers between devices: 24.3 us -> 5.94 us
  starting transfers between devices: 24.3 us -> 34 us
  Pallas kernels: 51.8 us -> 42.8 us
  local copies, waits for them, and re-layouts: 2.94 us -> 0.83 us
    ppermute x0 -> x14, starting transfers between devices: none -> 19.9 us  [trade(): got.append(lax.ppermute(chunks[s], 'wide', pairs))]
    all_to_all x2 -> x0, waiting for transfers between devices: 14.6 us -> none  [trade(): return lax.all_to_all(v, 'wide', split_axis=0, concat_axis=0, tiled=True)]
    ppermute x12, waiting for transfers between devices: 9.72 us -> 0.03 us  [swap(): return lax.ppermute(value, axis, pairs)]
    all_to_all x2 -> x0, starting transfers between devices: 9.61 us -> none  [trade(): return lax.all_to_all(v, 'wide', split_axis=0, concat_axis=0, tiled=True)]
    pallas_call x10 -> x9, Pallas kernels: 51.8 us -> 42.8 us  [call(): pl.pallas_call(body, out_shape=out_shape, in_specs=in_specs, out_specs=ou...]
    ppermute x0 -> x14, waiting for transfers between devices: none -> 5.91 us  [trade(): got.append(lax.ppermute(chunks[s], 'wide', pairs))]
    unnamed x20 -> x16, local copies, waits for them, and re-layouts: 2.94 us -> 0.83 us
  transfers between devices with their start and end apart: 14 -> 26, of which waited for: 2 -> 5; matrix products, arithmetic and copies ran while one was open for 0% -> 0% of each run, Pallas kernels for 33% -> 37%
where the time goes in v2:
time: 85.4 us; the launch traced here: 84.4 us
  Pallas kernels  42.8 us (50%)
  starting transfers between devices  34 us (40%)
  waiting for transfers between devices  5.94 us (7%)
    pallas_call x9, Pallas kernels, call(): pl.pallas_call(body, out_shape=out_shape, in_specs=in_specs, out_specs=ou...  42.8 us
    ppermute x14, starting transfers between devices, trade(): got.append(lax.ppermute(chunks[s], 'wide', pairs))  19.9 us
    ppermute x12, starting transfers between devices, swap(): return lax.ppermute(value, axis, pairs)  14.1 us
    ppermute x14, waiting for transfers between devices, trade(): got.append(lax.ppermute(chunks[s], 'wide', pairs))  5.91 us
  transfers between devices with their start and end apart: 26, of which 5 were waited for; matrix products, arithmetic and copies ran while one was open for 0% of the time, Pallas kernels for 37%

profile of v2, /device:TPU:0, one launch (start us, length us, event | category | flops | bytes accessed | tf_op | source)
XLA Modules:
  0.0 84.4 jit_solution(11995597600009694458)
XLA Ops:
  0.6 3.1 %shard_map.132 = (f32[416,128]{1,0:T(8,128)S(1)}, f32[416,128]{1,0:T(8,128)S(1)}, f32[416,128]{1,0:T(8,128)S(1)}, f32[416,128]{1,0:T(8,128)S(1)}, f32[416,128]{1...) custom-call(s32[256]{0:T(256)} %slot_ref.5, s32[3,256]{1,0:T(4,128)} %bitcast.20, ...), custom_call_target="tpu_custom_call" | custom-call | flops 100000000 | bytes 856128 | tf_op jit(solution)/shard_map/pallas_call | solution.py:769
  3.8 0.5 collective-permute-start
  4.3 2.5 %collective-permute-start.1 = (f32[416,128]{1,0:T(8,128)S(1)}, f32[416,128]{1,0:T(8,128)S(1)}, u32[]{:S(2)}, u32[]{:S(2)}) collective-permute-start(f32[416,128]{1,0:T(8,128)S(1)} %get-tuple-element.53), channel_id=1, source_target_pairs={{0,8},{4,12},{8,16},{12,20},{16,24},{20,28},{24,0},{28,4},{1,9},{5... | collective-permute-start | bytes 638984 | tf_op jit(solution)/shard_map/ppermute | solution.py:845
  6.9 2.4 %collective-permute-start.2 = (f32[416,128]{1,0:T(8,128)S(1)}, f32[416,128]{1,0:T(8,128)S(1)}, u32[]{:S(2)}, u32[]{:S(2)}) collective-permute-start(f32[416,128]{1,0:T(8,128)S(1)} %get-tuple-element.54), channel_id=1, source_target_pairs={{0,12},{4,16},{8,20},{12,24},{16,28},{20,0},{24,4},{28,8},{1,13},{... | collective-permute-start | bytes 638984 | tf_op jit(solution)/shard_map/ppermute | solution.py:845
  9.2 0.5 collective-permute-start.3
  9.7 0.1 collective-permute-start.4
  9.8 2.3 %collective-permute-done.refs_1_ = f32[416,128]{1,0:T(8,128)S(1)} collective-permute-done((f32[416,128]{1,0:T(8,128)S(1)}, f32[416,128]{1,0:T(8,128)S(1)}, u32[]{:S(2)}, u32[]{:S(2)}) %collective-permute-start) | collective-permute-done | bytes 213024 | tf_op jit(solution)/shard_map/ppermute | solution.py:845
  12.2 2.5 %collective-permute-start.5 = (f32[416,128]{1,0:T(8,128)S(1)}, f32[416,128]{1,0:T(8,128)S(1)}, u32[]{:S(2)}, u32[]{:S(2)}) collective-permute-start(f32[416,128]{1,0:T(8,128)S(1)} %get-tuple-element.57), channel_id=1, source_target_pairs={{0,24},{4,28},{8,0},{12,4},{16,8},{20,12},{24,16},{28,20},{1,25},{... | collective-permute-start | bytes 638984 | tf_op jit(solution)/shard_map/ppermute | solution.py:845
  14.7 4.3 %collective-permute-start.6 = (f32[416,128]{1,0:T(8,128)S(1)}, f32[416,128]{1,0:T(8,128)S(1)}, u32[]{:S(2)}, u32[]{:S(2)}) collective-permute-start(f32[416,128]{1,0:T(8,128)S(1)} %get-tuple-element.58), channel_id=1, source_target_pairs={{0,28},{4,0},{8,4},{12,8},{16,12},{20,16},{24,20},{28,24},{1,29},{... | collective-permute-start | bytes 638984 | tf_op jit(solution)/shard_map/ppermute | solution.py:845
  18.9 7.1 %shard_map.131 = (f32[4096,128]{1,0:T(8,128)S(1)}, f32[4096,128]{1,0:T(8,128)S(1)}, f32[272,128]{1,0:T(8,128)S(1)}, f32[272,128]{1,0:T(8,128)S(1)}, f32[272,128]...) custom-call(f32[16]{0:T(128)} %k_ref.9, ...), custom_call_target="tpu_custom_call" | custom-call | flops 100000000 | bytes 3412032 | tf_op jit(solution)/shard_map/pallas_call | solution.py:769
  26.0 0.0 collective-permute-done.2.refs_3_
  26.0 0.0 collective-permute-done.3.refs_4_
  26.1 0.4 collective-permute-done.4.refs_5_
  26.5 0.0 collective-permute-done.5.refs_6_
  26.5 0.0 collective-permute-done.6.refs_7_
  26.5 0.2 copy-done.3
  26.7 0.1 copy-done.4
  26.8 0.4 copy-done.5
  27.2 0.1 copy-done.6
  27.3 0.1 copy-done.7
  27.3 5.5 %shard_map.133 = (f32[4096,128]{1,0:T(8,128)S(1)}, f32[4096,128]{1,0:T(8,128)S(1)}, f32[2560,128]{1,0:T(8,128)S(1)}, f32[272,128]{1,0:T(8,128)S(1)}, f32[272,128]{1,0:T(8,128)S(1)}, /*index=5*/f32[1664,128]{1,0:T(8,128)S(1)}) custom-call(f32[16]{0:T(128)} %k_ref.9, s32[48,128]{1,0:T(8,128)S(1)} %get-tuple-element.50.tab, ...), custom_call_target="tpu_custom_call" | custom-call | flops 100000000 | bytes 1728576 | tf_op jit(solution)/shard_map/pallas_call | solution.py:769
  32.9 0.8 collective-permute-start.11
  33.6 2.5 %collective-permute-start.12 = (f32[272,128]{1,0:T(8,128)S(1)}, f32[272,128]{1,0:T(8,128)S(1)}, u32[]{:S(2)}, u32[]{:S(2)}) collective-permute-start(f32[272,128]{1,0:T(8,128)S(1)} %get-tuple-element.76), channel_id=1, source_target_pairs={{0,28},{4,8},{8,4},{12,16},{16,12},{20,24},{24,20},{28,0},{1,29},{... | collective-permute-start | bytes 417800 | tf_op jit(solution)/shard_map/ppermute | solution.py:755
  36.1 0.0 collective-permute-start.7
  36.1 0.4 collective-permute-start.8
  36.6 1.6 %collective-permute-start.9 = (f32[272,128]{1,0:T(8,128)S(1)}, f32[272,128]{1,0:T(8,128)S(1)}, u32[]{:S(2)}, u32[]{:S(2)}) collective-permute-start(f32[272,128]{1,0:T(8,128)S(1)} %get-tuple-element.70), channel_id=1, source_target_pairs={{0,1},{1,0},{2,3},{3,2},{4,5},{5,4},{6,7},{7,6},{8,9},{9,8},{10,11... | collective-permute-start | bytes 417800 | tf_op jit(solution)/shard_map/ppermute | solution.py:755
  38.1 0.7 collective-permute-start.10
  38.8 4.9 %shard_map.134 = (f32[4096,128]{1,0:T(8,128)S(1)}, f32[4096,128]{1,0:T(8,128)S(1)}, f32[2560,128]{1,0:T(8,128)S(1)}) custom-call(f32[16]{0:T(128)} %k_ref.9, s32[48,128]{1,0:T(8,128)S(1)} %get-tuple-element.50.tab, f32[1664,128]{1,0:T(8,128)S(1)} %get-tuple-element.59.recv, ...), custom_call_target="tpu_custom_call", output_to_operand_aliasing={{0}: (3, {}), {1}: (4, {}), {2}: (5, {})} | custom-call | flops 100000000 | bytes 6381632 | tf_op jit(solution)/shard_map/pallas_call | solution.py:769
  43.7 5.4 %shard_map.136 = (f32[4096,128]{1,0:T(8,128)S(1)}, f32[4096,128]{1,0:T(8,128)S(1)}, f32[272,128]{1,0:T(8,128)S(1)}, f32[272,128]{1,0:T(8,128)S(1)}) custom-call(f32[16]{0:T(128)} %k_ref.9, s32[48,128]{1,0:T(8,128)S(1)} %get-tuple-element.50.tab, f32[4096,128]{1,0:T(8,128)S(1)} %get-tuple-element.74.moles, f32[4096,128]{1,0:T(8,128)S(1)} %get-tuple-element.63.mobile_f.mobile, ...), custom_call_target="tpu_custom_call" | custom-call | flops 100000000 | bytes 7905344 | tf_op jit(solution)/shard_map/pallas_call | solution.py:769
  49.2 0.1 collective-permute-start.17
  49.3 2.1 %collective-permute-start.18 = (f32[272,128]{1,0:T(8,128)S(1)}, f32[272,128]{1,0:T(8,128)S(1)}, u32[]{:S(2)}, u32[]{:S(2)}) collective-permute-start(f32[272,128]{1,0:T(8,128)S(1)} %get-tuple-element.85), channel_id=1, source_target_pairs={{0,28},{4,8},{8,4},{12,16},{16,12},{20,24},{24,20},{28,0},{1,29},{... | collective-permute-start | bytes 417800 | tf_op jit(solution)/shard_map/ppermute | solution.py:755
  51.4 4.0 %shard_map.135 = (f32[4096,128]{1,0:T(8,128)S(1)}, f32[4096,128]{1,0:T(8,128)S(1)}, f32[272,128]{1,0:T(8,128)S(1)}, f32[272,128]{1,0:T(8,128)S(1)}, f32[272,128]{1,0:T(8,128)S(1)}, /*index=5*/f32[272,128]{1,0:T(8,128)S(1)}) custom-call(f32[16]{0:T(128)} %k_ref.9, f32[4096,128]{1,0:T(8,128)S(1)} %get-tuple-element.48.moles, ...), custom_call_target="tpu_custom_call" | custom-call | flops 100000000 | bytes 9470016 | tf_op jit(solution)/shard_map/pallas_call | solution.py:769
  55.4 0.1 collective-permute-start.13
  55.5 0.9 %collective-permute-start.14 = (f32[272,128]{1,0:T(8,128)S(1)}, f32[272,128]{1,0:T(8,128)S(1)}, u32[]{:S(2)}, u32[]{:S(2)}) collective-permute-start(f32[272,128]{1,0:T(8,128)S(1)} %get-tuple-element.79), channel_id=1, source_target_pairs={{0,28},{4,8},{8,4},{12,16},{16,12},{20,24},{24,20},{28,0},{1,29},{... | collective-permute-start | bytes 417800 | tf_op jit(solution)/shard_map/ppermute | solution.py:755
  56.3 4.4 %collective-permute-start.15 = (f32[272,128]{1,0:T(8,128)S(1)}, f32[272,128]{1,0:T(8,128)S(1)}, u32[]{:S(2)}, u32[]{:S(2)}) collective-permute-start(f32[272,128]{1,0:T(8,128)S(1)} %get-tuple-element.80), channel_id=1, source_target_pairs={{0,1},{1,0},{2,3},{3,2},{4,5},{5,4},{6,7},{7,6},{8,9},{9,8},{10,11... | collective-permute-start | bytes 417800 | tf_op jit(solution)/shard_map/ppermute | solution.py:755
  60.7 0.7 collective-permute-start.16
  61.4 5.9 %shard_map.138 = (f32[256,128]{1,0:T(8,128)}, f32[256,128]{1,0:T(8,128)}, f32[256,128]{1,0:T(8,128)}, f32[256,128]{1,0:T(8,128)}, f32[256,128]{1,0:T(8,128)}, /*...) custom-call(s32[48,128]{1,0:T(8,128)S(1)} %get-tuple-element.50.tab, ...), custom_call_target="tpu_custom_call" | custom-call | flops 100000000 | bytes 7938048 | tf_op jit(solution)/shard_map/pallas_call | solution.py:769
  67.3 0.1 collective-permute-start.19
  67.4 1.6 %collective-permute-start.20 = (f32[256,128]{1,0:T(8,128)}, f32[256,128]{1,0:T(8,128)S(1)}, u32[]{:S(2)}, u32[]{:S(2)}) collective-permute-start(f32[256,128]{1,0:T(8,128)} %get-tuple-element.88), channel_id=1, source_target_pairs={{0,8},{4,12},{8,16},{12,20},{16,24},{20,28},{24,0},{28,4},{1,9},{5... | collective-permute-start | bytes 393224 | tf_op jit(solution)/shard_map/ppermute | solution.py:845
  69.0 1.7 %collective-permute-start.21 = (f32[256,128]{1,0:T(8,128)}, f32[256,128]{1,0:T(8,128)S(1)}, u32[]{:S(2)}, u32[]{:S(2)}) collective-permute-start(f32[256,128]{1,0:T(8,128)} %get-tuple-element.89), channel_id=1, source_target_pairs={{0,12},{4,16},{8,20},{12,24},{16,28},{20,0},{24,4},{28,8},{1,13},{... | collective-permute-start | bytes 393224 | tf_op jit(solution)/shard_map/ppermute | solution.py:845
  70.7 0.9 %collective-permute-start.22 = (f32[256,128]{1,0:T(8,128)}, f32[256,128]{1,0:T(8,128)S(1)}, u32[]{:S(2)}, u32[]{:S(2)}) collective-permute-start(f32[256,128]{1,0:T(8,128)} %get-tuple-element.90), channel_id=1, source_target_pairs={{0,16},{4,20},{8,24},{12,28},{16,0},{20,4},{24,8},{28,12},{1,17},{... | collective-permute-start | bytes 393224 | tf_op jit(solution)/shard_map/ppermute | solution.py:845
  71.6 2.1 %collective-permute-done.19.refs_1_ = f32[256,128]{1,0:T(8,128)S(1)} collective-permute-done((f32[256,128]{1,0:T(8,128)}, f32[256,128]{1,0:T(8,128)S(1)}, u32[]{:S(2)}, u32[]{:S(2)}) %collective-permute-start.19) | collective-permute-done | bytes 131104 | tf_op jit(solution)/shard_map/ppermute | solution.py:845
  73.7 0.8 collective-permute-start.24
  74.5 0.5 collective-permute-done.20.refs_2_
  75.0 2.0 %collective-permute-start.25 = (f32[256,128]{1,0:T(8,128)}, f32[256,128]{1,0:T(8,128)S(1)}, u32[]{:S(2)}, u32[]{:S(2)}) collective-permute-start(f32[256,128]{1,0:T(8,128)} %get-tuple-element.93), channel_id=1, source_target_pairs={{0,28},{4,0},{8,4},{12,8},{16,12},{20,16},{24,20},{28,24},{1,29},{... | collective-permute-start | bytes 393224 | tf_op jit(solution)/shard_map/ppermute | solution.py:845
  77.1 3.9 %shard_map.137 = f32[4096,128]{1,0:T(8,128)} custom-call(f32[4096,128]{1,0:T(8,128)S(1)} %get-tuple-element.72.moles, f32[4096,128]{1,0:T(8,128)S(1)} %get-tuple-element.73.mobile.mobile_m, f32[4096,128]{1,0:T(8,128)S(1)} %get-tuple-element.77.mobile_f.mobile, f32[2560,128]{1,0:T(8,128)S(1)} %get-tuple-element.64.coef, ...), custom_call_target="tpu_custom_call" | custom-call | flops 100000000 | bytes 9469952 | tf_op jit(solution)/shard_map/pallas_call | solution.py:769
  80.9 0.5 collective-permute-done.23.refs_5_
  81.5 3.0 %shard_map.139 = f32[128,1024]{1,0:T(8,128)} custom-call(s32[256]{0:T(256)} %slot_ref.5, s32[3,256]{1,0:T(4,128)} %bitcast.22, f32[256,128]{1,0:T(8,128)S(1)} %copy-done, f32[256,128]{1,0:T(8,128)S(1)} %collective-permute-done.19.refs_1_, f32[256,128]{1,0:T(8,128)S(1)} %collective-permute-done.20.refs_2_, f32[256,128]{1,0:T(8,128)S(1)} %collective-permute-done.21.refs_3_, ...), custom_call_target="tpu_custom_call" | custom-call | flops 100000000 | bytes 1052672 | tf_op jit(solution)/shard_map/pallas_call | solution.py:769
  (29 shorter events, 0.1 us)
Async XLA Ops:
  3.8 8.4 %collective-permute-start = (f32[416,128]{1,0:T(8,128)S(1)}, f32[416,128]{1,0:T(8,128)S(1)}, u32[]{:S(2)}, u32[]{:S(2)}) collective-permute-start(f32[416,128]{1,0:T(8,128)S(1)} %get-tuple-element.52), channel_id=1, source_target_pairs={{0,4},{4,8},{8,12},{12,16},{16,20},{20,24},{24,28},{28,0},{1,5},{5... | collective-permute-start | bytes 638984 | tf_op jit(solution)/shard_map/ppermute | solution.py:845
  4.3 10.3 %collective-permute-start.1 = (f32[416,128]{1,0:T(8,128)S(1)}, f32[416,128]{1,0:T(8,128)S(1)}, u32[]{:S(2)}, u32[]{:S(2)}) collective-permute-start(f32[416,128]{1,0:T(8,128)S(1)} %get-tuple-element.53), channel_id=1, source_target_pairs={{0,8},{4,12},{8,16},{12,20},{16,24},{20,28},{24,0},{28,4},{1,9},{5... | collective-permute-start | bytes 638984 | tf_op jit(solution)/shard_map/ppermute | solution.py:845
  6.9 19.2 %collective-permute-start.2 = (f32[416,128]{1,0:T(8,128)S(1)}, f32[416,128]{1,0:T(8,128)S(1)}, u32[]{:S(2)}, u32[]{:S(2)}) collective-permute-start(f32[416,128]{1,0:T(8,128)S(1)} %get-tuple-element.54), channel_id=1, source_target_pairs={{0,12},{4,16},{8,20},{12,24},{16,28},{20,0},{24,4},{28,8},{1,13},{... | collective-permute-start | bytes 638984 | tf_op jit(solution)/shard_map/ppermute | solution.py:845
  9.2 16.8 %collective-permute-start.3 = (f32[416,128]{1,0:T(8,128)S(1)}, f32[416,128]{1,0:T(8,128)S(1)}, u32[]{:S(2)}, u32[]{:S(2)}) collective-permute-start(f32[416,128]{1,0:T(8,128)S(1)} %get-tuple-element.55), channel_id=1, source_target_pairs={{0,16},{4,20},{8,24},{12,28},{16,0},{20,4},{24,8},{28,12},{1,17},{... | collective-permute-start | bytes 638984 | tf_op jit(solution)/shard_map/ppermute | solution.py:845
  9.7 16.8 %collective-permute-start.4 = (f32[416,128]{1,0:T(8,128)S(1)}, f32[416,128]{1,0:T(8,128)S(1)}, u32[]{:S(2)}, u32[]{:S(2)}) collective-permute-start(f32[416,128]{1,0:T(8,128)S(1)} %get-tuple-element.56), channel_id=1, source_target_pairs={{0,20},{4,24},{8,28},{12,0},{16,4},{20,8},{24,12},{28,16},{1,21},{... | collective-permute-start | bytes 638984 | tf_op jit(solution)/shard_map/ppermute | solution.py:845
  12.2 14.3 %copy-start.1 = (f32[416,128]{1,0:T(8,128)}, f32[416,128]{1,0:T(8,128)S(1)}, u32[]{:S(2)}) copy-start(f32[416,128]{1,0:T(8,128)S(1)} %collective-permute-done.refs_1_) | copy-start | bytes 638980
  12.2 14.3 %collective-permute-start.5 = (f32[416,128]{1,0:T(8,128)S(1)}, f32[416,128]{1,0:T(8,128)S(1)}, u32[]{:S(2)}, u32[]{:S(2)}) collective-permute-start(f32[416,128]{1,0:T(8,128)S(1)} %get-tuple-element.57), channel_id=1, source_target_pairs={{0,24},{4,28},{8,0},{12,4},{16,8},{20,12},{24,16},{28,20},{1,25},{... | collective-permute-start | bytes 638984 | tf_op jit(solution)/shard_map/ppermute | solution.py:845
  14.7 11.9 %copy-start.2 = (f32[416,128]{1,0:T(8,128)}, f32[416,128]{1,0:T(8,128)S(1)}, u32[]{:S(2)}) copy-start(f32[416,128]{1,0:T(8,128)S(1)} %collective-permute-done.1.refs_2_) | copy-start | bytes 638980
  14.7 11.8 %collective-permute-start.6 = (f32[416,128]{1,0:T(8,128)S(1)}, f32[416,128]{1,0:T(8,128)S(1)}, u32[]{:S(2)}, u32[]{:S(2)}) collective-permute-start(f32[416,128]{1,0:T(8,128)S(1)} %get-tuple-element.58), channel_id=1, source_target_pairs={{0,28},{4,0},{8,4},{12,8},{16,12},{20,16},{24,20},{28,24},{1,29},{... | collective-permute-start | bytes 638984 | tf_op jit(solution)/shard_map/ppermute | solution.py:845
  26.0 0.7 copy-start.3
  26.1 0.7 copy-start.4
  26.5 0.7 copy-start.5
  26.5 0.8 copy-start.6
  26.5 0.8 copy-start.7
  32.9 5.3 %collective-permute-start.11 = (f32[272,128]{1,0:T(8,128)S(1)}, f32[272,128]{1,0:T(8,128)S(1)}, u32[]{:S(2)}, u32[]{:S(2)}) collective-permute-start(f32[272,128]{1,0:T(8,128)S(1)} %get-tuple-element.75), channel_id=1, source_target_pairs={{0,4},{4,0},{8,12},{12,8},{16,20},{20,16},{24,28},{28,24},{1,5},{5... | collective-permute-start | bytes 417800 | tf_op jit(solution)/shard_map/ppermute | solution.py:755
  33.6 10.1 %collective-permute-start.12 = (f32[272,128]{1,0:T(8,128)S(1)}, f32[272,128]{1,0:T(8,128)S(1)}, u32[]{:S(2)}, u32[]{:S(2)}) collective-permute-start(f32[272,128]{1,0:T(8,128)S(1)} %get-tuple-element.76), channel_id=1, source_target_pairs={{0,28},{4,8},{8,4},{12,16},{16,12},{20,24},{24,20},{28,0},{1,29},{... | collective-permute-start | bytes 417800 | tf_op jit(solution)/shard_map/ppermute | solution.py:755
  36.1 13.2 %collective-permute-start.7 = (f32[272,128]{1,0:T(8,128)S(1)}, f32[272,128]{1,0:T(8,128)S(1)}, u32[]{:S(2)}, u32[]{:S(2)}) collective-permute-start(f32[272,128]{1,0:T(8,128)S(1)} %get-tuple-element.68), channel_id=1, source_target_pairs={{0,4},{4,0},{8,12},{12,8},{16,20},{20,16},{24,28},{28,24},{1,5},{5... | collective-permute-start | bytes 417800 | tf_op jit(solution)/shard_map/ppermute | solution.py:755
  36.1 15.2 %collective-permute-start.8 = (f32[272,128]{1,0:T(8,128)S(1)}, f32[272,128]{1,0:T(8,128)S(1)}, u32[]{:S(2)}, u32[]{:S(2)}) collective-permute-start(f32[272,128]{1,0:T(8,128)S(1)} %get-tuple-element.69), channel_id=1, source_target_pairs={{0,28},{4,8},{8,4},{12,16},{16,12},{20,24},{24,20},{28,0},{1,29},{... | collective-permute-start | bytes 417800 | tf_op jit(solution)/shard_map/ppermute | solution.py:755
  36.6 14.8 %collective-permute-start.9 = (f32[272,128]{1,0:T(8,128)S(1)}, f32[272,128]{1,0:T(8,128)S(1)}, u32[]{:S(2)}, u32[]{:S(2)}) collective-permute-start(f32[272,128]{1,0:T(8,128)S(1)} %get-tuple-element.70), channel_id=1, source_target_pairs={{0,1},{1,0},{2,3},{3,2},{4,5},{5,4},{6,7},{7,6},{8,9},{9,8},{10,11... | collective-permute-start | bytes 417800 | tf_op jit(solution)/shard_map/ppermute | solution.py:755
  38.1 13.2 %collective-permute-start.10 = (f32[272,128]{1,0:T(8,128)S(1)}, f32[272,128]{1,0:T(8,128)S(1)}, u32[]{:S(2)}, u32[]{:S(2)}) collective-permute-start(f32[272,128]{1,0:T(8,128)S(1)} %get-tuple-element.71), channel_id=1, source_target_pairs={{1,2},{2,1},{5,6},{6,5},{9,10},{10,9},{13,14},{14,13},{17,18},{18,... | collective-permute-start | bytes 417800 | tf_op jit(solution)/shard_map/ppermute | solution.py:755
  49.2 11.5 %collective-permute-start.17 = (f32[272,128]{1,0:T(8,128)S(1)}, f32[272,128]{1,0:T(8,128)S(1)}, u32[]{:S(2)}, u32[]{:S(2)}) collective-permute-start(f32[272,128]{1,0:T(8,128)S(1)} %get-tuple-element.84), channel_id=1, source_target_pairs={{0,4},{4,0},{8,12},{12,8},{16,20},{20,16},{24,28},{28,24},{1,5},{5... | collective-permute-start | bytes 417800 | tf_op jit(solution)/shard_map/ppermute | solution.py:755
  49.3 12.1 %collective-permute-start.18 = (f32[272,128]{1,0:T(8,128)S(1)}, f32[272,128]{1,0:T(8,128)S(1)}, u32[]{:S(2)}, u32[]{:S(2)}) collective-permute-start(f32[272,128]{1,0:T(8,128)S(1)} %get-tuple-element.85), channel_id=1, source_target_pairs={{0,28},{4,8},{8,4},{12,16},{16,12},{20,24},{24,20},{28,0},{1,29},{... | collective-permute-start | bytes 417800 | tf_op jit(solution)/shard_map/ppermute | solution.py:755
  55.4 12.0 %collective-permute-start.13 = (f32[272,128]{1,0:T(8,128)S(1)}, f32[272,128]{1,0:T(8,128)S(1)}, u32[]{:S(2)}, u32[]{:S(2)}) collective-permute-start(f32[272,128]{1,0:T(8,128)S(1)} %get-tuple-element.78), channel_id=1, source_target_pairs={{0,4},{4,0},{8,12},{12,8},{16,20},{20,16},{24,28},{28,24},{1,5},{5... | collective-permute-start | bytes 417800 | tf_op jit(solution)/shard_map/ppermute | solution.py:755
  55.5 13.6 %collective-permute-start.14 = (f32[272,128]{1,0:T(8,128)S(1)}, f32[272,128]{1,0:T(8,128)S(1)}, u32[]{:S(2)}, u32[]{:S(2)}) collective-permute-start(f32[272,128]{1,0:T(8,128)S(1)} %get-tuple-element.79), channel_id=1, source_target_pairs={{0,28},{4,8},{8,4},{12,16},{16,12},{20,24},{24,20},{28,0},{1,29},{... | collective-permute-start | bytes 417800 | tf_op jit(solution)/shard_map/ppermute | solution.py:755
  56.3 14.4 %collective-permute-start.15 = (f32[272,128]{1,0:T(8,128)S(1)}, f32[272,128]{1,0:T(8,128)S(1)}, u32[]{:S(2)}, u32[]{:S(2)}) collective-permute-start(f32[272,128]{1,0:T(8,128)S(1)} %get-tuple-element.80), channel_id=1, source_target_pairs={{0,1},{1,0},{2,3},{3,2},{4,5},{5,4},{6,7},{7,6},{8,9},{9,8},{10,11... | collective-permute-start | bytes 417800 | tf_op jit(solution)/shard_map/ppermute | solution.py:755
  60.7 10.9 %collective-permute-start.16 = (f32[272,128]{1,0:T(8,128)S(1)}, f32[272,128]{1,0:T(8,128)S(1)}, u32[]{:S(2)}, u32[]{:S(2)}) collective-permute-start(f32[272,128]{1,0:T(8,128)S(1)} %get-tuple-element.81), channel_id=1, source_target_pairs={{1,2},{2,1},{5,6},{6,5},{9,10},{10,9},{13,14},{14,13},{17,18},{18,... | collective-permute-start | bytes 417800 | tf_op jit(solution)/shard_map/ppermute | solution.py:755
  67.3 6.4 %collective-permute-start.19 = (f32[256,128]{1,0:T(8,128)}, f32[256,128]{1,0:T(8,128)S(1)}, u32[]{:S(2)}, u32[]{:S(2)}) collective-permute-start(f32[256,128]{1,0:T(8,128)} %get-tuple-element.87), channel_id=1, source_target_pairs={{0,4},{4,8},{8,12},{12,16},{16,20},{20,24},{24,28},{28,0},{1,5},{5... | collective-permute-start | bytes 393224 | tf_op jit(solution)/shard_map/ppermute | solution.py:845
  67.4 7.6 %collective-permute-start.20 = (f32[256,128]{1,0:T(8,128)}, f32[256,128]{1,0:T(8,128)S(1)}, u32[]{:S(2)}, u32[]{:S(2)}) collective-permute-start(f32[256,128]{1,0:T(8,128)} %get-tuple-element.88), channel_id=1, source_target_pairs={{0,8},{4,12},{8,16},{12,20},{16,24},{20,28},{24,0},{28,4},{1,9},{5... | collective-permute-start | bytes 393224 | tf_op jit(solution)/shard_map/ppermute | solution.py:845
  69.0 11.9 %collective-permute-start.21 = (f32[256,128]{1,0:T(8,128)}, f32[256,128]{1,0:T(8,128)S(1)}, u32[]{:S(2)}, u32[]{:S(2)}) collective-permute-start(f32[256,128]{1,0:T(8,128)} %get-tuple-element.89), channel_id=1, source_target_pairs={{0,12},{4,16},{8,20},{12,24},{16,28},{20,0},{24,4},{28,8},{1,13},{... | collective-permute-start | bytes 393224 | tf_op jit(solution)/shard_map/ppermute | solution.py:845
  70.7 10.2 %collective-permute-start.22 = (f32[256,128]{1,0:T(8,128)}, f32[256,128]{1,0:T(8,128)S(1)}, u32[]{:S(2)}, u32[]{:S(2)}) collective-permute-start(f32[256,128]{1,0:T(8,128)} %get-tuple-element.90), channel_id=1, source_target_pairs={{0,16},{4,20},{8,24},{12,28},{16,0},{20,4},{24,8},{28,12},{1,17},{... | collective-permute-start | bytes 393224 | tf_op jit(solution)/shard_map/ppermute | solution.py:845
  71.6 9.9 %collective-permute-start.23 = (f32[256,128]{1,0:T(8,128)}, f32[256,128]{1,0:T(8,128)S(1)}, u32[]{:S(2)}, u32[]{:S(2)}) collective-permute-start(f32[256,128]{1,0:T(8,128)} %get-tuple-element.91), channel_id=1, source_target_pairs={{0,20},{4,24},{8,28},{12,0},{16,4},{20,8},{24,12},{28,16},{1,21},{... | collective-permute-start | bytes 393224 | tf_op jit(solution)/shard_map/ppermute | solution.py:845
  73.7 7.7 %collective-permute-start.24 = (f32[256,128]{1,0:T(8,128)}, f32[256,128]{1,0:T(8,128)S(1)}, u32[]{:S(2)}, u32[]{:S(2)}) collective-permute-start(f32[256,128]{1,0:T(8,128)} %get-tuple-element.92), channel_id=1, source_target_pairs={{0,24},{4,28},{8,0},{12,4},{16,8},{20,12},{24,16},{28,20},{1,25},{... | collective-permute-start | bytes 393224 | tf_op jit(solution)/shard_map/ppermute | solution.py:845
  75.0 6.4 %collective-permute-start.25 = (f32[256,128]{1,0:T(8,128)}, f32[256,128]{1,0:T(8,128)S(1)}, u32[]{:S(2)}, u32[]{:S(2)}) collective-permute-start(f32[256,128]{1,0:T(8,128)} %get-tuple-element.93), channel_id=1, source_target_pairs={{0,28},{4,0},{8,4},{12,8},{16,12},{20,16},{24,20},{28,24},{1,29},{... | collective-permute-start | bytes 393224 | tf_op jit(solution)/shard_map/ppermute | solution.py:845
  77.1 4.4 %copy-start = (f32[256,128]{1,0:T(8,128)S(1)}, f32[256,128]{1,0:T(8,128)}, u32[]{:S(2)}) copy-start(f32[256,128]{1,0:T(8,128)} %get-tuple-element.86.refs_0_) | copy-start | bytes 393220

commit v3 on v2

--- a/solution.py
+++ b/solution.py
@@ -15,7 +15,7 @@
 LANES = 128
 SUB = 8
 PARTS = 4
-FLASH_PLANES = 2
+FLASH_PLANES = 4
 F32 = jnp.float32
 I32 = jnp.int32
 
@@ -215,24 +215,26 @@
         column = jnp.where(sub == i, p0, column)
 
     own_slots(z, slot_ref, block_ref, visit)
-    for s in range(z.wide):
-        source = sender(z, s)
-        left = lax.rem(source, 2) * z.half
-        hit = column == lax.div(source, 2)
-
-        def tile(m, carry, s=s, left=left, hit=hit):
+    hits = [column == lax.div(sender(z, s), 2) for s in range(z.wide)]
+
+    def tile(m, carry):
+        for parity in range(2):
+            group = range(parity, z.wide, 2)
+            left = lax.rem(lax.axis_index("wide") + parity, 2) * z.half
             for j in range(z.jt):
-                row = (j * z.tiles_back + m) * SUB
-                part = chunks[s][pl.ds(pl.multiple_of(row, SUB), SUB), :]
+                rows = pl.ds(pl.multiple_of((j * z.tiles_back + m) * SUB, SUB), SUB)
+                parts = [chunks[s][rows, :] for s in group]
                 lanes = pl.ds(pl.multiple_of(left + j * LANES, LANES), LANES)
                 for cp in range(z.cpt):
-                    rows = pl.ds(pl.multiple_of((m * z.cpt + cp) * SUB, SUB), SUB)
-                    out[rows, lanes] = jnp.where(
-                        hit, sub_gather(part, cp * z.most + ranks), out[rows, lanes]
-                    )
-            return carry
-
-        lax.fori_loop(0, z.tiles_back, tile, 0, unroll=2)
+                    v = None
+                    for s, part in zip(group, parts):
+                        got = sub_gather(part, cp * z.most + ranks)
+                        v = got if v is None else jnp.where(hits[s], got, v)
+                    row = (m * z.cpt + cp) * SUB
+                    out[pl.ds(pl.multiple_of(row, SUB), SUB), lanes] = v
+        return carry
+
+    lax.fori_loop(0, z.tiles_back, tile, 0)
 
 
 def tables(z, slot_ref, block_ref, tab, gather):
@@ -372,9 +374,10 @@
         deep_b[rows, :] = g - out
 
 
-def flash_field(z, moles, mobile, k_ref, low=0, high=None, hop=1, arrived=None):
+def flash_field(z, moles, mobile, k_ref, low=0, high=None, hop=1, arrived=None,
+                planes=FLASH_PLANES):
     inverse, first = k_scalars(k_ref, z.nc)
-    step = FLASH_PLANES
+    step = planes
     high = z.x // step if high is None else high
 
     def block(n, carry):
@@ -498,7 +501,7 @@
 
     unroll = max(1, 8 // len(js))
     lax.fori_loop(0, z.nc, amount, 0, unroll=unroll)
-    lax.fori_loop(0, z.coefs, weight, 0, unroll=2)
+    lax.fori_loop(0, z.coefs, weight, 0, unroll=5)
 
 
 def frac_edge_kernel(z, k_ref, tab, *refs):
@@ -514,8 +517,8 @@
     for read in later:
         read.start()
     unpack_rows(z, tab, recv, edge, moles, coef)
-    last = z.x // FLASH_PLANES
-    flash_field(z, moles, mobile, k_ref, 0, last, last - 1)
+    last = z.x // 2
+    flash_field(z, moles, mobile, k_ref, 0, last, last - 1, planes=2)
     frac_messages(z, mobile, coef, tab, 0, frac_a, frac_b)
     for read in later:
         read.wait()
@@ -523,7 +526,7 @@
 
 def frac_inner_kernel(z, k_ref, tab, recv, moles_in, mobile_in, coef_in, moles, mobile, coef):
     unpack_rows(z, tab, recv, tuple(range(1, z.jt - 1)), moles, coef)
-    flash_field(z, moles, mobile, k_ref, 1, z.x // FLASH_PLANES - 1)
+    flash_field(z, moles, mobile, k_ref, 1, z.x // 2 - 1, planes=2)
 
 
 def each_plane(z, at):
@@ -537,18 +540,16 @@
 
 
 def matrix_update(z, t, moles, mobile, rate, upwind, pore, halos, new, mobile_f=None, coef=None):
-    wide_a, wide_b, deep_a, deep_b = halos or (None,) * 4
+    wide_a, wide_b = halos or (None, None)
     nc = z.nc
     even_w = lax.rem(lax.axis_index("wide"), 2) == 0
-    even_d = lax.rem(lax.axis_index("depth"), 2) == 0
     sub = iota((z.z, LANES), 0)
 
     def side(a, b, first, row, count):
         rows = pl.ds(row, count)
-        even = even_w if a is wide_a else even_d
         if first:
-            return jnp.where(even, b[rows, :], a[rows, :])
-        return jnp.where(even, a[rows, :], b[rows, :])
+            return jnp.where(even_w, b[rows, :], a[rows, :])
+        return jnp.where(even_w, a[rows, :], b[rows, :])
 
     def at(x, low, high):
         inv = 1.0 / plane(z, pore, 0, x)
@@ -559,15 +560,9 @@
             pox, pix = (1.0, side(wide_a, wide_b, True, nc * z.z, z.z)) if halos else (0.0, 0.0)
         else:
             pox, pix = face(z, rate, upwind, t, 0, x - 1)
-        if halos:
-            wz = jnp.broadcast_to(side(deep_a, deep_b, True, nc * z.x + x, 1), (z.z, LANES))
-            poz = jnp.where(sub == 0, 1.0, pltpu.roll(oz, 1, 0))
-            piz = jnp.where(sub == 0, wz, pltpu.roll(iz, 1, 0))
-            niz = iz
-        else:
-            poz = jnp.where(sub == 0, 0.0, pltpu.roll(oz, 1, 0))
-            piz = jnp.where(sub == 0, 0.0, pltpu.roll(iz, 1, 0))
-            niz = jnp.where(sub == z.z - 1, 0.0, iz)
+        poz = jnp.where(sub == 0, 0.0, pltpu.roll(oz, 1, 0))
+        piz = jnp.where(sub == 0, 0.0, pltpu.roll(iz, 1, 0))
+        niz = jnp.where(sub == z.z - 1, 0.0, iz)
         poy, piy = lane_roll(oy, 1), lane_roll(iy, 1)
         own = ox + pix + oz + piz + oy + piy
         if coef is not None:
@@ -590,11 +585,6 @@
             elif halos:
                 v = v + ax * side(wide_a, wide_b, False, c * z.z, z.z)
             zb, za = pltpu.roll(g, 1, 0), pltpu.roll(g, z.z - 1, 0)
-            if halos:
-                hz0 = jnp.broadcast_to(side(deep_a, deep_b, True, c * z.x + x, 1), (z.z, LANES))
-                hz1 = jnp.broadcast_to(side(deep_a, deep_b, False, c * z.x + x, 1), (z.z, LANES))
-                zb = jnp.where(sub == 0, hz0, zb)
-                za = jnp.where(sub == z.z - 1, hz1, za)
             v = v + (az * za + bz * zb)
             v = v + (ay * lane_roll(g, -1) + by * lane_roll(g, 1))
             if coef is not None:
@@ -659,11 +649,41 @@
 
 
 def last_matrix_kernel(
-    z, t, moles, mobile, mobile_f, coef, rate, upwind, pore, ha, hb, hc, hd, new
+    z, t, moles, mobile, mobile_f, coef, rate, upwind, pore, ha, hb, new
 ):
-    matrix_update(
-        z, t, moles, mobile, rate, upwind, pore, (ha, hb, hc, hd), new, mobile_f, coef
-    )
+    matrix_update(z, t, moles, mobile, rate, upwind, pore, (ha, hb), new, mobile_f, coef)
+
+
+def depth_kernel(z, t, before, mobile, rate, upwind, pore, hc, hd, new, result, sem):
+    even = lax.rem(lax.axis_index("depth"), 2) == 0
+    inner = lax.axis_index("depth") < z.depth - 1
+
+    def layer(ref, base, h, at):
+        return ref[pl.ds(base + h * SUB * z.z + at, SUB, stride=z.z), :]
+
+    def side(first, row):
+        rows = pl.ds(row, SUB)
+        if first:
+            return jnp.where(even, hd[rows, :], hc[rows, :])
+        return jnp.where(even, hc[rows, :], hd[rows, :])
+
+    for h in range(z.x // SUB):
+        face_at = z.z - 1
+        g = jnp.where(inner, layer(rate, z.cells, h, face_at), 0.0)
+        u = layer(upwind, (t * 3 + 1) * z.cells, h, face_at).astype(F32)
+        into = (g - g * u) / layer(pore, 0, h, face_at)
+        inv = 1.0 / layer(pore, 0, h, 0)
+        back = side(True, z.nc * z.x + h * SUB)
+        for c in range(z.nc):
+            base = c * z.cells
+            first = pl.ds(base + h * SUB * z.z, SUB, stride=z.z)
+            last = pl.ds(base + h * SUB * z.z + face_at, SUB, stride=z.z)
+            row = c * z.x + h * SUB
+            new[first, :] = new[first, :] + inv * (side(True, row) - back * mobile[first, :])
+            new[last, :] = new[last, :] + into * side(False, row)
+    copy = pltpu.make_async_copy(new, result, sem)
+    copy.start()
+    copy.wait()
 
 
 def frac_update(z, t, tab, moles, mobile, mobile_m, coef, frac_a, frac_b, new):
@@ -919,9 +939,16 @@
     )
     returned = trade(back)
     moles = call(
-        bind(last_matrix_kernel, t), [VMEM] * 11,
-        jax.ShapeDtypeStruct((z.nc * z.cells, LANES), F32),
-        in_vmem(moles, mobile_m, new_mobile_f, coef, rate, upwind, pore, *wide_halos, *deep_halos),
+        bind(last_matrix_kernel, t), [VMEM] * 9, field,
+        in_vmem(moles, mobile_m, new_mobile_f, coef, rate, upwind, pore, *wide_halos),
+    )
+    _, moles = call(
+        bind(depth_kernel, t), [VMEM] * 7,
+        (field, shape(z.nc * z.cells, space=pltpu.HBM)),
+        in_vmem(moles, mobile_m, rate, upwind, pore, *deep_halos),
+        scratch=[pltpu.SemaphoreType.DMA],
+        out_specs=(VMEM, HBM),
+        aliases={0: 0},
     )
     frac = call(
         bind(spread_kernel), [SMEM] * 2 + [VMEM] * z.wide,

time: 85.4 us -> 82.9 us (0.971)
  Pallas kernels: 42.8 us -> 40.2 us
    pallas_call x9 -> x10, Pallas kernels: 42.8 us -> 40.2 us  [call(): pl.pallas_call(body, out_shape=out_shape, in_specs=in_specs, out_specs=ou...]
where the time goes in v3:
time: 82.9 us; the launch traced here: 82 us
  Pallas kernels  40.2 us (48%)
  starting transfers between devices  34 us (41%)
  waiting for transfers between devices  6.04 us (7%)
  between operations  0.88 us (1%)
  local copies, waits for them, and re-layouts  0.84 us (1%)
    pallas_call x10, Pallas kernels, call(): pl.pallas_call(body, out_shape=out_shape, in_specs=in_specs, out_specs=ou...  40.2 us
    ppermute x14, starting transfers between devices, trade(): got.append(lax.ppermute(chunks[s], 'wide', pairs))  19.9 us
    ppermute x12, starting transfers between devices, swap(): return lax.ppermute(value, axis, pairs)  14.1 us
    ppermute x14, waiting for transfers between devices, trade(): got.append(lax.ppermute(chunks[s], 'wide', pairs))  6.01 us
  transfers between devices with their start and end apart: 26, of which 5 were waited for; matrix products, arithmetic and copies ran while one was open for 0% of the time, Pallas kernels for 37%

profile of v3, /device:TPU:0, one launch (start us, length us, event | category | flops | bytes accessed | tf_op | source)
XLA Modules:
  0.0 82.0 jit_solution(122377847762344980)
XLA Ops:
  0.6 3.1 %shard_map.132 = (f32[416,128]{1,0:T(8,128)S(1)}, f32[416,128]{1,0:T(8,128)S(1)}, f32[416,128]{1,0:T(8,128)S(1)}, f32[416,128]{1,0:T(8,128)S(1)}, f32[416,128]{1...) custom-call(s32[256]{0:T(256)} %slot_ref.5, s32[3,256]{1,0:T(4,128)} %bitcast.19, ...), custom_call_target="tpu_custom_call" | custom-call | flops 100000000 | bytes 856128 | tf_op jit(solution)/shard_map/pallas_call | solution.py:789
  3.8 0.5 collective-permute-start
  4.3 2.5 %collective-permute-start.1 = (f32[416,128]{1,0:T(8,128)S(1)}, f32[416,128]{1,0:T(8,128)S(1)}, u32[]{:S(2)}, u32[]{:S(2)}) collective-permute-start(f32[416,128]{1,0:T(8,128)S(1)} %get-tuple-element.54), channel_id=1, source_target_pairs={{0,8},{4,12},{8,16},{12,20},{16,24},{20,28},{24,0},{28,4},{1,9},{5... | collective-permute-start | bytes 638984 | tf_op jit(solution)/shard_map/ppermute | solution.py:865
  6.9 2.4 %collective-permute-start.2 = (f32[416,128]{1,0:T(8,128)S(1)}, f32[416,128]{1,0:T(8,128)S(1)}, u32[]{:S(2)}, u32[]{:S(2)}) collective-permute-start(f32[416,128]{1,0:T(8,128)S(1)} %get-tuple-element.55), channel_id=1, source_target_pairs={{0,12},{4,16},{8,20},{12,24},{16,28},{20,0},{24,4},{28,8},{1,13},{... | collective-permute-start | bytes 638984 | tf_op jit(solution)/shard_map/ppermute | solution.py:865
  9.2 0.5 collective-permute-start.3
  9.7 0.1 collective-permute-start.4
  9.8 2.3 %collective-permute-done.refs_1_ = f32[416,128]{1,0:T(8,128)S(1)} collective-permute-done((f32[416,128]{1,0:T(8,128)S(1)}, f32[416,128]{1,0:T(8,128)S(1)}, u32[]{:S(2)}, u32[]{:S(2)}) %collective-permute-start) | collective-permute-done | bytes 213024 | tf_op jit(solution)/shard_map/ppermute | solution.py:865
  12.2 2.5 %collective-permute-start.5 = (f32[416,128]{1,0:T(8,128)S(1)}, f32[416,128]{1,0:T(8,128)S(1)}, u32[]{:S(2)}, u32[]{:S(2)}) collective-permute-start(f32[416,128]{1,0:T(8,128)S(1)} %get-tuple-element.58), channel_id=1, source_target_pairs={{0,24},{4,28},{8,0},{12,4},{16,8},{20,12},{24,16},{28,20},{1,25},{... | collective-permute-start | bytes 638984 | tf_op jit(solution)/shard_map/ppermute | solution.py:865
  14.7 4.3 %collective-permute-start.6 = (f32[416,128]{1,0:T(8,128)S(1)}, f32[416,128]{1,0:T(8,128)S(1)}, u32[]{:S(2)}, u32[]{:S(2)}) collective-permute-start(f32[416,128]{1,0:T(8,128)S(1)} %get-tuple-element.59), channel_id=1, source_target_pairs={{0,28},{4,0},{8,4},{12,8},{16,12},{20,16},{24,20},{28,24},{1,29},{... | collective-permute-start | bytes 638984 | tf_op jit(solution)/shard_map/ppermute | solution.py:865
  18.9 6.9 %shard_map.131 = (f32[4096,128]{1,0:T(8,128)S(1)}, f32[4096,128]{1,0:T(8,128)S(1)}, f32[272,128]{1,0:T(8,128)S(1)}, f32[272,128]{1,0:T(8,128)S(1)}, f32[272,128]...) custom-call(f32[16]{0:T(128)} %k_ref.9, ...), custom_call_target="tpu_custom_call" | custom-call | flops 100000000 | bytes 3412032 | tf_op jit(solution)/shard_map/pallas_call | solution.py:789
  25.8 0.0 collective-permute-done.2.refs_3_
  25.9 0.6 collective-permute-done.4.refs_5_
  26.5 0.0 collective-permute-done.5.refs_6_
  26.5 0.0 collective-permute-done.6.refs_7_
  26.5 0.1 copy-done.4
  26.6 0.6 copy-done.5
  27.2 0.1 copy-done.6
  27.3 0.1 copy-done.7
  27.4 5.0 %shard_map.133 = (f32[4096,128]{1,0:T(8,128)S(1)}, f32[4096,128]{1,0:T(8,128)S(1)}, f32[2560,128]{1,0:T(8,128)S(1)}, f32[272,128]{1,0:T(8,128)S(1)}, f32[272,128]{1,0:T(8,128)S(1)}, /*index=5*/f32[1664,128]{1,0:T(8,128)S(1)}) custom-call(f32[16]{0:T(128)} %k_ref.9, s32[48,128]{1,0:T(8,128)S(1)} %get-tuple-element.51.tab, ...), custom_call_target="tpu_custom_call" | custom-call | flops 100000000 | bytes 1728576 | tf_op jit(solution)/shard_map/pallas_call | solution.py:789
  32.4 0.8 collective-permute-start.11
  33.1 2.5 %collective-permute-start.12 = (f32[272,128]{1,0:T(8,128)S(1)}, f32[272,128]{1,0:T(8,128)S(1)}, u32[]{:S(2)}, u32[]{:S(2)}) collective-permute-start(f32[272,128]{1,0:T(8,128)S(1)} %get-tuple-element.77), channel_id=1, source_target_pairs={{0,28},{4,8},{8,4},{12,16},{16,12},{20,24},{24,20},{28,0},{1,29},{... | collective-permute-start | bytes 417800 | tf_op jit(solution)/shard_map/ppermute | solution.py:775
  35.6 0.4 collective-permute-start.8
  36.1 1.6 %collective-permute-start.9 = (f32[272,128]{1,0:T(8,128)S(1)}, f32[272,128]{1,0:T(8,128)S(1)}, u32[]{:S(2)}, u32[]{:S(2)}) collective-permute-start(f32[272,128]{1,0:T(8,128)S(1)} %get-tuple-element.71), channel_id=1, source_target_pairs={{0,1},{1,0},{2,3},{3,2},{4,5},{5,4},{6,7},{7,6},{8,9},{9,8},{10,11... | collective-permute-start | bytes 417800 | tf_op jit(solution)/shard_map/ppermute | solution.py:775
  37.6 0.0 collective-permute-done.11.fa
  37.6 0.7 collective-permute-start.10
  38.3 4.4 %shard_map.134 = (f32[4096,128]{1,0:T(8,128)S(1)}, f32[4096,128]{1,0:T(8,128)S(1)}, f32[2560,128]{1,0:T(8,128)S(1)}) custom-call(f32[16]{0:T(128)} %k_ref.9, s32[48,128]{1,0:T(8,128)S(1)} %get-tuple-element.51.tab, f32[1664,128]{1,0:T(8,128)S(1)} %get-tuple-element.60.recv, ...), custom_call_target="tpu_custom_call", output_to_operand_aliasing={{0}: (3, {}), {1}: (4, {}), {2}: (5, {})} | custom-call | flops 100000000 | bytes 6381632 | tf_op jit(solution)/shard_map/pallas_call | solution.py:789
  42.7 5.3 %shard_map.136 = (f32[4096,128]{1,0:T(8,128)S(1)}, f32[4096,128]{1,0:T(8,128)S(1)}, f32[272,128]{1,0:T(8,128)S(1)}, f32[272,128]{1,0:T(8,128)S(1)}) custom-call(f32[16]{0:T(128)} %k_ref.9, s32[48,128]{1,0:T(8,128)S(1)} %get-tuple-element.51.tab, f32[4096,128]{1,0:T(8,128)S(1)} %get-tuple-element.75.moles, f32[4096,128]{1,0:T(8,128)S(1)} %get-tuple-element.64.mobile_f.mobile, ...), custom_call_target="tpu_custom_call" | custom-call | flops 100000000 | bytes 7905344 | tf_op jit(solution)/shard_map/pallas_call | solution.py:789
  48.1 0.1 collective-permute-start.17
  48.2 2.1 %collective-permute-start.18 = (f32[272,128]{1,0:T(8,128)S(1)}, f32[272,128]{1,0:T(8,128)S(1)}, u32[]{:S(2)}, u32[]{:S(2)}) collective-permute-start(f32[272,128]{1,0:T(8,128)S(1)} %get-tuple-element.87), channel_id=1, source_target_pairs={{0,28},{4,8},{8,4},{12,16},{16,12},{20,24},{24,20},{28,0},{1,29},{... | collective-permute-start | bytes 417800 | tf_op jit(solution)/shard_map/ppermute | solution.py:775
  50.3 3.8 %shard_map.135 = (f32[4096,128]{1,0:T(8,128)S(1)}, f32[4096,128]{1,0:T(8,128)S(1)}, f32[272,128]{1,0:T(8,128)S(1)}, f32[272,128]{1,0:T(8,128)S(1)}, f32[272,128]{1,0:T(8,128)S(1)}, /*index=5*/f32[272,128]{1,0:T(8,128)S(1)}) custom-call(f32[16]{0:T(128)} %k_ref.9, f32[4096,128]{1,0:T(8,128)S(1)} %get-tuple-element.49.moles, ...), custom_call_target="tpu_custom_call" | custom-call | flops 100000000 | bytes 9470016 | tf_op jit(solution)/shard_map/pallas_call | solution.py:789
  54.1 0.1 collective-permute-start.13
  54.2 0.9 %collective-permute-start.14 = (f32[272,128]{1,0:T(8,128)S(1)}, f32[272,128]{1,0:T(8,128)S(1)}, u32[]{:S(2)}, u32[]{:S(2)}) collective-permute-start(f32[272,128]{1,0:T(8,128)S(1)} %get-tuple-element.80), channel_id=1, source_target_pairs={{0,28},{4,8},{8,4},{12,16},{16,12},{20,24},{24,20},{28,0},{1,29},{... | collective-permute-start | bytes 417800 | tf_op jit(solution)/shard_map/ppermute | solution.py:775
  55.0 4.4 %collective-permute-start.15 = (f32[272,128]{1,0:T(8,128)S(1)}, f32[272,128]{1,0:T(8,128)S(1)}, u32[]{:S(2)}, u32[]{:S(2)}) collective-permute-start(f32[272,128]{1,0:T(8,128)S(1)} %get-tuple-element.81), channel_id=1, source_target_pairs={{0,1},{1,0},{2,3},{3,2},{4,5},{5,4},{6,7},{7,6},{8,9},{9,8},{10,11... | collective-permute-start | bytes 417800 | tf_op jit(solution)/shard_map/ppermute | solution.py:775
  59.4 0.7 collective-permute-start.16
  60.1 5.9 %shard_map.139 = (f32[256,128]{1,0:T(8,128)}, f32[256,128]{1,0:T(8,128)}, f32[256,128]{1,0:T(8,128)}, f32[256,128]{1,0:T(8,128)}, f32[256,128]{1,0:T(8,128)}, /*...) custom-call(s32[48,128]{1,0:T(8,128)S(1)} %get-tuple-element.51.tab, ...), custom_call_target="tpu_custom_call" | custom-call | flops 100000000 | bytes 7938048 | tf_op jit(solution)/shard_map/pallas_call | solution.py:789
  66.0 0.1 collective-permute-start.19
  66.1 1.6 %collective-permute-start.20 = (f32[256,128]{1,0:T(8,128)}, f32[256,128]{1,0:T(8,128)S(1)}, u32[]{:S(2)}, u32[]{:S(2)}) collective-permute-start(f32[256,128]{1,0:T(8,128)} %get-tuple-element.90), channel_id=1, source_target_pairs={{0,8},{4,12},{8,16},{12,20},{16,24},{20,28},{24,0},{28,4},{1,9},{5... | collective-permute-start | bytes 393224 | tf_op jit(solution)/shard_map/ppermute | solution.py:865
  67.7 1.7 %collective-permute-start.21 = (f32[256,128]{1,0:T(8,128)}, f32[256,128]{1,0:T(8,128)S(1)}, u32[]{:S(2)}, u32[]{:S(2)}) collective-permute-start(f32[256,128]{1,0:T(8,128)} %get-tuple-element.91), channel_id=1, source_target_pairs={{0,12},{4,16},{8,20},{12,24},{16,28},{20,0},{24,4},{28,8},{1,13},{... | collective-permute-start | bytes 393224 | tf_op jit(solution)/shard_map/ppermute | solution.py:865
  69.4 0.9 %collective-permute-start.22 = (f32[256,128]{1,0:T(8,128)}, f32[256,128]{1,0:T(8,128)S(1)}, u32[]{:S(2)}, u32[]{:S(2)}) collective-permute-start(f32[256,128]{1,0:T(8,128)} %get-tuple-element.92), channel_id=1, source_target_pairs={{0,16},{4,20},{8,24},{12,28},{16,0},{20,4},{24,8},{28,12},{1,17},{... | collective-permute-start | bytes 393224 | tf_op jit(solution)/shard_map/ppermute | solution.py:865
  70.3 2.1 %collective-permute-done.19.refs_1_ = f32[256,128]{1,0:T(8,128)S(1)} collective-permute-done((f32[256,128]{1,0:T(8,128)}, f32[256,128]{1,0:T(8,128)S(1)}, u32[]{:S(2)}, u32[]{:S(2)}) %collective-permute-start.19) | collective-permute-done | bytes 131104 | tf_op jit(solution)/shard_map/ppermute | solution.py:865
  72.4 0.8 collective-permute-start.24
  73.2 0.5 collective-permute-done.20.refs_2_
  73.7 2.0 %collective-permute-start.25 = (f32[256,128]{1,0:T(8,128)}, f32[256,128]{1,0:T(8,128)S(1)}, u32[]{:S(2)}, u32[]{:S(2)}) collective-permute-start(f32[256,128]{1,0:T(8,128)} %get-tuple-element.95), channel_id=1, source_target_pairs={{0,28},{4,0},{8,4},{12,8},{16,12},{20,16},{24,20},{28,24},{1,29},{... | collective-permute-start | bytes 393224 | tf_op jit(solution)/shard_map/ppermute | solution.py:865
  75.8 2.4 %shard_map.137.before = f32[4096,128]{1,0:T(8,128)S(1)} custom-call(f32[4096,128]{1,0:T(8,128)S(1)} %get-tuple-element.73.moles, f32[4096,128]{1,0:T(8,128)S(1)} %get-tuple-element.74.mobile.mobile_m, f32[4096,128]{1,0:T(8,128)S(1)} %get-tuple-element.78.mobile_f.mobile, f32[2560,128]{1,0:T(8,128)S(1)} %get-tuple-element.65.coef, ...), custom_call_target="tpu_custom_call" | custom-call | flops 100000000 | bytes 9191424 | tf_op jit(solution)/shard_map/pallas_call | solution.py:789
  78.2 0.0 copy-start
  78.2 1.5 %shard_map.138 = (f32[4096,128]{1,0:T(8,128)S(1)}, f32[4096,128]{1,0:T(8,128)}) custom-call(f32[4096,128]{1,0:T(8,128)S(1)} %shard_map.137.before, f32[4096,128]{1,0:T(8,128)S(1)} %get-tuple-element.74.mobile.mobile_m, f32[768,128]{1,0:T(8,128)S(1)} %get-tuple-element.66.rate, ...), custom_call_target="tpu_custom_call", output_to_operand_aliasing={{0}: (0, {})} | custom-call | flops 100000000 | bytes 5783552 | tf_op jit(solution)/shard_map/pallas_call | solution.py:789
  79.7 0.4 collective-permute-done.23.refs_5_
  80.2 1.8 %shard_map.140 = f32[128,1024]{1,0:T(8,128)} custom-call(s32[256]{0:T(256)} %slot_ref.5, s32[3,256]{1,0:T(4,128)} %bitcast.21, f32[256,128]{1,0:T(8,128)S(1)} %copy-done, f32[256,128]{1,0:T(8,128)S(1)} %collective-permute-done.19.refs_1_, f32[256,128]{1,0:T(8,128)S(1)} %collective-permute-done.20.refs_2_, f32[256,128]{1,0:T(8,128)S(1)} %collective-permute-done.21.refs_3_, ...), custom_call_target="tpu_custom_call" | custom-call | flops 100000000 | bytes 1052672 | tf_op jit(solution)/shard_map/pallas_call | solution.py:789
  (30 shorter events, 0.1 us)
Async XLA Ops:
  3.8 8.4 %collective-permute-start = (f32[416,128]{1,0:T(8,128)S(1)}, f32[416,128]{1,0:T(8,128)S(1)}, u32[]{:S(2)}, u32[]{:S(2)}) collective-permute-start(f32[416,128]{1,0:T(8,128)S(1)} %get-tuple-element.53), channel_id=1, source_target_pairs={{0,4},{4,8},{8,12},{12,16},{16,20},{20,24},{24,28},{28,0},{1,5},{5... | collective-permute-start | bytes 638984 | tf_op jit(solution)/shard_map/ppermute | solution.py:865
  4.3 10.3 %collective-permute-start.1 = (f32[416,128]{1,0:T(8,128)S(1)}, f32[416,128]{1,0:T(8,128)S(1)}, u32[]{:S(2)}, u32[]{:S(2)}) collective-permute-start(f32[416,128]{1,0:T(8,128)S(1)} %get-tuple-element.54), channel_id=1, source_target_pairs={{0,8},{4,12},{8,16},{12,20},{16,24},{20,28},{24,0},{28,4},{1,9},{5... | collective-permute-start | bytes 638984 | tf_op jit(solution)/shard_map/ppermute | solution.py:865
  6.9 19.0 %collective-permute-start.2 = (f32[416,128]{1,0:T(8,128)S(1)}, f32[416,128]{1,0:T(8,128)S(1)}, u32[]{:S(2)}, u32[]{:S(2)}) collective-permute-start(f32[416,128]{1,0:T(8,128)S(1)} %get-tuple-element.55), channel_id=1, source_target_pairs={{0,12},{4,16},{8,20},{12,24},{16,28},{20,0},{24,4},{28,8},{1,13},{... | collective-permute-start | bytes 638984 | tf_op jit(solution)/shard_map/ppermute | solution.py:865
  9.2 16.6 %collective-permute-start.3 = (f32[416,128]{1,0:T(8,128)S(1)}, f32[416,128]{1,0:T(8,128)S(1)}, u32[]{:S(2)}, u32[]{:S(2)}) collective-permute-start(f32[416,128]{1,0:T(8,128)S(1)} %get-tuple-element.56), channel_id=1, source_target_pairs={{0,16},{4,20},{8,24},{12,28},{16,0},{20,4},{24,8},{28,12},{1,17},{... | collective-permute-start | bytes 638984 | tf_op jit(solution)/shard_map/ppermute | solution.py:865
  9.7 16.8 %collective-permute-start.4 = (f32[416,128]{1,0:T(8,128)S(1)}, f32[416,128]{1,0:T(8,128)S(1)}, u32[]{:S(2)}, u32[]{:S(2)}) collective-permute-start(f32[416,128]{1,0:T(8,128)S(1)} %get-tuple-element.57), channel_id=1, source_target_pairs={{0,20},{4,24},{8,28},{12,0},{16,4},{20,8},{24,12},{28,16},{1,21},{... | collective-permute-start | bytes 638984 | tf_op jit(solution)/shard_map/ppermute | solution.py:865
  12.2 14.3 %copy-start.1 = (f32[416,128]{1,0:T(8,128)}, f32[416,128]{1,0:T(8,128)S(1)}, u32[]{:S(2)}) copy-start(f32[416,128]{1,0:T(8,128)S(1)} %collective-permute-done.refs_1_) | copy-start | bytes 638980
  12.2 14.3 %collective-permute-start.5 = (f32[416,128]{1,0:T(8,128)S(1)}, f32[416,128]{1,0:T(8,128)S(1)}, u32[]{:S(2)}, u32[]{:S(2)}) collective-permute-start(f32[416,128]{1,0:T(8,128)S(1)} %get-tuple-element.58), channel_id=1, source_target_pairs={{0,24},{4,28},{8,0},{12,4},{16,8},{20,12},{24,16},{28,20},{1,25},{... | collective-permute-start | bytes 638984 | tf_op jit(solution)/shard_map/ppermute | solution.py:865
  14.7 11.9 %copy-start.2 = (f32[416,128]{1,0:T(8,128)}, f32[416,128]{1,0:T(8,128)S(1)}, u32[]{:S(2)}) copy-start(f32[416,128]{1,0:T(8,128)S(1)} %collective-permute-done.1.refs_2_) | copy-start | bytes 638980
  14.7 11.8 %collective-permute-start.6 = (f32[416,128]{1,0:T(8,128)S(1)}, f32[416,128]{1,0:T(8,128)S(1)}, u32[]{:S(2)}, u32[]{:S(2)}) collective-permute-start(f32[416,128]{1,0:T(8,128)S(1)} %get-tuple-element.59), channel_id=1, source_target_pairs={{0,28},{4,0},{8,4},{12,8},{16,12},{20,16},{24,20},{28,24},{1,29},{... | collective-permute-start | bytes 638984 | tf_op jit(solution)/shard_map/ppermute | solution.py:865
  25.8 0.7 copy-start.3
  25.9 0.7 copy-start.4
  26.5 0.7 copy-start.5
  26.5 0.8 copy-start.6
  26.5 0.9 %copy-start.7 = (f32[416,128]{1,0:T(8,128)}, f32[416,128]{1,0:T(8,128)S(1)}, u32[]{:S(2)}) copy-start(f32[416,128]{1,0:T(8,128)S(1)} %collective-permute-done.6.refs_7_) | copy-start | bytes 638980
  32.4 5.3 %collective-permute-start.11 = (f32[272,128]{1,0:T(8,128)S(1)}, f32[272,128]{1,0:T(8,128)S(1)}, u32[]{:S(2)}, u32[]{:S(2)}) collective-permute-start(f32[272,128]{1,0:T(8,128)S(1)} %get-tuple-element.76), channel_id=1, source_target_pairs={{0,4},{4,0},{8,12},{12,8},{16,20},{20,16},{24,28},{28,24},{1,5},{5... | collective-permute-start | bytes 417800 | tf_op jit(solution)/shard_map/ppermute | solution.py:775
  33.1 9.6 %collective-permute-start.12 = (f32[272,128]{1,0:T(8,128)S(1)}, f32[272,128]{1,0:T(8,128)S(1)}, u32[]{:S(2)}, u32[]{:S(2)}) collective-permute-start(f32[272,128]{1,0:T(8,128)S(1)} %get-tuple-element.77), channel_id=1, source_target_pairs={{0,28},{4,8},{8,4},{12,16},{16,12},{20,24},{24,20},{28,0},{1,29},{... | collective-permute-start | bytes 417800 | tf_op jit(solution)/shard_map/ppermute | solution.py:775
  35.6 12.6 %collective-permute-start.7 = (f32[272,128]{1,0:T(8,128)S(1)}, f32[272,128]{1,0:T(8,128)S(1)}, u32[]{:S(2)}, u32[]{:S(2)}) collective-permute-start(f32[272,128]{1,0:T(8,128)S(1)} %get-tuple-element.69), channel_id=1, source_target_pairs={{0,4},{4,0},{8,12},{12,8},{16,20},{20,16},{24,28},{28,24},{1,5},{5... | collective-permute-start | bytes 417800 | tf_op jit(solution)/shard_map/ppermute | solution.py:775
  35.6 14.6 %collective-permute-start.8 = (f32[272,128]{1,0:T(8,128)S(1)}, f32[272,128]{1,0:T(8,128)S(1)}, u32[]{:S(2)}, u32[]{:S(2)}) collective-permute-start(f32[272,128]{1,0:T(8,128)S(1)} %get-tuple-element.70), channel_id=1, source_target_pairs={{0,28},{4,8},{8,4},{12,16},{16,12},{20,24},{24,20},{28,0},{1,29},{... | collective-permute-start | bytes 417800 | tf_op jit(solution)/shard_map/ppermute | solution.py:775
  36.1 14.2 %collective-permute-start.9 = (f32[272,128]{1,0:T(8,128)S(1)}, f32[272,128]{1,0:T(8,128)S(1)}, u32[]{:S(2)}, u32[]{:S(2)}) collective-permute-start(f32[272,128]{1,0:T(8,128)S(1)} %get-tuple-element.71), channel_id=1, source_target_pairs={{0,1},{1,0},{2,3},{3,2},{4,5},{5,4},{6,7},{7,6},{8,9},{9,8},{10,11... | collective-permute-start | bytes 417800 | tf_op jit(solution)/shard_map/ppermute | solution.py:775
  37.6 12.6 %collective-permute-start.10 = (f32[272,128]{1,0:T(8,128)S(1)}, f32[272,128]{1,0:T(8,128)S(1)}, u32[]{:S(2)}, u32[]{:S(2)}) collective-permute-start(f32[272,128]{1,0:T(8,128)S(1)} %get-tuple-element.72), channel_id=1, source_target_pairs={{1,2},{2,1},{5,6},{6,5},{9,10},{10,9},{13,14},{14,13},{17,18},{18,... | collective-permute-start | bytes 417800 | tf_op jit(solution)/shard_map/ppermute | solution.py:775
  48.1 11.4 %collective-permute-start.17 = (f32[272,128]{1,0:T(8,128)S(1)}, f32[272,128]{1,0:T(8,128)S(1)}, u32[]{:S(2)}, u32[]{:S(2)}) collective-permute-start(f32[272,128]{1,0:T(8,128)S(1)} %get-tuple-element.86), channel_id=1, source_target_pairs={{0,4},{4,0},{8,12},{12,8},{16,20},{20,16},{24,28},{28,24},{1,5},{5... | collective-permute-start | bytes 417800 | tf_op jit(solution)/shard_map/ppermute | solution.py:775
  48.2 11.9 %collective-permute-start.18 = (f32[272,128]{1,0:T(8,128)S(1)}, f32[272,128]{1,0:T(8,128)S(1)}, u32[]{:S(2)}, u32[]{:S(2)}) collective-permute-start(f32[272,128]{1,0:T(8,128)S(1)} %get-tuple-element.87), channel_id=1, source_target_pairs={{0,28},{4,8},{8,4},{12,16},{16,12},{20,24},{24,20},{28,0},{1,29},{... | collective-permute-start | bytes 417800 | tf_op jit(solution)/shard_map/ppermute | solution.py:775
  54.1 12.0 %collective-permute-start.13 = (f32[272,128]{1,0:T(8,128)S(1)}, f32[272,128]{1,0:T(8,128)S(1)}, u32[]{:S(2)}, u32[]{:S(2)}) collective-permute-start(f32[272,128]{1,0:T(8,128)S(1)} %get-tuple-element.79), channel_id=1, source_target_pairs={{0,4},{4,0},{8,12},{12,8},{16,20},{20,16},{24,28},{28,24},{1,5},{5... | collective-permute-start | bytes 417800 | tf_op jit(solution)/shard_map/ppermute | solution.py:775
  54.2 13.6 %collective-permute-start.14 = (f32[272,128]{1,0:T(8,128)S(1)}, f32[272,128]{1,0:T(8,128)S(1)}, u32[]{:S(2)}, u32[]{:S(2)}) collective-permute-start(f32[272,128]{1,0:T(8,128)S(1)} %get-tuple-element.80), channel_id=1, source_target_pairs={{0,28},{4,8},{8,4},{12,16},{16,12},{20,24},{24,20},{28,0},{1,29},{... | collective-permute-start | bytes 417800 | tf_op jit(solution)/shard_map/ppermute | solution.py:775
  55.0 14.4 %collective-permute-start.15 = (f32[272,128]{1,0:T(8,128)S(1)}, f32[272,128]{1,0:T(8,128)S(1)}, u32[]{:S(2)}, u32[]{:S(2)}) collective-permute-start(f32[272,128]{1,0:T(8,128)S(1)} %get-tuple-element.81), channel_id=1, source_target_pairs={{0,1},{1,0},{2,3},{3,2},{4,5},{5,4},{6,7},{7,6},{8,9},{9,8},{10,11... | collective-permute-start | bytes 417800 | tf_op jit(solution)/shard_map/ppermute | solution.py:775
  59.4 10.9 %collective-permute-start.16 = (f32[272,128]{1,0:T(8,128)S(1)}, f32[272,128]{1,0:T(8,128)S(1)}, u32[]{:S(2)}, u32[]{:S(2)}) collective-permute-start(f32[272,128]{1,0:T(8,128)S(1)} %get-tuple-element.82), channel_id=1, source_target_pairs={{1,2},{2,1},{5,6},{6,5},{9,10},{10,9},{13,14},{14,13},{17,18},{18,... | collective-permute-start | bytes 417800 | tf_op jit(solution)/shard_map/ppermute | solution.py:775
  66.0 6.4 %collective-permute-start.19 = (f32[256,128]{1,0:T(8,128)}, f32[256,128]{1,0:T(8,128)S(1)}, u32[]{:S(2)}, u32[]{:S(2)}) collective-permute-start(f32[256,128]{1,0:T(8,128)} %get-tuple-element.89), channel_id=1, source_target_pairs={{0,4},{4,8},{8,12},{12,16},{16,20},{20,24},{24,28},{28,0},{1,5},{5... | collective-permute-start | bytes 393224 | tf_op jit(solution)/shard_map/ppermute | solution.py:865
  66.1 7.6 %collective-permute-start.20 = (f32[256,128]{1,0:T(8,128)}, f32[256,128]{1,0:T(8,128)S(1)}, u32[]{:S(2)}, u32[]{:S(2)}) collective-permute-start(f32[256,128]{1,0:T(8,128)} %get-tuple-element.90), channel_id=1, source_target_pairs={{0,8},{4,12},{8,16},{12,20},{16,24},{20,28},{24,0},{28,4},{1,9},{5... | collective-permute-start | bytes 393224 | tf_op jit(solution)/shard_map/ppermute | solution.py:865
  67.7 12.0 %collective-permute-start.21 = (f32[256,128]{1,0:T(8,128)}, f32[256,128]{1,0:T(8,128)S(1)}, u32[]{:S(2)}, u32[]{:S(2)}) collective-permute-start(f32[256,128]{1,0:T(8,128)} %get-tuple-element.91), channel_id=1, source_target_pairs={{0,12},{4,16},{8,20},{12,24},{16,28},{20,0},{24,4},{28,8},{1,13},{... | collective-permute-start | bytes 393224 | tf_op jit(solution)/shard_map/ppermute | solution.py:865
  69.4 10.3 %collective-permute-start.22 = (f32[256,128]{1,0:T(8,128)}, f32[256,128]{1,0:T(8,128)S(1)}, u32[]{:S(2)}, u32[]{:S(2)}) collective-permute-start(f32[256,128]{1,0:T(8,128)} %get-tuple-element.92), channel_id=1, source_target_pairs={{0,16},{4,20},{8,24},{12,28},{16,0},{20,4},{24,8},{28,12},{1,17},{... | collective-permute-start | bytes 393224 | tf_op jit(solution)/shard_map/ppermute | solution.py:865
  70.3 9.9 %collective-permute-start.23 = (f32[256,128]{1,0:T(8,128)}, f32[256,128]{1,0:T(8,128)S(1)}, u32[]{:S(2)}, u32[]{:S(2)}) collective-permute-start(f32[256,128]{1,0:T(8,128)} %get-tuple-element.93), channel_id=1, source_target_pairs={{0,20},{4,24},{8,28},{12,0},{16,4},{20,8},{24,12},{28,16},{1,21},{... | collective-permute-start | bytes 393224 | tf_op jit(solution)/shard_map/ppermute | solution.py:865
  72.4 7.7 %collective-permute-start.24 = (f32[256,128]{1,0:T(8,128)}, f32[256,128]{1,0:T(8,128)S(1)}, u32[]{:S(2)}, u32[]{:S(2)}) collective-permute-start(f32[256,128]{1,0:T(8,128)} %get-tuple-element.94), channel_id=1, source_target_pairs={{0,24},{4,28},{8,0},{12,4},{16,8},{20,12},{24,16},{28,20},{1,25},{... | collective-permute-start | bytes 393224 | tf_op jit(solution)/shard_map/ppermute | solution.py:865
  73.7 6.4 %collective-permute-start.25 = (f32[256,128]{1,0:T(8,128)}, f32[256,128]{1,0:T(8,128)S(1)}, u32[]{:S(2)}, u32[]{:S(2)}) collective-permute-start(f32[256,128]{1,0:T(8,128)} %get-tuple-element.95), channel_id=1, source_target_pairs={{0,28},{4,0},{8,4},{12,8},{16,12},{20,16},{24,20},{28,24},{1,29},{... | collective-permute-start | bytes 393224 | tf_op jit(solution)/shard_map/ppermute | solution.py:865
  78.2 2.0 %copy-start = (f32[256,128]{1,0:T(8,128)S(1)}, f32[256,128]{1,0:T(8,128)}, u32[]{:S(2)}) copy-start(f32[256,128]{1,0:T(8,128)} %get-tuple-element.88.refs_0_) | copy-start | bytes 393220

commit v4 on v3

--- a/solution.py
+++ b/solution.py
@@ -204,7 +204,7 @@
 
 
 def spread_kernel(z, slot_ref, block_ref, *refs):
-    chunks, out = refs[: z.wide], refs[z.wide]
+    chunks, (result, out, sem) = refs[: z.wide], refs[z.wide :]
     sub = iota((SUB, LANES), 0)
     ranks = jnp.zeros((SUB, LANES), I32)
     column = jnp.zeros((SUB, LANES), I32)
@@ -232,9 +232,16 @@
                         v = got if v is None else jnp.where(hits[s], got, v)
                     row = (m * z.cpt + cp) * SUB
                     out[pl.ds(pl.multiple_of(row, SUB), SUB), lanes] = v
+        written(m).start()
         return carry
 
+    def written(m):
+        rows = pl.ds(pl.multiple_of(m * z.cpt * SUB, SUB), z.cpt * SUB)
+        return pltpu.make_async_copy(out.at[rows, :], result.at[rows, :], sem.at[m])
+
     lax.fori_loop(0, z.tiles_back, tile, 0)
+    for m in range(z.tiles_back):
+        written(m).wait()
 
 
 def tables(z, slot_ref, block_ref, tab, gather):
@@ -667,23 +674,27 @@
             return jnp.where(even, hd[rows, :], hc[rows, :])
         return jnp.where(even, hc[rows, :], hd[rows, :])
 
+    face_at = z.z - 1
+    weights = []
     for h in range(z.x // SUB):
-        face_at = z.z - 1
         g = jnp.where(inner, layer(rate, z.cells, h, face_at), 0.0)
         u = layer(upwind, (t * 3 + 1) * z.cells, h, face_at).astype(F32)
         into = (g - g * u) / layer(pore, 0, h, face_at)
-        inv = 1.0 / layer(pore, 0, h, 0)
-        back = side(True, z.nc * z.x + h * SUB)
-        for c in range(z.nc):
-            base = c * z.cells
+        weights.append((into, 1.0 / layer(pore, 0, h, 0), side(True, z.nc * z.x + h * SUB)))
+    copies = []
+    for c in range(z.nc):
+        base = c * z.cells
+        for h, (into, inv, back) in enumerate(weights):
             first = pl.ds(base + h * SUB * z.z, SUB, stride=z.z)
             last = pl.ds(base + h * SUB * z.z + face_at, SUB, stride=z.z)
             row = c * z.x + h * SUB
             new[first, :] = new[first, :] + inv * (side(True, row) - back * mobile[first, :])
             new[last, :] = new[last, :] + into * side(False, row)
-    copy = pltpu.make_async_copy(new, result, sem)
-    copy.start()
-    copy.wait()
+        rows = pl.ds(base, z.cells)
+        copies.append(pltpu.make_async_copy(new.at[rows, :], result.at[rows, :], sem.at[c]))
+        copies[-1].start()
+    for copy in copies:
+        copy.wait()
 
 
 def frac_update(z, t, tab, moles, mobile, mobile_m, coef, frac_a, frac_b, new):
@@ -946,14 +957,16 @@
         bind(depth_kernel, t), [VMEM] * 7,
         (field, shape(z.nc * z.cells, space=pltpu.HBM)),
         in_vmem(moles, mobile_m, rate, upwind, pore, *deep_halos),
-        scratch=[pltpu.SemaphoreType.DMA],
+        scratch=[pltpu.SemaphoreType.DMA((z.nc,))],
         out_specs=(VMEM, HBM),
         aliases={0: 0},
     )
     frac = call(
         bind(spread_kernel), [SMEM] * 2 + [VMEM] * z.wide,
-        jax.ShapeDtypeStruct((z.nc * z.slots, z.pc), F32),
+        shape(z.nc * z.slots, z.pc, pltpu.HBM),
         (slot_patch, blocks, *in_vmem(*returned)),
+        scratch=[pltpu.VMEM((z.nc * z.slots, z.pc), F32), pltpu.SemaphoreType.DMA((z.tiles_back,))],
+        out_specs=HBM,
     )
     return moles.reshape(matrix_moles.shape), frac.reshape(frac_moles.shape)
 

time: 82.9 us -> 82.9 us (level)
  no operation moved by 1% of the time
where the time goes in v4:
time: 82.9 us; the launch traced here: 81.9 us
  Pallas kernels  40.1 us (48%)
  starting transfers between devices  34 us (41%)
  waiting for transfers between devices  6.09 us (7%)
  between operations  0.88 us (1%)
  local copies, waits for them, and re-layouts  0.84 us (1%)
    pallas_call x10, Pallas kernels, call(): pl.pallas_call(body, out_shape=out_shape, in_specs=in_specs, out_specs=ou...  40.1 us
    ppermute x14, starting transfers between devices, trade(): got.append(lax.ppermute(chunks[s], 'wide', pairs))  19.9 us
    ppermute x12, starting transfers between devices, swap(): return lax.ppermute(value, axis, pairs)  14.1 us
    ppermute x14, waiting for transfers between devices, trade(): got.append(lax.ppermute(chunks[s], 'wide', pairs))  6.06 us
  transfers between devices with their start and end apart: 26, of which 5 were waited for; matrix products, arithmetic and copies ran while one was open for 0% of the time, Pallas kernels for 37%

profile of v4, /device:TPU:0, one launch (start us, length us, event | category | flops | bytes accessed | tf_op | source)
XLA Modules:
  0.0 81.9 jit_solution(13134395071878815833)
XLA Ops:
  0.6 3.1 %shard_map.132 = (f32[416,128]{1,0:T(8,128)S(1)}, f32[416,128]{1,0:T(8,128)S(1)}, f32[416,128]{1,0:T(8,128)S(1)}, f32[416,128]{1,0:T(8,128)S(1)}, f32[416,128]{1...) custom-call(s32[256]{0:T(256)} %slot_ref.5, s32[3,256]{1,0:T(4,128)} %bitcast.19, ...), custom_call_target="tpu_custom_call" | custom-call | flops 100000000 | bytes 856128 | tf_op jit(solution)/shard_map/pallas_call | solution.py:800
  3.8 0.5 collective-permute-start
  4.3 2.5 %collective-permute-start.1 = (f32[416,128]{1,0:T(8,128)S(1)}, f32[416,128]{1,0:T(8,128)S(1)}, u32[]{:S(2)}, u32[]{:S(2)}) collective-permute-start(f32[416,128]{1,0:T(8,128)S(1)} %get-tuple-element.54), channel_id=1, source_target_pairs={{0,8},{4,12},{8,16},{12,20},{16,24},{20,28},{24,0},{28,4},{1,9},{5... | collective-permute-start | bytes 638984 | tf_op jit(solution)/shard_map/ppermute | solution.py:876
  6.9 2.4 %collective-permute-start.2 = (f32[416,128]{1,0:T(8,128)S(1)}, f32[416,128]{1,0:T(8,128)S(1)}, u32[]{:S(2)}, u32[]{:S(2)}) collective-permute-start(f32[416,128]{1,0:T(8,128)S(1)} %get-tuple-element.55), channel_id=1, source_target_pairs={{0,12},{4,16},{8,20},{12,24},{16,28},{20,0},{24,4},{28,8},{1,13},{... | collective-permute-start | bytes 638984 | tf_op jit(solution)/shard_map/ppermute | solution.py:876
  9.2 0.5 collective-permute-start.3
  9.7 0.1 collective-permute-start.4
  9.8 2.3 %collective-permute-done.refs_1_ = f32[416,128]{1,0:T(8,128)S(1)} collective-permute-done((f32[416,128]{1,0:T(8,128)S(1)}, f32[416,128]{1,0:T(8,128)S(1)}, u32[]{:S(2)}, u32[]{:S(2)}) %collective-permute-start) | collective-permute-done | bytes 213024 | tf_op jit(solution)/shard_map/ppermute | solution.py:876
  12.2 2.5 %collective-permute-start.5 = (f32[416,128]{1,0:T(8,128)S(1)}, f32[416,128]{1,0:T(8,128)S(1)}, u32[]{:S(2)}, u32[]{:S(2)}) collective-permute-start(f32[416,128]{1,0:T(8,128)S(1)} %get-tuple-element.58), channel_id=1, source_target_pairs={{0,24},{4,28},{8,0},{12,4},{16,8},{20,12},{24,16},{28,20},{1,25},{... | collective-permute-start | bytes 638984 | tf_op jit(solution)/shard_map/ppermute | solution.py:876
  14.7 4.3 %collective-permute-start.6 = (f32[416,128]{1,0:T(8,128)S(1)}, f32[416,128]{1,0:T(8,128)S(1)}, u32[]{:S(2)}, u32[]{:S(2)}) collective-permute-start(f32[416,128]{1,0:T(8,128)S(1)} %get-tuple-element.59), channel_id=1, source_target_pairs={{0,28},{4,0},{8,4},{12,8},{16,12},{20,16},{24,20},{28,24},{1,29},{... | collective-permute-start | bytes 638984 | tf_op jit(solution)/shard_map/ppermute | solution.py:876
  18.9 6.9 %shard_map.131 = (f32[4096,128]{1,0:T(8,128)S(1)}, f32[4096,128]{1,0:T(8,128)S(1)}, f32[272,128]{1,0:T(8,128)S(1)}, f32[272,128]{1,0:T(8,128)S(1)}, f32[272,128]...) custom-call(f32[16]{0:T(128)} %k_ref.9, ...), custom_call_target="tpu_custom_call" | custom-call | flops 100000000 | bytes 3412032 | tf_op jit(solution)/shard_map/pallas_call | solution.py:800
  25.8 0.0 collective-permute-done.2.refs_3_
  25.9 0.6 collective-permute-done.4.refs_5_
  26.5 0.0 collective-permute-done.5.refs_6_
  26.5 0.0 collective-permute-done.6.refs_7_
  26.5 0.1 copy-done.4
  26.6 0.6 copy-done.5
  27.2 0.1 copy-done.6
  27.3 0.1 copy-done.7
  27.4 5.0 %shard_map.133 = (f32[4096,128]{1,0:T(8,128)S(1)}, f32[4096,128]{1,0:T(8,128)S(1)}, f32[2560,128]{1,0:T(8,128)S(1)}, f32[272,128]{1,0:T(8,128)S(1)}, f32[272,128]{1,0:T(8,128)S(1)}, /*index=5*/f32[1664,128]{1,0:T(8,128)S(1)}) custom-call(f32[16]{0:T(128)} %k_ref.9, s32[48,128]{1,0:T(8,128)S(1)} %get-tuple-element.51.tab, ...), custom_call_target="tpu_custom_call" | custom-call | flops 100000000 | bytes 1728576 | tf_op jit(solution)/shard_map/pallas_call | solution.py:800
  32.4 0.8 collective-permute-start.11
  33.1 2.5 %collective-permute-start.12 = (f32[272,128]{1,0:T(8,128)S(1)}, f32[272,128]{1,0:T(8,128)S(1)}, u32[]{:S(2)}, u32[]{:S(2)}) collective-permute-start(f32[272,128]{1,0:T(8,128)S(1)} %get-tuple-element.77), channel_id=1, source_target_pairs={{0,28},{4,8},{8,4},{12,16},{16,12},{20,24},{24,20},{28,0},{1,29},{... | collective-permute-start | bytes 417800 | tf_op jit(solution)/shard_map/ppermute | solution.py:786
  35.6 0.4 collective-permute-start.8
  36.1 1.6 %collective-permute-start.9 = (f32[272,128]{1,0:T(8,128)S(1)}, f32[272,128]{1,0:T(8,128)S(1)}, u32[]{:S(2)}, u32[]{:S(2)}) collective-permute-start(f32[272,128]{1,0:T(8,128)S(1)} %get-tuple-element.71), channel_id=1, source_target_pairs={{0,1},{1,0},{2,3},{3,2},{4,5},{5,4},{6,7},{7,6},{8,9},{9,8},{10,11... | collective-permute-start | bytes 417800 | tf_op jit(solution)/shard_map/ppermute | solution.py:786
  37.6 0.0 collective-permute-done.11.fa
  37.6 0.7 collective-permute-start.10
  38.3 4.4 %shard_map.134 = (f32[4096,128]{1,0:T(8,128)S(1)}, f32[4096,128]{1,0:T(8,128)S(1)}, f32[2560,128]{1,0:T(8,128)S(1)}) custom-call(f32[16]{0:T(128)} %k_ref.9, s32[48,128]{1,0:T(8,128)S(1)} %get-tuple-element.51.tab, f32[1664,128]{1,0:T(8,128)S(1)} %get-tuple-element.60.recv, ...), custom_call_target="tpu_custom_call", output_to_operand_aliasing={{0}: (3, {}), {1}: (4, {}), {2}: (5, {})} | custom-call | flops 100000000 | bytes 6381632 | tf_op jit(solution)/shard_map/pallas_call | solution.py:800
  42.7 5.3 %shard_map.136 = (f32[4096,128]{1,0:T(8,128)S(1)}, f32[4096,128]{1,0:T(8,128)S(1)}, f32[272,128]{1,0:T(8,128)S(1)}, f32[272,128]{1,0:T(8,128)S(1)}) custom-call(f32[16]{0:T(128)} %k_ref.9, s32[48,128]{1,0:T(8,128)S(1)} %get-tuple-element.51.tab, f32[4096,128]{1,0:T(8,128)S(1)} %get-tuple-element.75.moles, f32[4096,128]{1,0:T(8,128)S(1)} %get-tuple-element.64.mobile_f.mobile, ...), custom_call_target="tpu_custom_call" | custom-call | flops 100000000 | bytes 7905344 | tf_op jit(solution)/shard_map/pallas_call | solution.py:800
  48.1 0.1 collective-permute-start.17
  48.2 2.1 %collective-permute-start.18 = (f32[272,128]{1,0:T(8,128)S(1)}, f32[272,128]{1,0:T(8,128)S(1)}, u32[]{:S(2)}, u32[]{:S(2)}) collective-permute-start(f32[272,128]{1,0:T(8,128)S(1)} %get-tuple-element.87), channel_id=1, source_target_pairs={{0,28},{4,8},{8,4},{12,16},{16,12},{20,24},{24,20},{28,0},{1,29},{... | collective-permute-start | bytes 417800 | tf_op jit(solution)/shard_map/ppermute | solution.py:786
  50.3 3.8 %shard_map.135 = (f32[4096,128]{1,0:T(8,128)S(1)}, f32[4096,128]{1,0:T(8,128)S(1)}, f32[272,128]{1,0:T(8,128)S(1)}, f32[272,128]{1,0:T(8,128)S(1)}, f32[272,128]{1,0:T(8,128)S(1)}, /*index=5*/f32[272,128]{1,0:T(8,128)S(1)}) custom-call(f32[16]{0:T(128)} %k_ref.9, f32[4096,128]{1,0:T(8,128)S(1)} %get-tuple-element.49.moles, ...), custom_call_target="tpu_custom_call" | custom-call | flops 100000000 | bytes 9470016 | tf_op jit(solution)/shard_map/pallas_call | solution.py:800
  54.1 0.1 collective-permute-start.13
  54.2 0.9 %collective-permute-start.14 = (f32[272,128]{1,0:T(8,128)S(1)}, f32[272,128]{1,0:T(8,128)S(1)}, u32[]{:S(2)}, u32[]{:S(2)}) collective-permute-start(f32[272,128]{1,0:T(8,128)S(1)} %get-tuple-element.80), channel_id=1, source_target_pairs={{0,28},{4,8},{8,4},{12,16},{16,12},{20,24},{24,20},{28,0},{1,29},{... | collective-permute-start | bytes 417800 | tf_op jit(solution)/shard_map/ppermute | solution.py:786
  55.0 4.4 %collective-permute-start.15 = (f32[272,128]{1,0:T(8,128)S(1)}, f32[272,128]{1,0:T(8,128)S(1)}, u32[]{:S(2)}, u32[]{:S(2)}) collective-permute-start(f32[272,128]{1,0:T(8,128)S(1)} %get-tuple-element.81), channel_id=1, source_target_pairs={{0,1},{1,0},{2,3},{3,2},{4,5},{5,4},{6,7},{7,6},{8,9},{9,8},{10,11... | collective-permute-start | bytes 417800 | tf_op jit(solution)/shard_map/ppermute | solution.py:786
  59.4 0.7 collective-permute-start.16
  60.1 5.9 %shard_map.139 = (f32[256,128]{1,0:T(8,128)}, f32[256,128]{1,0:T(8,128)}, f32[256,128]{1,0:T(8,128)}, f32[256,128]{1,0:T(8,128)}, f32[256,128]{1,0:T(8,128)}, /*...) custom-call(s32[48,128]{1,0:T(8,128)S(1)} %get-tuple-element.51.tab, ...), custom_call_target="tpu_custom_call" | custom-call | flops 100000000 | bytes 7938048 | tf_op jit(solution)/shard_map/pallas_call | solution.py:800
  66.0 0.1 collective-permute-start.19
  66.1 1.6 %collective-permute-start.20 = (f32[256,128]{1,0:T(8,128)}, f32[256,128]{1,0:T(8,128)S(1)}, u32[]{:S(2)}, u32[]{:S(2)}) collective-permute-start(f32[256,128]{1,0:T(8,128)} %get-tuple-element.90), channel_id=1, source_target_pairs={{0,8},{4,12},{8,16},{12,20},{16,24},{20,28},{24,0},{28,4},{1,9},{5... | collective-permute-start | bytes 393224 | tf_op jit(solution)/shard_map/ppermute | solution.py:876
  67.7 1.7 %collective-permute-start.21 = (f32[256,128]{1,0:T(8,128)}, f32[256,128]{1,0:T(8,128)S(1)}, u32[]{:S(2)}, u32[]{:S(2)}) collective-permute-start(f32[256,128]{1,0:T(8,128)} %get-tuple-element.91), channel_id=1, source_target_pairs={{0,12},{4,16},{8,20},{12,24},{16,28},{20,0},{24,4},{28,8},{1,13},{... | collective-permute-start | bytes 393224 | tf_op jit(solution)/shard_map/ppermute | solution.py:876
  69.4 0.9 %collective-permute-start.22 = (f32[256,128]{1,0:T(8,128)}, f32[256,128]{1,0:T(8,128)S(1)}, u32[]{:S(2)}, u32[]{:S(2)}) collective-permute-start(f32[256,128]{1,0:T(8,128)} %get-tuple-element.92), channel_id=1, source_target_pairs={{0,16},{4,20},{8,24},{12,28},{16,0},{20,4},{24,8},{28,12},{1,17},{... | collective-permute-start | bytes 393224 | tf_op jit(solution)/shard_map/ppermute | solution.py:876
  70.3 2.1 %collective-permute-done.19.refs_1_ = f32[256,128]{1,0:T(8,128)S(1)} collective-permute-done((f32[256,128]{1,0:T(8,128)}, f32[256,128]{1,0:T(8,128)S(1)}, u32[]{:S(2)}, u32[]{:S(2)}) %collective-permute-start.19) | collective-permute-done | bytes 131104 | tf_op jit(solution)/shard_map/ppermute | solution.py:876
  72.4 0.8 collective-permute-start.24
  73.2 0.5 collective-permute-done.20.refs_2_
  73.7 2.0 %collective-permute-start.25 = (f32[256,128]{1,0:T(8,128)}, f32[256,128]{1,0:T(8,128)S(1)}, u32[]{:S(2)}, u32[]{:S(2)}) collective-permute-start(f32[256,128]{1,0:T(8,128)} %get-tuple-element.95), channel_id=1, source_target_pairs={{0,28},{4,0},{8,4},{12,8},{16,12},{20,16},{24,20},{28,24},{1,29},{... | collective-permute-start | bytes 393224 | tf_op jit(solution)/shard_map/ppermute | solution.py:876
  75.8 2.4 %shard_map.137.before = f32[4096,128]{1,0:T(8,128)S(1)} custom-call(f32[4096,128]{1,0:T(8,128)S(1)} %get-tuple-element.73.moles, f32[4096,128]{1,0:T(8,128)S(1)} %get-tuple-element.74.mobile.mobile_m, f32[4096,128]{1,0:T(8,128)S(1)} %get-tuple-element.78.mobile_f.mobile, f32[2560,128]{1,0:T(8,128)S(1)} %get-tuple-element.65.coef, ...), custom_call_target="tpu_custom_call" | custom-call | flops 100000000 | bytes 9191424 | tf_op jit(solution)/shard_map/pallas_call | solution.py:800
  78.2 0.0 copy-start
  78.2 1.5 %shard_map.138 = (f32[4096,128]{1,0:T(8,128)S(1)}, f32[4096,128]{1,0:T(8,128)}) custom-call(f32[4096,128]{1,0:T(8,128)S(1)} %shard_map.137.before, f32[4096,128]{1,0:T(8,128)S(1)} %get-tuple-element.74.mobile.mobile_m, f32[768,128]{1,0:T(8,128)S(1)} %get-tuple-element.66.rate, ...), custom_call_target="tpu_custom_call", output_to_operand_aliasing={{0}: (0, {})} | custom-call | flops 100000000 | bytes 5783552 | tf_op jit(solution)/shard_map/pallas_call | solution.py:800
  79.7 0.5 collective-permute-done.23.refs_5_
  80.2 1.8 %shard_map.140 = f32[128,1024]{1,0:T(8,128)} custom-call(s32[256]{0:T(256)} %slot_ref.5, s32[3,256]{1,0:T(4,128)} %bitcast.21, f32[256,128]{1,0:T(8,128)S(1)} %copy-done, f32[256,128]{1,0:T(8,128)S(1)} %collective-permute-done.19.refs_1_, f32[256,128]{1,0:T(8,128)S(1)} %collective-permute-done.20.refs_2_, f32[256,128]{1,0:T(8,128)S(1)} %collective-permute-done.21.refs_3_, ...), custom_call_target="tpu_custom_call" | custom-call | flops 100000000 | bytes 1052672 | tf_op jit(solution)/shard_map/pallas_call | solution.py:800
  (30 shorter events, 0.1 us)
Async XLA Ops:
  3.8 8.4 %collective-permute-start = (f32[416,128]{1,0:T(8,128)S(1)}, f32[416,128]{1,0:T(8,128)S(1)}, u32[]{:S(2)}, u32[]{:S(2)}) collective-permute-start(f32[416,128]{1,0:T(8,128)S(1)} %get-tuple-element.53), channel_id=1, source_target_pairs={{0,4},{4,8},{8,12},{12,16},{16,20},{20,24},{24,28},{28,0},{1,5},{5... | collective-permute-start | bytes 638984 | tf_op jit(solution)/shard_map/ppermute | solution.py:876
  4.3 10.3 %collective-permute-start.1 = (f32[416,128]{1,0:T(8,128)S(1)}, f32[416,128]{1,0:T(8,128)S(1)}, u32[]{:S(2)}, u32[]{:S(2)}) collective-permute-start(f32[416,128]{1,0:T(8,128)S(1)} %get-tuple-element.54), channel_id=1, source_target_pairs={{0,8},{4,12},{8,16},{12,20},{16,24},{20,28},{24,0},{28,4},{1,9},{5... | collective-permute-start | bytes 638984 | tf_op jit(solution)/shard_map/ppermute | solution.py:876
  6.9 19.0 %collective-permute-start.2 = (f32[416,128]{1,0:T(8,128)S(1)}, f32[416,128]{1,0:T(8,128)S(1)}, u32[]{:S(2)}, u32[]{:S(2)}) collective-permute-start(f32[416,128]{1,0:T(8,128)S(1)} %get-tuple-element.55), channel_id=1, source_target_pairs={{0,12},{4,16},{8,20},{12,24},{16,28},{20,0},{24,4},{28,8},{1,13},{... | collective-permute-start | bytes 638984 | tf_op jit(solution)/shard_map/ppermute | solution.py:876
  9.2 16.6 %collective-permute-start.3 = (f32[416,128]{1,0:T(8,128)S(1)}, f32[416,128]{1,0:T(8,128)S(1)}, u32[]{:S(2)}, u32[]{:S(2)}) collective-permute-start(f32[416,128]{1,0:T(8,128)S(1)} %get-tuple-element.56), channel_id=1, source_target_pairs={{0,16},{4,20},{8,24},{12,28},{16,0},{20,4},{24,8},{28,12},{1,17},{... | collective-permute-start | bytes 638984 | tf_op jit(solution)/shard_map/ppermute | solution.py:876
  9.7 16.8 %collective-permute-start.4 = (f32[416,128]{1,0:T(8,128)S(1)}, f32[416,128]{1,0:T(8,128)S(1)}, u32[]{:S(2)}, u32[]{:S(2)}) collective-permute-start(f32[416,128]{1,0:T(8,128)S(1)} %get-tuple-element.57), channel_id=1, source_target_pairs={{0,20},{4,24},{8,28},{12,0},{16,4},{20,8},{24,12},{28,16},{1,21},{... | collective-permute-start | bytes 638984 | tf_op jit(solution)/shard_map/ppermute | solution.py:876
  12.2 14.3 %copy-start.1 = (f32[416,128]{1,0:T(8,128)}, f32[416,128]{1,0:T(8,128)S(1)}, u32[]{:S(2)}) copy-start(f32[416,128]{1,0:T(8,128)S(1)} %collective-permute-done.refs_1_) | copy-start | bytes 638980
  12.2 14.3 %collective-permute-start.5 = (f32[416,128]{1,0:T(8,128)S(1)}, f32[416,128]{1,0:T(8,128)S(1)}, u32[]{:S(2)}, u32[]{:S(2)}) collective-permute-start(f32[416,128]{1,0:T(8,128)S(1)} %get-tuple-element.58), channel_id=1, source_target_pairs={{0,24},{4,28},{8,0},{12,4},{16,8},{20,12},{24,16},{28,20},{1,25},{... | collective-permute-start | bytes 638984 | tf_op jit(solution)/shard_map/ppermute | solution.py:876
  14.7 11.9 %copy-start.2 = (f32[416,128]{1,0:T(8,128)}, f32[416,128]{1,0:T(8,128)S(1)}, u32[]{:S(2)}) copy-start(f32[416,128]{1,0:T(8,128)S(1)} %collective-permute-done.1.refs_2_) | copy-start | bytes 638980
  14.7 11.8 %collective-permute-start.6 = (f32[416,128]{1,0:T(8,128)S(1)}, f32[416,128]{1,0:T(8,128)S(1)}, u32[]{:S(2)}, u32[]{:S(2)}) collective-permute-start(f32[416,128]{1,0:T(8,128)S(1)} %get-tuple-element.59), channel_id=1, source_target_pairs={{0,28},{4,0},{8,4},{12,8},{16,12},{20,16},{24,20},{28,24},{1,29},{... | collective-permute-start | bytes 638984 | tf_op jit(solution)/shard_map/ppermute | solution.py:876
  25.8 0.7 copy-start.3
  25.9 0.7 copy-start.4
  26.5 0.7 copy-start.5
  26.5 0.8 copy-start.6
  26.5 0.9 %copy-start.7 = (f32[416,128]{1,0:T(8,128)}, f32[416,128]{1,0:T(8,128)S(1)}, u32[]{:S(2)}) copy-start(f32[416,128]{1,0:T(8,128)S(1)} %collective-permute-done.6.refs_7_) | copy-start | bytes 638980
  32.4 5.3 %collective-permute-start.11 = (f32[272,128]{1,0:T(8,128)S(1)}, f32[272,128]{1,0:T(8,128)S(1)}, u32[]{:S(2)}, u32[]{:S(2)}) collective-permute-start(f32[272,128]{1,0:T(8,128)S(1)} %get-tuple-element.76), channel_id=1, source_target_pairs={{0,4},{4,0},{8,12},{12,8},{16,20},{20,16},{24,28},{28,24},{1,5},{5... | collective-permute-start | bytes 417800 | tf_op jit(solution)/shard_map/ppermute | solution.py:786
  33.1 9.6 %collective-permute-start.12 = (f32[272,128]{1,0:T(8,128)S(1)}, f32[272,128]{1,0:T(8,128)S(1)}, u32[]{:S(2)}, u32[]{:S(2)}) collective-permute-start(f32[272,128]{1,0:T(8,128)S(1)} %get-tuple-element.77), channel_id=1, source_target_pairs={{0,28},{4,8},{8,4},{12,16},{16,12},{20,24},{24,20},{28,0},{1,29},{... | collective-permute-start | bytes 417800 | tf_op jit(solution)/shard_map/ppermute | solution.py:786
  35.6 12.6 %collective-permute-start.7 = (f32[272,128]{1,0:T(8,128)S(1)}, f32[272,128]{1,0:T(8,128)S(1)}, u32[]{:S(2)}, u32[]{:S(2)}) collective-permute-start(f32[272,128]{1,0:T(8,128)S(1)} %get-tuple-element.69), channel_id=1, source_target_pairs={{0,4},{4,0},{8,12},{12,8},{16,20},{20,16},{24,28},{28,24},{1,5},{5... | collective-permute-start | bytes 417800 | tf_op jit(solution)/shard_map/ppermute | solution.py:786
  35.6 14.6 %collective-permute-start.8 = (f32[272,128]{1,0:T(8,128)S(1)}, f32[272,128]{1,0:T(8,128)S(1)}, u32[]{:S(2)}, u32[]{:S(2)}) collective-permute-start(f32[272,128]{1,0:T(8,128)S(1)} %get-tuple-element.70), channel_id=1, source_target_pairs={{0,28},{4,8},{8,4},{12,16},{16,12},{20,24},{24,20},{28,0},{1,29},{... | collective-permute-start | bytes 417800 | tf_op jit(solution)/shard_map/ppermute | solution.py:786
  36.1 14.2 %collective-permute-start.9 = (f32[272,128]{1,0:T(8,128)S(1)}, f32[272,128]{1,0:T(8,128)S(1)}, u32[]{:S(2)}, u32[]{:S(2)}) collective-permute-start(f32[272,128]{1,0:T(8,128)S(1)} %get-tuple-element.71), channel_id=1, source_target_pairs={{0,1},{1,0},{2,3},{3,2},{4,5},{5,4},{6,7},{7,6},{8,9},{9,8},{10,11... | collective-permute-start | bytes 417800 | tf_op jit(solution)/shard_map/ppermute | solution.py:786
  37.6 12.6 %collective-permute-start.10 = (f32[272,128]{1,0:T(8,128)S(1)}, f32[272,128]{1,0:T(8,128)S(1)}, u32[]{:S(2)}, u32[]{:S(2)}) collective-permute-start(f32[272,128]{1,0:T(8,128)S(1)} %get-tuple-element.72), channel_id=1, source_target_pairs={{1,2},{2,1},{5,6},{6,5},{9,10},{10,9},{13,14},{14,13},{17,18},{18,... | collective-permute-start | bytes 417800 | tf_op jit(solution)/shard_map/ppermute | solution.py:786
  48.1 11.4 %collective-permute-start.17 = (f32[272,128]{1,0:T(8,128)S(1)}, f32[272,128]{1,0:T(8,128)S(1)}, u32[]{:S(2)}, u32[]{:S(2)}) collective-permute-start(f32[272,128]{1,0:T(8,128)S(1)} %get-tuple-element.86), channel_id=1, source_target_pairs={{0,4},{4,0},{8,12},{12,8},{16,20},{20,16},{24,28},{28,24},{1,5},{5... | collective-permute-start | bytes 417800 | tf_op jit(solution)/shard_map/ppermute | solution.py:786
  48.2 11.9 %collective-permute-start.18 = (f32[272,128]{1,0:T(8,128)S(1)}, f32[272,128]{1,0:T(8,128)S(1)}, u32[]{:S(2)}, u32[]{:S(2)}) collective-permute-start(f32[272,128]{1,0:T(8,128)S(1)} %get-tuple-element.87), channel_id=1, source_target_pairs={{0,28},{4,8},{8,4},{12,16},{16,12},{20,24},{24,20},{28,0},{1,29},{... | collective-permute-start | bytes 417800 | tf_op jit(solution)/shard_map/ppermute | solution.py:786
  54.1 12.0 %collective-permute-start.13 = (f32[272,128]{1,0:T(8,128)S(1)}, f32[272,128]{1,0:T(8,128)S(1)}, u32[]{:S(2)}, u32[]{:S(2)}) collective-permute-start(f32[272,128]{1,0:T(8,128)S(1)} %get-tuple-element.79), channel_id=1, source_target_pairs={{0,4},{4,0},{8,12},{12,8},{16,20},{20,16},{24,28},{28,24},{1,5},{5... | collective-permute-start | bytes 417800 | tf_op jit(solution)/shard_map/ppermute | solution.py:786
  54.2 13.6 %collective-permute-start.14 = (f32[272,128]{1,0:T(8,128)S(1)}, f32[272,128]{1,0:T(8,128)S(1)}, u32[]{:S(2)}, u32[]{:S(2)}) collective-permute-start(f32[272,128]{1,0:T(8,128)S(1)} %get-tuple-element.80), channel_id=1, source_target_pairs={{0,28},{4,8},{8,4},{12,16},{16,12},{20,24},{24,20},{28,0},{1,29},{... | collective-permute-start | bytes 417800 | tf_op jit(solution)/shard_map/ppermute | solution.py:786
  55.0 14.4 %collective-permute-start.15 = (f32[272,128]{1,0:T(8,128)S(1)}, f32[272,128]{1,0:T(8,128)S(1)}, u32[]{:S(2)}, u32[]{:S(2)}) collective-permute-start(f32[272,128]{1,0:T(8,128)S(1)} %get-tuple-element.81), channel_id=1, source_target_pairs={{0,1},{1,0},{2,3},{3,2},{4,5},{5,4},{6,7},{7,6},{8,9},{9,8},{10,11... | collective-permute-start | bytes 417800 | tf_op jit(solution)/shard_map/ppermute | solution.py:786
  59.4 10.9 %collective-permute-start.16 = (f32[272,128]{1,0:T(8,128)S(1)}, f32[272,128]{1,0:T(8,128)S(1)}, u32[]{:S(2)}, u32[]{:S(2)}) collective-permute-start(f32[272,128]{1,0:T(8,128)S(1)} %get-tuple-element.82), channel_id=1, source_target_pairs={{1,2},{2,1},{5,6},{6,5},{9,10},{10,9},{13,14},{14,13},{17,18},{18,... | collective-permute-start | bytes 417800 | tf_op jit(solution)/shard_map/ppermute | solution.py:786
  66.0 6.4 %collective-permute-start.19 = (f32[256,128]{1,0:T(8,128)}, f32[256,128]{1,0:T(8,128)S(1)}, u32[]{:S(2)}, u32[]{:S(2)}) collective-permute-start(f32[256,128]{1,0:T(8,128)} %get-tuple-element.89), channel_id=1, source_target_pairs={{0,4},{4,8},{8,12},{12,16},{16,20},{20,24},{24,28},{28,0},{1,5},{5... | collective-permute-start | bytes 393224 | tf_op jit(solution)/shard_map/ppermute | solution.py:876
  66.1 7.6 %collective-permute-start.20 = (f32[256,128]{1,0:T(8,128)}, f32[256,128]{1,0:T(8,128)S(1)}, u32[]{:S(2)}, u32[]{:S(2)}) collective-permute-start(f32[256,128]{1,0:T(8,128)} %get-tuple-element.90), channel_id=1, source_target_pairs={{0,8},{4,12},{8,16},{12,20},{16,24},{20,28},{24,0},{28,4},{1,9},{5... | collective-permute-start | bytes 393224 | tf_op jit(solution)/shard_map/ppermute | solution.py:876
  67.7 11.9 %collective-permute-start.21 = (f32[256,128]{1,0:T(8,128)}, f32[256,128]{1,0:T(8,128)S(1)}, u32[]{:S(2)}, u32[]{:S(2)}) collective-permute-start(f32[256,128]{1,0:T(8,128)} %get-tuple-element.91), channel_id=1, source_target_pairs={{0,12},{4,16},{8,20},{12,24},{16,28},{20,0},{24,4},{28,8},{1,13},{... | collective-permute-start | bytes 393224 | tf_op jit(solution)/shard_map/ppermute | solution.py:876
  69.4 10.3 %collective-permute-start.22 = (f32[256,128]{1,0:T(8,128)}, f32[256,128]{1,0:T(8,128)S(1)}, u32[]{:S(2)}, u32[]{:S(2)}) collective-permute-start(f32[256,128]{1,0:T(8,128)} %get-tuple-element.92), channel_id=1, source_target_pairs={{0,16},{4,20},{8,24},{12,28},{16,0},{20,4},{24,8},{28,12},{1,17},{... | collective-permute-start | bytes 393224 | tf_op jit(solution)/shard_map/ppermute | solution.py:876
  70.3 9.9 %collective-permute-start.23 = (f32[256,128]{1,0:T(8,128)}, f32[256,128]{1,0:T(8,128)S(1)}, u32[]{:S(2)}, u32[]{:S(2)}) collective-permute-start(f32[256,128]{1,0:T(8,128)} %get-tuple-element.93), channel_id=1, source_target_pairs={{0,20},{4,24},{8,28},{12,0},{16,4},{20,8},{24,12},{28,16},{1,21},{... | collective-permute-start | bytes 393224 | tf_op jit(solution)/shard_map/ppermute | solution.py:876
  72.4 7.7 %collective-permute-start.24 = (f32[256,128]{1,0:T(8,128)}, f32[256,128]{1,0:T(8,128)S(1)}, u32[]{:S(2)}, u32[]{:S(2)}) collective-permute-start(f32[256,128]{1,0:T(8,128)} %get-tuple-element.94), channel_id=1, source_target_pairs={{0,24},{4,28},{8,0},{12,4},{16,8},{20,12},{24,16},{28,20},{1,25},{... | collective-permute-start | bytes 393224 | tf_op jit(solution)/shard_map/ppermute | solution.py:876
  73.7 6.4 %collective-permute-start.25 = (f32[256,128]{1,0:T(8,128)}, f32[256,128]{1,0:T(8,128)S(1)}, u32[]{:S(2)}, u32[]{:S(2)}) collective-permute-start(f32[256,128]{1,0:T(8,128)} %get-tuple-element.95), channel_id=1, source_target_pairs={{0,28},{4,0},{8,4},{12,8},{16,12},{20,16},{24,20},{28,24},{1,29},{... | collective-permute-start | bytes 393224 | tf_op jit(solution)/shard_map/ppermute | solution.py:876
  78.2 2.0 %copy-start = (f32[256,128]{1,0:T(8,128)S(1)}, f32[256,128]{1,0:T(8,128)}, u32[]{:S(2)}) copy-start(f32[256,128]{1,0:T(8,128)} %get-tuple-element.88.refs_0_) | copy-start | bytes 393220
